TPU v7x, 512 devices: a whole 4x8x8 slice. The times are simulated.
512 devices in a mesh: rep: 64 (over z_hi, y, core), fsdp: 8 (over x, z_lo).
Axes of the slice: x: 4, y: 8, z: 8 (z_hi: 4, z_lo: 2; z = z_hi * 2 + z_lo), core: 2. Of those that a mesh axis runs over, the one named last changes fastest.
Arguments:
- anchor: float32 [4096, 512], P('fsdp', 'rep'), may hold values from -6 to 6
- momentum: float32 [4096, 512], P('fsdp', 'rep'), may hold values from -1.2 to 1.2
- tokens: bfloat16 [64, 2048, 4096], P('rep', 'fsdp'), may hold values from -6 to 6
- targets: bfloat16 [64, 2048, 512], P('rep', 'fsdp'), may hold values from -6 to 6
- first_moment: float32 [64, 4096, 512], P('rep', 'fsdp'), may hold values from -0.0018 to 0.0018
- second_moment: float32 [64, 4096, 512], P('rep', 'fsdp'), may hold values from 2e-08 to 2e-07
Outputs:
- anchor_next: float32 [4096, 512], P('fsdp', 'rep')
- momentum_next: float32 [4096, 512], P('fsdp', 'rep')
All inputs are finite; a program needn't handle non-finite values.
Results may differ from a plain program's by a relative error of at most 0.002.
Values may be sent and summed in bfloat16 or wider, within the bound.
No kernel may reach another device: no remote copies, remote signals or barrier semaphores. Data moves between devices by JAX's collectives and lax.ppermute only.
A program may use at most 64 MiB of HBM per device.

v0:
```python
import math

import jax
import jax.numpy as jnp
from jax import lax
from jax.sharding import PartitionSpec as P

beta_one = 0.9
beta_two = 0.95
adam_eps = 1e-08
inner_rate = 0.2
decay_rate = 0.1
outer_rate = 0.7
outer_mom = 0.9


def local(anchor, momentum, tokens, targets, first_moment, second_moment):
    own_columns = anchor.astype(jnp.bfloat16)
    start_rows = lax.all_gather(own_columns, "rep", axis=1, tiled=True)
    local_tokens = tokens[0]
    model_width = local_tokens.shape[1]
    groups = lax.axis_size("fsdp")
    count_tokens = local_tokens.shape[0] * groups
    columns = local_tokens
    projected = jnp.dot(
        columns,
        lax.all_gather(start_rows, "fsdp", axis=0, tiled=True),
        preferred_element_type=jnp.float32,
    )
    projected = projected * model_width ** (-0.5)
    residual = (projected - targets[0].astype(jnp.float32)).astype(jnp.bfloat16)
    columns = local_tokens
    summed = lax.psum_scatter(
        lax.dot_general(
            columns, residual, (((0,), (0,)), ((), ())), preferred_element_type=jnp.float32
        ).astype(jnp.bfloat16),
        "fsdp",
        scatter_dimension=0,
        tiled=True,
    ).astype(jnp.float32)
    gradient = summed * (1.0 / (math.sqrt(model_width) * count_tokens))
    moment_one = beta_one * first_moment[0] + (1.0 - beta_one) * gradient
    moment_two = beta_two * second_moment[0] + (1.0 - beta_two) * gradient * gradient
    direction = moment_one / (jnp.sqrt(moment_two) + adam_eps)
    update_delta = inner_rate * (direction + decay_rate * start_rows.astype(jnp.float32))
    owned_count = anchor.shape[1]
    total = lax.psum(update_delta, "rep")
    owned_sum = lax.dynamic_slice_in_dim(total, lax.axis_index("rep") * owned_count, owned_count, 1)
    mean_delta = owned_sum / lax.axis_size("rep")
    momentum_next = outer_mom * momentum + mean_delta
    anchor_next = anchor - outer_rate * (mean_delta + outer_mom * momentum_next)
    return (anchor_next, momentum_next)


def solution(mesh):
    placed = (
        P("fsdp", "rep"),
        P("fsdp", "rep"),
        P("rep", "fsdp", None),
        P("rep", "fsdp", None),
        P("rep", "fsdp", None),
        P("rep", "fsdp", None),
    )
    return jax.shard_map(
        local,
        mesh=mesh,
        in_specs=placed,
        out_specs=(P("fsdp", "rep"), P("fsdp", "rep")),
        check_vma=False,
    )
```

profile of v0, /device:TPU:1, one launch (start us, length us, event | category | flops | bytes accessed | tf_op | source)
XLA Modules:
  0.0 863.5 jit_solution(5334465605169246126)
XLA Ops:
  7.2 0.0 copy-start
  7.2 0.0 all-gather.2.cloned.1.call-start
  7.2 0.9 convert_element_type.24
  8.1 96.5 %all_gather.6 = bf16[512,512]{0,1:T(8,128)(2,1)} all-gather(bf16[512,8]{0,1:T(8,128)(2,1)S(1)} %convert_element_type.24), channel_id=1, replica_groups=mesh['rep'=64,'fsdp'=8] {'rep'}, dimensions={1}, use_global_device_ids=true | all-gather | bytes 532480 | tf_op jit(solution)/shard_map/all_gather | solution.py:19
  104.6 0.0 all-gather.2.cloned.1.call-update
  104.6 0.0 reduce-scatter.2.cloned.1.call-start
  104.6 87.4 %all-gather.2.cloned.1.call-done = bf16[4096,512]{0,1:T(8,128)(2,1)} async-done(((bf16[512,512]{0,1:T(8,128)(2,1)}), bf16[4096,512]{0,1:T(8,128)(2,1)}) %all-gather.2.cloned.1.call-update) | async-done | bytes 4194320 | tf_op jit(solution)/shard_map/all_gather | solution.py:27
  192.1 0.0 copy-done
  192.1 6.7 fusion
  198.8 0.0 copy-start.1
  198.8 0.0 reduce-scatter.2.cloned.1.call-update
  198.8 0.0 all-reduce.2.cloned.1.call-start
  198.9 2.6 copy.9
  201.5 0.0 copy-start.2
  201.5 0.0 copy-start.3
  201.5 2.5 copy.8
  204.0 91.6 %reduce-scatter.2.cloned.1.call-done = bf16[512,512]{0,1:T(8,128)(2,1)} async-done(((bf16[4096,512]{0,1:T(8,128)(2,1)}), bf16[512,512]{0,1:T(8,128)(2,1)}) %reduce-scatter.2.cloned.1.call-update) | async-done | bytes 524304 | tf_op jit(solution)/shard_map/reduce_scatter | solution.py:33
  295.6 0.0 copy-done.1
  295.6 3.5 fusion.18
  299.1 0.0 all-reduce.2.cloned.1.call-update
  299.1 556.5 %all-reduce.2.cloned.1.call-done = f32[512,512]{0,1:T(8,128)} async-done(((f32[512,512]{0,1:T(8,128)}), f32[512,512]{0,1:T(8,128)}) %all-reduce.2.cloned.1.call-update) | async-done | bytes 1048592 | tf_op jit(solution)/shard_map/psum | solution.py:47
  855.6 0.0 copy-done.2
  855.7 0.0 copy-done.3
  855.7 1.3 multiply_subtract_fusion
Async XLA Ops:
  7.2 184.9 %copy-start = (bf16[1,256,4096]{2,1,0:T(8,128)(2,1)S(1)}, bf16[1,256,4096]{2,1,0:T(8,128)(2,1)}, u32[]{:S(2)}) copy-start(bf16[1,256,4096]{2,1,0:T(8,128)(2,1)} %param.8) | copy-start | bytes 6291460
  7.2 184.9 %all-gather.2.cloned.1.call-start = ((), (), s32[]{:S(2)}) async-start(), calls=%async_computation.1 | async-start | bytes 4718592 | tf_op jit(solution)/shard_map/all_gather | solution.py:27
  104.6 191.0 %reduce-scatter.2.cloned.1.call-start = ((), (), s32[]{:S(2)}) async-start(), calls=%async_computation.2 | async-start | bytes 4718592 | tf_op jit(solution)/shard_map/reduce_scatter | solution.py:33
  198.8 96.8 %copy-start.1 = (bf16[512,512]{0,1:T(8,128)(2,1)S(1)}, bf16[512,512]{0,1:T(8,128)(2,1)}, u32[]{:S(2)}) copy-start(bf16[512,512]{0,1:T(8,128)(2,1)} %all_gather.6) | copy-start | bytes 1572868
  198.8 656.8 %all-reduce.2.cloned.1.call-start = ((), (), s32[]{:S(2)}) async-start(), calls=%async_computation.3 | async-start | bytes 2097152 | tf_op jit(solution)/shard_map/psum | solution.py:47
  201.5 654.2 %copy-start.2 = (f32[512,8]{0,1:T(8,128)S(1)}, f32[512,8]{0,1:T(8,128)}, u32[]{:S(2)}) copy-start(f32[512,8]{0,1:T(8,128)} %param.6) | copy-start | bytes 49156
  201.5 654.2 %copy-start.3 = (f32[512,8]{0,1:T(8,128)S(1)}, f32[512,8]{0,1:T(8,128)}, u32[]{:S(2)}) copy-start(f32[512,8]{0,1:T(8,128)} %param.7) | copy-start | bytes 49156
Sparse Core Ops, SparseCore 0:
  104.7 87.3 all-gather.1
  198.9 96.6 reduce-scatter.1
  299.3 556.3 all-reduce.1
where the time goes:
time: 864 us
  waiting for transfers between devices  736 us (85%)
  blocking collectives  96.5 us (11%)
  between operations  13.8 us (2%)
    psum x1, waiting for transfers between devices, local(): total = lax.psum(update_delta, 'rep')  557 us
    all_gather x1, blocking collectives, local(): start_rows = lax.all_gather(own_columns, 'rep', axis=1, tiled=True)  96.5 us
    reduce_scatter x1, waiting for transfers between devices, local(): lax.psum_scatter(lax.dot_general(columns, residual, (((0,), (0,)), ((), (...  91.6 us
    all_gather x1, waiting for transfers between devices, local(): lax.all_gather(start_rows, 'fsdp', axis=0, tiled=True)  87.4 us
  transfers between devices with their start and end apart: 3, of which 3 were waited for; matrix products, arithmetic and copies ran while one was open for 1% of the time, Pallas kernels for 0%

commit v1 on v0

v1 whole, which is shorter than its diff:
```python
import math

import jax
import jax.numpy as jnp
from jax import lax
from jax.sharding import Mesh, PartitionSpec as P

beta_one = 0.9
beta_two = 0.95
adam_eps = 1e-08
inner_rate = 0.2
decay_rate = 0.1
outer_rate = 0.7
outer_mom = 0.9

REP = ("zh", "y", "c")
FSDP = ("x", "zl")


def exchange(blocks, axes):
    return lax.all_to_all(blocks, axes, 0, 0)


def spread(block, axes):
    n = lax.axis_size(axes)
    return exchange(jnp.broadcast_to(block[None], (n,) + block.shape), axes)


def local(anchor, momentum, tokens, targets, first_moment, second_moment):
    groups = lax.axis_size(FSDP)
    replicas = lax.axis_size(REP)
    rows, owned = anchor.shape
    count, width = tokens.shape[1:]
    columns = targets.shape[2]

    own = anchor.astype(jnp.bfloat16).T
    wide = spread(own, FSDP)
    wide = wide.transpose(1, 0, 2).reshape(owned, width)
    part = spread(wide, ("zh", "c"))
    full = lax.all_gather(part, "y", axis=0)
    sizes = tuple(lax.axis_size(a) for a in REP)
    full = full.reshape(sizes[1], sizes[0], sizes[2], owned, width)
    full = full.transpose(1, 0, 2, 3, 4).reshape(columns, width)

    mine = exchange(tokens[0].reshape(count, groups, rows).transpose(1, 0, 2), FSDP)
    mine = mine.reshape(groups * count, rows)

    projected = lax.dot_general(
        tokens[0], full, (((1,), (1,)), ((), ())), preferred_element_type=jnp.float32
    )
    projected = projected * width ** (-0.5)
    residual = (projected - targets[0].astype(jnp.float32)).astype(jnp.bfloat16)
    residual = spread(residual, FSDP).reshape(groups * count, columns)

    summed = lax.dot_general(
        residual, mine, (((0,), (0,)), ((), ())), preferred_element_type=jnp.float32
    )
    gradient = summed * (1.0 / (math.sqrt(width) * groups * count))
    moment_one = beta_one * first_moment[0].T + (1.0 - beta_one) * gradient
    moment_two = beta_two * second_moment[0].T + (1.0 - beta_two) * gradient * gradient
    direction = moment_one / (jnp.sqrt(moment_two) + adam_eps)
    sent = direction.astype(jnp.bfloat16).reshape(replicas, owned, rows)
    total = jnp.sum(exchange(sent, REP).astype(jnp.float32), axis=0).T

    start = anchor.astype(jnp.bfloat16).astype(jnp.float32)
    mean_delta = inner_rate * (total / replicas + decay_rate * start)
    momentum_next = outer_mom * momentum + mean_delta
    anchor_next = anchor - outer_rate * (mean_delta + outer_mom * momentum_next)
    return (anchor_next, momentum_next)


def solution(mesh):
    fine = Mesh(mesh.devices.reshape(4, 8, 2, 4, 2), REP + FSDP)
    outer = P(FSDP, REP)
    inner = P(REP, FSDP, None)
    return jax.shard_map(
        local,
        mesh=fine,
        in_specs=(outer, outer, inner, inner, inner, inner),
        out_specs=(outer, outer),
        check_vma=False,
    )
```

time: 864 us -> 179 us (0.21)
  waiting for transfers between devices: 736 us -> 66 us
  blocking collectives: 96.5 us -> 69.1 us
  starting transfers between devices: 0.12 us -> 9.16 us
  local copies, waits for them, and re-layouts: 5.18 us -> 14.1 us
    psum x1 -> x0, waiting for transfers between devices: 557 us -> none  [local(): total = lax.psum(update_delta, 'rep')]
    all_gather x1 -> x0, blocking collectives: 96.5 us -> none  [local(): start_rows = lax.all_gather(own_columns, 'rep', axis=1, tiled=True)]
    reduce_scatter x1 -> x0, waiting for transfers between devices: 91.6 us -> none  [local(): lax.psum_scatter(lax.dot_general(columns, residual, (((0,), (0,)), ((), (...]
    all_to_all x0 -> x3, blocking collectives: none -> 69.1 us  [exchange(): return lax.all_to_all(blocks, axes, 0, 0)]
    all_gather x1, waiting for transfers between devices: 87.4 us -> 43.7 us  [local(): full = lax.all_gather(part, 'y', axis=0)]
    all_to_all x0 -> x2, waiting for transfers between devices: none -> 22.2 us  [exchange(): return lax.all_to_all(blocks, axes, 0, 0)]
    all_to_all x0 -> x2, starting transfers between devices: none -> 9.12 us  [exchange(): return lax.all_to_all(blocks, axes, 0, 0)]
  transfers between devices with their start and end apart: 3 -> 3, of which waited for: 3 -> 2; matrix products, arithmetic and copies ran while one was open for 1% -> 8% of each run, Pallas kernels for 0% -> 0%
where the time goes in v1:
time: 179 us
  blocking collectives  69.1 us (39%)
  waiting for transfers between devices  66 us (37%)
  local copies, waits for them, and re-layouts  14.1 us (8%)
  between operations  14.1 us (8%)
  starting transfers between devices  9.16 us (5%)
  matrix products  4.89 us (3%)
    all_to_all x3, blocking collectives, exchange(): return lax.all_to_all(blocks, axes, 0, 0)  69.1 us
    all_gather x1, waiting for transfers between devices, local(): full = lax.all_gather(part, 'y', axis=0)  43.7 us
    all_to_all x2, waiting for transfers between devices, exchange(): return lax.all_to_all(blocks, axes, 0, 0)  22.2 us
    all_to_all x2, starting transfers between devices, exchange(): return lax.all_to_all(blocks, axes, 0, 0)  9.12 us
    unnamed x15, local copies, waits for them, and re-layouts  7.48 us
    dot_general x1, matrix products, local(): lax.dot_general(residual, mine, (((0,), (0,)), ((), ())), preferred_eleme...  3.59 us
  transfers between devices with their start and end apart: 3, of which 2 were waited for; matrix products, arithmetic and copies ran while one was open for 8% of the time, Pallas kernels for 0%

profile of v1, /device:TPU:1, one launch (start us, length us, event | category | flops | bytes accessed | tf_op | source)
XLA Modules:
  0.0 178.8 jit_solution(14965916682024416387)
XLA Ops:
  7.2 0.0 all-gather.3.cloned.1.call-start
  7.2 0.7 convert_bitcast_fusion
  7.9 11.6 %all_to_all.25 = bf16[8,8,512]{2,1,0:T(8,128)(2,1)S(1)} all-to-all(bf16[8,8,512]{2,1,0:T(8,128)(2,1)S(1)} %broadcast_in_dim.8), channel_id=1, replica_groups=mesh['zh'=4,'y'=8,'c'=2,'x'=4,'zl'=2] {'x','zl'}, dimensions={0} | all-to-all | bytes 131072 | tf_op jit(solution)/shard_map/all_to_all | solution.py:21
  19.6 27.4 %all_to_all.26 = bf16[8,8,4096]{2,1,0:T(8,128)(2,1)} all-to-all(bf16[8,8,4096]{2,1,0:T(8,128)(2,1)S(1)} %broadcast_in_dim.10), channel_id=1, replica_groups=mesh['zh'=4,'y'=8,'c'=2,'x'=4,'zl'=2] {'zh','c'}, dimensions={0} | all-to-all | bytes 1048576 | tf_op jit(solution)/shard_map/all_to_all | solution.py:21
  47.1 0.0 all-gather.3.cloned.1.call-update
  47.1 3.3 %copy.25 = bf16[1,256,4096]{1,2,0:T(8,128)(2,1)S(1)} copy(bf16[1,256,4096]{2,1,0:T(8,128)(2,1)} %param.8) | data formatting | bytes 4194304 | tf_op args[2]
  50.4 2.4 %copy.26 = bf16[256,8,512]{2,0,1:T(8,128)(2,1)} copy(bf16[256,8,512]{0,2,1:T(8,128)(2,1)S(1)} %bitcast.69) | data formatting | bytes 4194304 | tf_op jit(solution)/shard_map/reshape;squeeze | solution.py:45
  52.8 3.9 %all-to-all-start.3 = ((bf16[8,256,512]{2,1,0:T(8,128)(2,1)}), bf16[8,256,512]{2,1,0:T(8,128)(2,1)S(1)}, u32[]{:S(2)}, u32[]{:S(2)}) async-start(bf16[8,256,512]{2,1,0:T(8,128)(2,1)} %bitcast.11), calls=%async_computation.3 | async-start | bytes 4194304 | tf_op jit(solution)/shard_map/all_to_all | solution.py:21
  56.7 43.7 %all-gather.3.cloned.1.call-done = bf16[64,8,4096]{2,1,0:T(8,128)(2,1)} async-done(((bf16[8,8,4096]{2,1,0:T(8,128)(2,1)}), bf16[64,8,4096]{2,1,0:T(8,128)(2,1)}) %all-gather.3.cloned.1.call-update) | async-done | bytes 4194320 | tf_op jit(solution)/shard_map/all_gather | solution.py:40
  100.4 0.0 copy-start
  100.4 0.0 copy-start.5
  100.4 2.6 %copy.23 = bf16[4,8,2,8,4096]{4,3,2,1,0:T(8,128)(2,1)S(1)} copy(bf16[4,8,2,8,4096]{4,3,2,0,1:T(8,128)(2,1)} %bitcast.70) | data formatting | bytes 8388608 | tf_op jit(solution)/shard_map/transpose | solution.py:43
  103.0 0.2 copy-done
  103.3 0.0 copy-done.5
  103.3 1.3 fusion.8
  104.6 0.1 copy.24
  104.7 0.0 all-to-all-done.3
  104.7 1.5 broadcast_in_dim.22
  106.2 0.0 copy-start.1
  106.2 5.2 %all-to-all-start.2 = ((bf16[8,256,512]{1,2,0:T(8,128)(2,1)}), bf16[8,256,512]{1,2,0:T(8,128)(2,1)}, u32[]{:S(2)}, u32[]{:S(2)}) async-start(bf16[8,256,512]{1,2,0:T(8,128)(2,1)} %broadcast_in_dim.22), calls=%async_computation.2 | async-start | bytes 4194304 | tf_op jit(solution)/shard_map/all_to_all | solution.py:21
  111.4 0.0 copy-done.1
  111.4 1.3 copy.22
  112.7 0.0 copy-start.2
  112.7 2.6 %copy.27 = f32[1,512,512]{1,2,0:T(8,128)} copy(f32[1,512,512]{2,1,0:T(8,128)} %param.11) | data formatting | bytes 2097152 | tf_op args[5]
  115.3 0.0 copy-start.3
  115.3 0.0 copy-start.4
  115.3 22.2 %all-to-all-done.2 = bf16[8,256,512]{1,2,0:T(8,128)(2,1)} async-done(((bf16[8,256,512]{1,2,0:T(8,128)(2,1)}), bf16[8,256,512]{1,2,0:T(8,128)(2,1)}, u32[]{:S(2)}, u32[]{:S(2)}) %all-to-all-start.2) | async-done | bytes 2097184 | tf_op jit(solution)/shard_map/all_to_all | solution.py:21
  137.6 0.0 copy-done.2
  137.6 3.6 %fusion.15 = bf16[64,8,512]{2,1,0:T(8,128)(2,1)S(1)} fusion(f32[1,512,512]{1,2,0:T(8,128)} %copy.27, bf16[8,256,512]{1,2,0:T(8,128)(2,1)} %all-to-all-done.2, bf16[8,256,512]{2,1,0:T(8,128)(2,1)S(1)} %all-to-all-done.3, f32[1,512,512]{1,2,0:T(8,128)S(1)} %copy-done.2), kind=kOutput, calls=%fused_computation.13 | convolution fusion | flops 1076625408 | bytes 6815744 | tf_op jit(solution)/shard_map/dot_general | solution.py:55
  141.2 30.1 %all_to_all.27 = bf16[64,8,512]{2,1,0:T(8,128)(2,1)S(1)} all-to-all(bf16[64,8,512]{2,1,0:T(8,128)(2,1)S(1)} %fusion.15), channel_id=1, replica_groups=mesh['zh'=4,'y'=8,'c'=2,'x'=4,'zl'=2] {'zh','y','c'}, dimensions={0} | all-to-all | bytes 1048576 | tf_op jit(solution)/shard_map/all_to_all | solution.py:21
  171.2 0.1 convert_reduce_fusion
  171.3 0.0 copy-done.3
  171.3 0.0 copy-done.4
  171.3 0.6 multiply_subtract_fusion
  (2 shorter events, 0.0 us)
Async XLA Ops:
  7.2 93.3 %all-gather.3.cloned.1.call-start = ((), (), s32[]{:S(2)}) async-start(), calls=%async_computation.5 | async-start | bytes 4718592 | tf_op jit(solution)/shard_map/all_gather | solution.py:40
  52.8 52.0 %all-to-all-start.3 = ((bf16[8,256,512]{2,1,0:T(8,128)(2,1)}), bf16[8,256,512]{2,1,0:T(8,128)(2,1)S(1)}, u32[]{:S(2)}, u32[]{:S(2)}) async-start(bf16[8,256,512]{2,1,0:T(8,128)(2,1)} %bitcast.11), calls=%async_computation.3 | async-start | bytes 4194304 | tf_op jit(solution)/shard_map/all_to_all | solution.py:21
  100.4 2.9 %copy-start = (bf16[1,256,4096]{2,1,0:T(8,128)(2,1)S(1)}, bf16[1,256,4096]{2,1,0:T(8,128)(2,1)}, u32[]{:S(2)}) copy-start(bf16[1,256,4096]{2,1,0:T(8,128)(2,1)} %param.8) | copy-start | bytes 6291460
  100.4 2.9 %copy-start.5 = (bf16[1,256,512]{2,1,0:T(8,128)(2,1)S(1)}, bf16[1,256,512]{2,1,0:T(8,128)(2,1)}, u32[]{:S(2)}) copy-start(bf16[1,256,512]{2,1,0:T(8,128)(2,1)} %param.9) | copy-start | bytes 786436
  106.2 5.2 %copy-start.1 = (f32[1,512,512]{2,1,0:T(8,128)S(1)}, f32[1,512,512]{2,1,0:T(8,128)}, u32[]{:S(2)}) copy-start(f32[1,512,512]{2,1,0:T(8,128)} %param.10) | copy-start | bytes 3145732
  106.2 31.4 %all-to-all-start.2 = ((bf16[8,256,512]{1,2,0:T(8,128)(2,1)}), bf16[8,256,512]{1,2,0:T(8,128)(2,1)}, u32[]{:S(2)}, u32[]{:S(2)}) async-start(bf16[8,256,512]{1,2,0:T(8,128)(2,1)} %broadcast_in_dim.22), calls=%async_computation.2 | async-start | bytes 4194304 | tf_op jit(solution)/shard_map/all_to_all | solution.py:21
  112.7 24.8 %copy-start.2 = (f32[1,512,512]{1,2,0:T(8,128)S(1)}, f32[1,512,512]{1,2,0:T(8,128)}, u32[]{:S(2)}) copy-start(f32[1,512,512]{1,2,0:T(8,128)} %copy.22) | copy-start | bytes 3145732
  115.3 56.0 %copy-start.3 = (f32[512,8]{0,1:T(8,128)S(1)}, f32[512,8]{0,1:T(8,128)}, u32[]{:S(2)}) copy-start(f32[512,8]{0,1:T(8,128)} %param.6) | copy-start | bytes 49156
  115.3 56.0 %copy-start.4 = (f32[512,8]{0,1:T(8,128)S(1)}, f32[512,8]{0,1:T(8,128)}, u32[]{:S(2)}) copy-start(f32[512,8]{0,1:T(8,128)} %param.7) | copy-start | bytes 49156
Sparse Core Ops, SparseCore 0:
  47.2 53.1 all-gather.2

commit v2 on v1

v2 whole, which is shorter than its diff:
```python
import math

import jax
import jax.numpy as jnp
from jax import lax
from jax.sharding import Mesh, PartitionSpec as P

beta_one = 0.9
beta_two = 0.95
adam_eps = 1e-08
inner_rate = 0.2
decay_rate = 0.1
outer_rate = 0.7
outer_mom = 0.9

REP = ("zh", "y", "c")
FSDP = ("x", "zl")


def exchange(blocks, axes):
    return lax.all_to_all(blocks, axes, 0, 0)


def spread(block, axes):
    n = lax.axis_size(axes)
    return exchange(jnp.broadcast_to(block[None], (n,) + block.shape), axes)


def local(anchor, momentum, tokens, targets, first_moment, second_moment):
    nx = lax.axis_size("x")
    groups = lax.axis_size(FSDP)
    replicas = lax.axis_size(REP)
    rows, owned = anchor.shape
    count, width = tokens.shape[1:]
    columns = targets.shape[2]
    at_x, at_zl = lax.axis_index("x"), lax.axis_index("zl")
    swap = [(0, 1), (1, 0)]

    own = anchor.astype(jnp.bfloat16).T
    pair = jnp.concatenate([own, lax.ppermute(own, "zl", swap)], axis=1)

    tok = tokens[0]

    def cut(x):
        first = lax.dynamic_slice_in_dim(tok, (2 * x + at_zl) * rows, rows, 1)
        second = lax.dynamic_slice_in_dim(tok, (2 * x + 1 - at_zl) * rows, rows, 1)
        return jnp.concatenate([first, second], axis=1)

    held = jnp.zeros((nx, count, 2 * rows), tok.dtype)
    for d in (2, 1, 3, 0):
        block = cut((at_x + d) % nx)
        if d:
            block = lax.ppermute(block, "x", [(i, (i + d) % nx) for i in range(nx)])
        held = lax.dynamic_update_slice_in_dim(held, block[None], (at_x - d) % nx, 0)
    held = held.reshape(nx * count, 2 * rows)

    start = spread(pair, REP).reshape(columns, 2 * rows)
    partial = lax.dot_general(
        held, start, (((1,), (1,)), ((), ())), preferred_element_type=jnp.float32
    ).astype(jnp.bfloat16)
    parts = exchange(partial.reshape(nx, count, columns), "x").astype(jnp.float32)
    projected = jnp.sum(parts, axis=0) * width ** (-0.5)
    residual = (projected - targets[0].astype(jnp.float32)).astype(jnp.bfloat16)
    residual = spread(residual, "x").reshape(nx * count, columns)

    def term(tok):
        return lax.dot_general(
            residual, tok, (((0,), (0,)), ((), ())), preferred_element_type=jnp.float32
        )

    other = lax.ppermute(term(held[:, rows:]).astype(jnp.bfloat16), "zl", swap)
    summed = term(held[:, :rows]) + other.astype(jnp.float32)
    gradient = summed * (1.0 / (math.sqrt(width) * groups * count))
    moment_one = beta_one * first_moment[0].T + (1.0 - beta_one) * gradient
    moment_two = beta_two * second_moment[0].T + (1.0 - beta_two) * gradient * gradient
    direction = moment_one / (jnp.sqrt(moment_two) + adam_eps)
    sent = direction.astype(jnp.bfloat16).reshape(replicas, owned, rows)
    total = jnp.sum(exchange(sent, REP).astype(jnp.float32), axis=0).T

    begin = anchor.astype(jnp.bfloat16).astype(jnp.float32)
    mean_delta = inner_rate * (total / replicas + decay_rate * begin)
    momentum_next = outer_mom * momentum + mean_delta
    anchor_next = anchor - outer_rate * (mean_delta + outer_mom * momentum_next)
    return (anchor_next, momentum_next)


def solution(mesh):
    fine = Mesh(mesh.devices.reshape(4, 8, 2, 4, 2), REP + FSDP)
    outer = P(FSDP, REP)
    inner = P(REP, FSDP, None)
    return jax.shard_map(
        local,
        mesh=fine,
        in_specs=(outer, outer, inner, inner, inner, inner),
        out_specs=(outer, outer),
        check_vma=False,
    )
```

time: 179 us -> 147 us (0.82)
  waiting for transfers between devices: 66 us -> 20.6 us
  starting transfers between devices: 9.16 us -> 36.3 us
  between operations: 14.1 us -> 1 us
  local copies, waits for them, and re-layouts: 14.1 us -> 10.7 us
  other arithmetic: 1.44 us -> 3.64 us
    all_gather x1 -> x0, waiting for transfers between devices: 43.7 us -> none  [local(): full = lax.all_gather(part, 'y', axis=0)]
    all_to_all x2 -> x1, waiting for transfers between devices: 22.2 us -> 0.01 us  [exchange(): return lax.all_to_all(blocks, axes, 0, 0)]
    ppermute x0 -> x5, waiting for transfers between devices: none -> 20.6 us  [the longest x3 14.2 us: local(): block = lax.ppermute(block, 'x', [(i, (i + d) % nx) for i in range(nx)])]
    ppermute x0 -> x5, starting transfers between devices: none -> 19 us  [the longest x3 11.1 us: local(): block = lax.ppermute(block, 'x', [(i, (i + d) % nx) for i in range(nx)])]
    all_to_all x2 -> x1, starting transfers between devices: 9.12 us -> 17.3 us  [exchange(): return lax.all_to_all(blocks, axes, 0, 0)]
    dynamic_update_slice x0 -> x3, local copies, waits for them, and re-layouts: none -> 3.28 us  [local(): lax.dynamic_update_slice_in_dim(held, block[None], (at_x - d) % nx, 0)]
    transpose x1 -> x0, local copies, waits for them, and re-layouts: 2.61 us -> none  [local(): full = full.transpose(1, 0, 2, 3, 4).reshape(columns, width)]
    unnamed x15 -> x18, local copies, waits for them, and re-layouts: 7.48 us -> 5 us
  transfers between devices with their start and end apart: 3 -> 6, of which waited for: 2 -> 4; matrix products, arithmetic and copies ran while one was open for 8% -> 7% of each run, Pallas kernels for 0% -> 0%
where the time goes in v2:
time: 147 us
  blocking collectives  68.6 us (47%)
  starting transfers between devices  36.3 us (25%)
  waiting for transfers between devices  20.6 us (14%)
  local copies, waits for them, and re-layouts  10.7 us (7%)
  matrix products  5.79 us (4%)
  other arithmetic  3.64 us (2%)
    all_to_all x3, blocking collectives, exchange(): return lax.all_to_all(blocks, axes, 0, 0)  68.6 us
    all_to_all x1, starting transfers between devices, exchange(): return lax.all_to_all(blocks, axes, 0, 0)  17.3 us
    ppermute x3, waiting for transfers between devices, local(): block = lax.ppermute(block, 'x', [(i, (i + d) % nx) for i in range(nx)])  14.2 us
    ppermute x3, starting transfers between devices, local(): block = lax.ppermute(block, 'x', [(i, (i + d) % nx) for i in range(nx)])  11.1 us
    ppermute x1, waiting for transfers between devices, local(): other = lax.ppermute(term(held[:, rows:]).astype(jnp.bfloat16), 'zl', swap)  5.35 us
    unnamed x18, local copies, waits for them, and re-layouts  5 us
    ppermute x1, starting transfers between devices, local(): pair = jnp.concatenate([own, lax.ppermute(own, 'zl', swap)], axis=1)  4.82 us
    dot_general x2, matrix products, term(): lax.dot_general(residual, tok, (((0,), (0,)), ((), ())), preferred_elemen...  4.51 us
  transfers between devices with their start and end apart: 6, of which 4 were waited for; matrix products, arithmetic and copies ran while one was open for 7% of the time, Pallas kernels for 0%

profile of v2, /device:TPU:1, one launch (start us, length us, event | category | flops | bytes accessed | tf_op | source)
XLA Modules:
  0.0 146.7 jit_solution(17320987016491246192)
XLA Ops:
  0.6 0.0 copy-start
  0.6 0.9 convert_bitcast_fusion
  1.5 4.8 %collective-permute-start.3 = (bf16[8,512]{1,0:T(8,128)(2,1)S(1)}, bf16[8,512]{1,0:T(8,128)(2,1)S(1)}, u32[]{:S(2)}, u32[]{:S(2)}) collective-permute-start(bf16[8,512]{1,0:T(8,128)(2,1)S(1)} %convert_bitcast_fusion), channel_id=1, source_target_pairs={{0,1},{1,0},{2,3},{3,2},{4,5},{5,4},{6,7},{7,6},{8,9},{9,8},{10,11... | collective-permute-start | bytes 24584 | tf_op jit(solution)/shard_map/ppermute | solution.py:40
  6.3 1.0 collective-permute-done.3
  7.4 1.1 broadcast_in_dim.34
  8.5 17.3 %all-to-all-start = ((bf16[64,8,1024]{2,1,0:T(8,128)(2,1)}), bf16[64,8,1024]{2,1,0:T(8,128)(2,1)S(1)}, u32[]{:S(2)}, u32[]{:S(2)}) async-start(bf16[64,8,1024]{2,1,0:T(8,128)(2,1)} %broadcast_in_dim.34), calls=%async_computation | async-start | bytes 2097152 | tf_op jit(solution)/shard_map/all_to_all | solution.py:21
  25.9 0.0 copy-done
  25.9 1.0 dynamic-slice_bitcast_fusion.1
  26.9 4.7 %collective-permute-start = (bf16[256,1024]{1,0:T(8,128)(2,1)S(1)}, bf16[256,1024]{1,0:T(8,128)(2,1)}, u32[]{:S(2)}, u32[]{:S(2)}) collective-permute-start(bf16[256,1024]{1,0:T(8,128)(2,1)S(1)} %pad_maximum_fusion), channel_id=1, source_target_pairs={{0,4},{2,6},{4,0},{6,2},{1,5},{3,7},{5,1},{7,3},{8,12},{10,14},{12... | collective-permute-start | bytes 1572872 | tf_op jit(solution)/shard_map/ppermute | solution.py:53
  31.6 0.9 pad_maximum_fusion.1
  32.4 2.2 %collective-permute-start.1 = (bf16[256,1024]{1,0:T(8,128)(2,1)}, bf16[256,1024]{1,0:T(8,128)(2,1)}, u32[]{:S(2)}, u32[]{:S(2)}) collective-permute-start(bf16[256,1024]{1,0:T(8,128)(2,1)} %pad_maximum_fusion.1), channel_id=1, source_target_pairs={{0,2},{2,4},{4,6},{6,0},{1,3},{3,5},{5,7},{7,1},{8,10},{10,12},{12... | collective-permute-start | bytes 1572872 | tf_op jit(solution)/shard_map/ppermute | solution.py:53
  34.6 0.9 pad_maximum_fusion.2
  35.5 4.3 %collective-permute-start.2 = (bf16[256,1024]{1,0:T(8,128)(2,1)}, bf16[256,1024]{1,0:T(8,128)(2,1)}, u32[]{:S(2)}, u32[]{:S(2)}) collective-permute-start(bf16[256,1024]{1,0:T(8,128)(2,1)} %pad_maximum_fusion.2), channel_id=1, source_target_pairs={{0,6},{2,0},{4,2},{6,4},{1,7},{3,1},{5,3},{7,5},{8,14},{10,8},{12,... | collective-permute-start | bytes 1572872 | tf_op jit(solution)/shard_map/ppermute | solution.py:53
  39.8 3.7 %collective-permute-done = bf16[256,1024]{1,0:T(8,128)(2,1)} collective-permute-done((bf16[256,1024]{1,0:T(8,128)(2,1)S(1)}, bf16[256,1024]{1,0:T(8,128)(2,1)}, u32[]{:S(2)}, u32[]{:S(2)}) %collective-permute-start) | collective-permute-done | bytes 524320 | tf_op jit(solution)/shard_map/ppermute | solution.py:53
  43.5 0.3 broadcast_in_dim.29
  43.8 0.0 copy-start.4
  43.8 1.1 bitcast_dynamic-update-slice_fusion.2
  44.9 10.6 %collective-permute-done.1 = bf16[256,1024]{1,0:T(8,128)(2,1)} collective-permute-done((bf16[256,1024]{1,0:T(8,128)(2,1)}, bf16[256,1024]{1,0:T(8,128)(2,1)}, u32[]{:S(2)}, u32[]{:S(2)}) %collective-permute-start.1) | collective-permute-done | bytes 524320 | tf_op jit(solution)/shard_map/ppermute | solution.py:53
  55.5 1.1 bitcast_dynamic-update-slice_fusion.1
  56.6 0.0 collective-permute-done.2
  56.6 1.1 bitcast_dynamic-update-slice_fusion
  57.7 0.0 copy-done.4
  57.7 0.1 fusion.16
  57.7 0.0 all-to-all-done
  57.8 1.3 convolution_convert_fusion
  59.0 0.0 copy-start.5
  59.1 18.1 %all_to_all.20 = bf16[4,256,512]{2,1,0:T(8,128)(2,1)S(1)} all-to-all(bf16[4,256,512]{2,1,0:T(8,128)(2,1)S(1)} %bitcast.85), channel_id=1, replica_groups=mesh['zh'=4,'y'=8,'c'=2,'x'=4,'zl'=2] {'x'}, dimensions={0} | all-to-all | bytes 2097152 | tf_op jit(solution)/shard_map/all_to_all | solution.py:21
  77.1 0.1 convert_reduce_fusion
  77.3 0.0 copy-done.5
  77.3 0.1 fusion.18
  77.4 0.1 broadcast_in_dim.36
  77.5 15.3 %all_to_all.21 = bf16[4,256,512]{2,1,0:T(8,128)(2,1)S(1)} all-to-all(bf16[4,256,512]{2,1,0:T(8,128)(2,1)S(1)} %broadcast_in_dim.36), channel_id=1, replica_groups=mesh['zh'=4,'y'=8,'c'=2,'x'=4,'zl'=2] {'x'}, dimensions={0} | all-to-all | bytes 2097152 | tf_op jit(solution)/shard_map/all_to_all | solution.py:21
  92.8 0.0 copy-start.2
  92.8 0.0 copy-start.1
  92.8 1.0 copy-done.2
  93.8 1.5 %convolution_convert_fusion.1 = bf16[512,512]{1,0:T(8,128)(2,1)} fusion(bf16[1024,512]{1,0:T(8,128)(2,1)S(1)} %bitcast.83, bf16[1024,1024]{1,0:T(8,128)(2,1)S(1)} %bitcast.81), kind=kOutput, calls=%fused_computation.2 | convolution fusion | flops 537133056 | bytes 2621440 | tf_op jit(solution)/shard_map/dot_general | solution.py:67
  95.3 3.1 %collective-permute-start.4 = (bf16[512,512]{1,0:T(8,128)(2,1)}, bf16[512,512]{1,0:T(8,128)(2,1)}, u32[]{:S(2)}, u32[]{:S(2)}) collective-permute-start(bf16[512,512]{1,0:T(8,128)(2,1)} %convolution_convert_fusion.1), channel_id=1, source_target_pairs={{0,1},{1,0},{2,3},{3,2},{4,5},{5,4},{6,7},{7,6},{8,9},{9,8},{10,11... | collective-permute-start | bytes 1572872 | tf_op jit(solution)/shard_map/ppermute | solution.py:71
  98.4 0.0 copy-done.1
  98.4 1.3 copy.8
  99.7 0.0 copy-start.3
  99.7 2.7 %copy.9 = f32[1,512,512]{1,2,0:T(8,128)} copy(f32[1,512,512]{2,1,0:T(8,128)} %param.11) | data formatting | bytes 2097152 | tf_op args[5]
  102.4 0.0 copy-start.6
  102.4 0.0 copy-start.7
  102.4 5.4 %collective-permute-done.4 = bf16[512,512]{1,0:T(8,128)(2,1)} collective-permute-done((bf16[512,512]{1,0:T(8,128)(2,1)}, bf16[512,512]{1,0:T(8,128)(2,1)}, u32[]{:S(2)}, u32[]{:S(2)}) %collective-permute-start.4) | collective-permute-done | bytes 524320 | tf_op jit(solution)/shard_map/ppermute | solution.py:71
  107.7 0.0 copy-done.3
  107.7 3.0 %fusion.13 = bf16[64,8,512]{2,1,0:T(8,128)(2,1)S(1)} fusion(f32[1,512,512]{1,2,0:T(8,128)} %copy.9, bf16[512,512]{1,0:T(8,128)(2,1)} %collective-permute-done.4, bf16[1024,512]{1,0:T(8,128)(2,1)S(1)} %bitcast.84, bf16[1024,1024]{1,0:T(8,128)(2,1)S(1)} %bitcast.82, f32[1,512,512]{1,2,0:T(8,128)} %copy.8), kind=kOutput, calls=%fused_computation.15 | convolution fusion | flops 540278784 | bytes 5242880 | tf_op jit(solution)/shard_map/dot_general | solution.py:67
  110.7 35.3 %all_to_all.22 = bf16[64,8,512]{2,1,0:T(8,128)(2,1)S(1)} all-to-all(bf16[64,8,512]{2,1,0:T(8,128)(2,1)S(1)} %fusion.13), channel_id=1, replica_groups=mesh['zh'=4,'y'=8,'c'=2,'x'=4,'zl'=2] {'zh','y','c'}, dimensions={0} | all-to-all | bytes 1048576 | tf_op jit(solution)/shard_map/all_to_all | solution.py:21
  146.0 0.1 convert_reduce_fusion.1
  146.1 0.0 copy-done.6
  146.1 0.0 copy-done.7
  146.1 0.6 multiply_subtract_fusion
  (2 shorter events, 0.1 us)
Async XLA Ops:
  0.6 25.2 %copy-start = (bf16[1,256,4096]{2,1,0:T(8,128)(2,1)S(1)}, bf16[1,256,4096]{2,1,0:T(8,128)(2,1)}, u32[]{:S(2)}) copy-start(bf16[1,256,4096]{2,1,0:T(8,128)(2,1)} %param.8) | copy-start | bytes 6291460
  1.5 5.9 %collective-permute-start.3 = (bf16[8,512]{1,0:T(8,128)(2,1)S(1)}, bf16[8,512]{1,0:T(8,128)(2,1)S(1)}, u32[]{:S(2)}, u32[]{:S(2)}) collective-permute-start(bf16[8,512]{1,0:T(8,128)(2,1)S(1)} %convert_bitcast_fusion), channel_id=1, source_target_pairs={{0,1},{1,0},{2,3},{3,2},{4,5},{5,4},{6,7},{7,6},{8,9},{9,8},{10,11... | collective-permute-start | bytes 24584 | tf_op jit(solution)/shard_map/ppermute | solution.py:40
  8.5 49.3 %all-to-all-start = ((bf16[64,8,1024]{2,1,0:T(8,128)(2,1)}), bf16[64,8,1024]{2,1,0:T(8,128)(2,1)S(1)}, u32[]{:S(2)}, u32[]{:S(2)}) async-start(bf16[64,8,1024]{2,1,0:T(8,128)(2,1)} %broadcast_in_dim.34), calls=%async_computation | async-start | bytes 2097152 | tf_op jit(solution)/shard_map/all_to_all | solution.py:21
  26.9 16.6 %collective-permute-start = (bf16[256,1024]{1,0:T(8,128)(2,1)S(1)}, bf16[256,1024]{1,0:T(8,128)(2,1)}, u32[]{:S(2)}, u32[]{:S(2)}) collective-permute-start(bf16[256,1024]{1,0:T(8,128)(2,1)S(1)} %pad_maximum_fusion), channel_id=1, source_target_pairs={{0,4},{2,6},{4,0},{6,2},{1,5},{3,7},{5,1},{7,3},{8,12},{10,14},{12... | collective-permute-start | bytes 1572872 | tf_op jit(solution)/shard_map/ppermute | solution.py:53
  32.4 23.1 %collective-permute-start.1 = (bf16[256,1024]{1,0:T(8,128)(2,1)}, bf16[256,1024]{1,0:T(8,128)(2,1)}, u32[]{:S(2)}, u32[]{:S(2)}) collective-permute-start(bf16[256,1024]{1,0:T(8,128)(2,1)} %pad_maximum_fusion.1), channel_id=1, source_target_pairs={{0,2},{2,4},{4,6},{6,0},{1,3},{3,5},{5,7},{7,1},{8,10},{10,12},{12... | collective-permute-start | bytes 1572872 | tf_op jit(solution)/shard_map/ppermute | solution.py:53
  35.5 21.1 %collective-permute-start.2 = (bf16[256,1024]{1,0:T(8,128)(2,1)}, bf16[256,1024]{1,0:T(8,128)(2,1)}, u32[]{:S(2)}, u32[]{:S(2)}) collective-permute-start(bf16[256,1024]{1,0:T(8,128)(2,1)} %pad_maximum_fusion.2), channel_id=1, source_target_pairs={{0,6},{2,0},{4,2},{6,4},{1,7},{3,1},{5,3},{7,5},{8,14},{10,8},{12,... | collective-permute-start | bytes 1572872 | tf_op jit(solution)/shard_map/ppermute | solution.py:53
  43.8 13.9 %copy-start.4 = (bf16[256,512]{1,0:T(8,128)(2,1)S(1)}, bf16[256,512]{1,0:T(8,128)(2,1)}, u32[]{:S(2)}) copy-start(bf16[256,512]{1,0:T(8,128)(2,1)} %get-tuple-element.11) | copy-start | bytes 786436
  59.0 18.2 %copy-start.5 = (bf16[1,256,512]{2,1,0:T(8,128)(2,1)S(1)}, bf16[1,256,512]{2,1,0:T(8,128)(2,1)}, u32[]{:S(2)}) copy-start(bf16[1,256,512]{2,1,0:T(8,128)(2,1)} %param.9) | copy-start | bytes 786436
  92.8 1.0 copy-start.2
  92.8 5.6 %copy-start.1 = (f32[1,512,512]{2,1,0:T(8,128)S(1)}, f32[1,512,512]{2,1,0:T(8,128)}, u32[]{:S(2)}) copy-start(f32[1,512,512]{2,1,0:T(8,128)} %param.10) | copy-start | bytes 3145732
  95.3 12.5 %collective-permute-start.4 = (bf16[512,512]{1,0:T(8,128)(2,1)}, bf16[512,512]{1,0:T(8,128)(2,1)}, u32[]{:S(2)}, u32[]{:S(2)}) collective-permute-start(bf16[512,512]{1,0:T(8,128)(2,1)} %convolution_convert_fusion.1), channel_id=1, source_target_pairs={{0,1},{1,0},{2,3},{3,2},{4,5},{5,4},{6,7},{7,6},{8,9},{9,8},{10,11... | collective-permute-start | bytes 1572872 | tf_op jit(solution)/shard_map/ppermute | solution.py:71
  99.7 8.0 %copy-start.3 = (bf16[4,256,512]{2,1,0:T(8,128)(2,1)S(1)}, bf16[4,256,512]{2,1,0:T(8,128)(2,1)}, u32[]{:S(2)}) copy-start(bf16[4,256,512]{2,1,0:T(8,128)(2,1)} %copy-done.2) | copy-start | bytes 3145732
  102.4 43.7 %copy-start.6 = (f32[512,8]{0,1:T(8,128)S(1)}, f32[512,8]{0,1:T(8,128)}, u32[]{:S(2)}) copy-start(f32[512,8]{0,1:T(8,128)} %param.6) | copy-start | bytes 49156
  102.4 43.7 %copy-start.7 = (f32[512,8]{0,1:T(8,128)S(1)}, f32[512,8]{0,1:T(8,128)}, u32[]{:S(2)}) copy-start(f32[512,8]{0,1:T(8,128)} %param.7) | copy-start | bytes 49156

commit v3 on v2

--- a/solution.py
+++ b/solution.py
@@ -15,6 +15,7 @@
 
 REP = ("zh", "y", "c")
 FSDP = ("x", "zl")
+FAR = ("zh", "y")
 
 
 def exchange(blocks, axes):
@@ -33,28 +34,29 @@
     rows, owned = anchor.shape
     count, width = tokens.shape[1:]
     columns = targets.shape[2]
-    at_x, at_zl = lax.axis_index("x"), lax.axis_index("zl")
+    far = columns // owned // 2
+    at_x, at_zl, at_c = lax.axis_index("x"), lax.axis_index("zl"), lax.axis_index("c")
     swap = [(0, 1), (1, 0)]
 
-    own = anchor.astype(jnp.bfloat16).T
-    pair = jnp.concatenate([own, lax.ppermute(own, "zl", swap)], axis=1)
+    def ordered(mine, other, at, axis):
+        first = jnp.where(at == 0, mine, other)
+        return jnp.stack([first, jnp.where(at == 0, other, mine)], axis)
 
     tok = tokens[0]
-
-    def cut(x):
-        first = lax.dynamic_slice_in_dim(tok, (2 * x + at_zl) * rows, rows, 1)
-        second = lax.dynamic_slice_in_dim(tok, (2 * x + 1 - at_zl) * rows, rows, 1)
-        return jnp.concatenate([first, second], axis=1)
-
     held = jnp.zeros((nx, count, 2 * rows), tok.dtype)
     for d in (2, 1, 3, 0):
-        block = cut((at_x + d) % nx)
+        block = lax.dynamic_slice_in_dim(tok, (at_x + d) % nx * 2 * rows, 2 * rows, 1)
         if d:
             block = lax.ppermute(block, "x", [(i, (i + d) % nx) for i in range(nx)])
         held = lax.dynamic_update_slice_in_dim(held, block[None], (at_x - d) % nx, 0)
     held = held.reshape(nx * count, 2 * rows)
 
-    start = spread(pair, REP).reshape(columns, 2 * rows)
+    own = anchor.astype(jnp.bfloat16).T
+    pair = ordered(own, lax.ppermute(own, "zl", swap), at_zl, 1).reshape(owned, 2 * rows)
+    half = spread(pair, FAR)
+    start = ordered(half, lax.ppermute(half, "c", swap), at_c, 1)
+    start = start.reshape(columns, 2 * rows)
+
     partial = lax.dot_general(
         held, start, (((1,), (1,)), ((), ())), preferred_element_type=jnp.float32
     ).astype(jnp.bfloat16)
@@ -63,19 +65,27 @@
     residual = (projected - targets[0].astype(jnp.float32)).astype(jnp.bfloat16)
     residual = spread(residual, "x").reshape(nx * count, columns)
 
-    def term(tok):
+    def term(at):
         return lax.dot_general(
-            residual, tok, (((0,), (0,)), ((), ())), preferred_element_type=jnp.float32
+            residual,
+            lax.dynamic_slice_in_dim(held, at * rows, rows, 1),
+            (((0,), (0,)), ((), ())),
+            preferred_element_type=jnp.float32,
         )
 
-    other = lax.ppermute(term(held[:, rows:]).astype(jnp.bfloat16), "zl", swap)
-    summed = term(held[:, :rows]) + other.astype(jnp.float32)
+    other = lax.ppermute(term(1 - at_zl).astype(jnp.bfloat16), "zl", swap)
+    summed = term(at_zl) + other.astype(jnp.float32)
     gradient = summed * (1.0 / (math.sqrt(width) * groups * count))
     moment_one = beta_one * first_moment[0].T + (1.0 - beta_one) * gradient
     moment_two = beta_two * second_moment[0].T + (1.0 - beta_two) * gradient * gradient
     direction = moment_one / (jnp.sqrt(moment_two) + adam_eps)
-    sent = direction.astype(jnp.bfloat16).reshape(replicas, owned, rows)
-    total = jnp.sum(exchange(sent, REP).astype(jnp.float32), axis=0).T
+
+    direction = direction.reshape(far, 2, owned, rows)
+    given = lax.dynamic_index_in_dim(direction, 1 - at_c, 1, keepdims=False)
+    kept = lax.dynamic_index_in_dim(direction, at_c, 1, keepdims=False)
+    given = lax.ppermute(given.astype(jnp.bfloat16), "c", swap)
+    sent = (kept + given.astype(jnp.float32)).astype(jnp.bfloat16)
+    total = jnp.sum(exchange(sent, FAR).astype(jnp.float32), axis=0).T
 
     begin = anchor.astype(jnp.bfloat16).astype(jnp.float32)
     mean_delta = inner_rate * (total / replicas + decay_rate * begin)

time: 147 us -> 151 us (1.027)
  the two profiles are of different devices: /device:TPU:1 before, /device:TPU:8 now
where the time goes in v3:
time: 151 us; the launch traced here: 150 us
  blocking collectives  46.5 us (31%)
  starting transfers between devices  43.5 us (29%)
  waiting for transfers between devices  33.5 us (22%)
  local copies, waits for them, and re-layouts  15 us (10%)
  matrix products  6.38 us (4%)
  other arithmetic  3.62 us (2%)
    all_to_all x2, blocking collectives, exchange(): return lax.all_to_all(blocks, axes, 0, 0)  46.5 us
    all_to_all x2, starting transfers between devices, exchange(): return lax.all_to_all(blocks, axes, 0, 0)  20.1 us
    all_to_all x2, waiting for transfers between devices, exchange(): return lax.all_to_all(blocks, axes, 0, 0)  14.2 us
    ppermute x3, starting transfers between devices, local(): block = lax.ppermute(block, 'x', [(i, (i + d) % nx) for i in range(nx)])  12 us
    ppermute x3, waiting for transfers between devices, local(): block = lax.ppermute(block, 'x', [(i, (i + d) % nx) for i in range(nx)])  11.3 us
    unnamed x10, local copies, waits for them, and re-layouts  6.06 us
    dot_general x2, matrix products, term(): lax.dot_general(residual, lax.dynamic_slice_in_dim(held, at * rows, rows,...  5.09 us
    ppermute x1, waiting for transfers between devices, local(): other = lax.ppermute(term(1 - at_zl).astype(jnp.bfloat16), 'zl', swap)  4.89 us
  transfers between devices with their start and end apart: 9, of which 6 were waited for; matrix products, arithmetic and copies ran while one was open for 8% of the time, Pallas kernels for 0%

profile of v3, /device:TPU:8, one launch (start us, length us, event | category | flops | bytes accessed | tf_op | source)
XLA Modules:
  0.0 149.5 jit_solution(7411523467448399999)
XLA Ops:
  0.6 0.7 convert_bitcast_fusion
  1.4 4.3 %collective-permute-start.3 = (bf16[8,512]{1,0:T(8,128)(2,1)S(1)}, bf16[8,512]{1,0:T(8,128)(2,1)S(1)}, u32[]{:S(2)}, u32[]{:S(2)}) collective-permute-start(bf16[8,512]{1,0:T(8,128)(2,1)S(1)} %convert_bitcast_fusion), channel_id=1, source_target_pairs={{0,1},{1,0},{2,3},{3,2},{4,5},{5,4},{6,7},{7,6},{8,9},{9,8},{10,11... | collective-permute-start | bytes 24584 | tf_op jit(solution)/shard_map/ppermute | solution.py:55
  5.6 1.6 %collective-permute-done.3 = bf16[8,512]{1,0:T(8,128)(2,1)S(1)} collective-permute-done((bf16[8,512]{1,0:T(8,128)(2,1)S(1)}, bf16[8,512]{1,0:T(8,128)(2,1)S(1)}, u32[]{:S(2)}, u32[]{:S(2)}) %collective-permute-start.3) | collective-permute-done | bytes 8224 | tf_op jit(solution)/shard_map/ppermute | solution.py:55
  7.2 0.7 select_bitcast_fusion.3
  8.0 0.9 broadcast_in_dim.33
  8.8 15.8 %all-to-all-start = ((bf16[32,8,1024]{2,1,0:T(8,128)(2,1)}), bf16[32,8,1024]{2,1,0:T(8,128)(2,1)S(1)}, u32[]{:S(2)}, u32[]{:S(2)}) async-start(bf16[32,8,1024]{2,1,0:T(8,128)(2,1)} %broadcast_in_dim.33), calls=%async_computation | async-start | bytes 1048576 | tf_op jit(solution)/shard_map/all_to_all | solution.py:22
  24.7 2.3 %dynamic-slice_bitcast_fusion = (bf16[256,1024]{1,0:T(8,128)(2,1)S(1)}, bf16[256,1024]{1,0:T(8,128)(2,1)}, bf16[256,1024]{1,0:T(8,128)(2,1)S(1)}) fusion(bf16[1,256,4096]{2,1,0:T(8,128)(2,1)} %param.8, s32[]{:T(128)S(6)} %select_n.103, s32[]{:T(128)S(6)} %select_n.99, s32[]{:T(128)S(6)} %select_n.95), kind=kLoop, calls=%fused_computation.24 | loop fusion | bytes 3145740 | tf_op jit(solution)/shard_map/dynamic_slice | solution.py:48
  27.0 4.9 %collective-permute-start = (bf16[256,1024]{1,0:T(8,128)(2,1)S(1)}, bf16[256,1024]{1,0:T(8,128)(2,1)}, u32[]{:S(2)}, u32[]{:S(2)}) collective-permute-start(bf16[256,1024]{1,0:T(8,128)(2,1)S(1)} %get-tuple-element.6), channel_id=1, source_target_pairs={{0,4},{2,6},{4,0},{6,2},{1,5},{3,7},{5,1},{7,3},{8,12},{10,14},{12... | collective-permute-start | bytes 1572872 | tf_op jit(solution)/shard_map/ppermute | solution.py:50
  32.0 2.5 %collective-permute-start.1 = (bf16[256,1024]{1,0:T(8,128)(2,1)}, bf16[256,1024]{1,0:T(8,128)(2,1)}, u32[]{:S(2)}, u32[]{:S(2)}) collective-permute-start(bf16[256,1024]{1,0:T(8,128)(2,1)} %get-tuple-element.5), channel_id=1, source_target_pairs={{0,2},{2,4},{4,6},{6,0},{1,3},{3,5},{5,7},{7,1},{8,10},{10,12},{12... | collective-permute-start | bytes 1572872 | tf_op jit(solution)/shard_map/ppermute | solution.py:50
  34.5 4.6 %collective-permute-start.2 = (bf16[256,1024]{1,0:T(8,128)(2,1)S(1)}, bf16[256,1024]{1,0:T(8,128)(2,1)}, u32[]{:S(2)}, u32[]{:S(2)}) collective-permute-start(bf16[256,1024]{1,0:T(8,128)(2,1)S(1)} %get-tuple-element.4), channel_id=1, source_target_pairs={{0,6},{2,0},{4,2},{6,4},{1,7},{3,1},{5,3},{7,5},{8,14},{10,8},{12,... | collective-permute-start | bytes 1572872 | tf_op jit(solution)/shard_map/ppermute | solution.py:50
  39.1 6.3 %collective-permute-done = bf16[256,1024]{1,0:T(8,128)(2,1)} collective-permute-done((bf16[256,1024]{1,0:T(8,128)(2,1)S(1)}, bf16[256,1024]{1,0:T(8,128)(2,1)}, u32[]{:S(2)}, u32[]{:S(2)}) %collective-permute-start) | collective-permute-done | bytes 524320 | tf_op jit(solution)/shard_map/ppermute | solution.py:50
  45.4 0.3 broadcast_in_dim.28
  45.7 1.1 bitcast_dynamic-update-slice_fusion.2
  46.8 0.0 all-to-all-done
  46.8 1.9 %collective-permute-start.4 = (bf16[32,8,1024]{2,1,0:T(8,128)(2,1)S(1)}, bf16[32,8,1024]{2,1,0:T(8,128)(2,1)S(1)}, u32[]{:S(2)}, u32[]{:S(2)}) collective-permute-start(bf16[32,8,1024]{2,1,0:T(8,128)(2,1)S(1)} %all-to-all-done), channel_id=1, source_target_pairs={{0,8},{8,0},{1,9},{9,1},{2,10},{10,2},{3,11},{11,3},{4,12},{12,4},... | collective-permute-start | bytes 1572872 | tf_op jit(solution)/shard_map/ppermute | solution.py:57
  48.7 5.0 %collective-permute-done.1 = bf16[256,1024]{1,0:T(8,128)(2,1)} collective-permute-done((bf16[256,1024]{1,0:T(8,128)(2,1)}, bf16[256,1024]{1,0:T(8,128)(2,1)}, u32[]{:S(2)}, u32[]{:S(2)}) %collective-permute-start.1) | collective-permute-done | bytes 524320 | tf_op jit(solution)/shard_map/ppermute | solution.py:50
  53.7 1.1 bitcast_dynamic-update-slice_fusion.1
  54.8 0.0 collective-permute-done.2
  54.8 1.1 bitcast_dynamic-update-slice_fusion
  55.9 1.1 dynamic-slice_dynamic-update-slice_fusion
  57.0 0.0 collective-permute-done.4
  57.0 0.1 select_bitcast_fusion.1
  57.1 0.1 pad_maximum_fusion
  57.2 1.3 convolution_convert_fusion
  58.5 0.0 copy-start.1
  58.5 19.5 %all_to_all.20 = bf16[4,256,512]{2,1,0:T(8,128)(2,1)S(1)} all-to-all(bf16[4,256,512]{2,1,0:T(8,128)(2,1)S(1)} %bitcast.79), channel_id=1, replica_groups=mesh['zh'=4,'y'=8,'c'=2,'x'=4,'zl'=2] {'x'}, dimensions={0} | all-to-all | bytes 2097152 | tf_op jit(solution)/shard_map/all_to_all | solution.py:22
  78.0 0.1 convert_reduce_fusion
  78.1 0.0 copy-done.1
  78.2 0.1 fusion.11
  78.2 1.1 broadcast_in_dim.35
  79.3 4.2 %all-to-all-start.2 = ((bf16[4,256,512]{2,1,0:T(8,128)(2,1)}), bf16[4,256,512]{2,1,0:T(8,128)(2,1)}, u32[]{:S(2)}, u32[]{:S(2)}) async-start(bf16[4,256,512]{2,1,0:T(8,128)(2,1)} %broadcast_in_dim.35), calls=%async_computation.2 | async-start | bytes 2097152 | tf_op jit(solution)/shard_map/all_to_all | solution.py:22
  83.6 14.2 %all-to-all-done.2 = bf16[4,256,512]{2,1,0:T(8,128)(2,1)} async-done(((bf16[4,256,512]{2,1,0:T(8,128)(2,1)}), bf16[4,256,512]{2,1,0:T(8,128)(2,1)}, u32[]{:S(2)}, u32[]{:S(2)}) %all-to-all-start.2) | async-done | bytes 1048608 | tf_op jit(solution)/shard_map/all_to_all | solution.py:22
  97.8 2.0 %convolution_convert_fusion.1 = bf16[512,512]{1,0:T(8,128)(2,1)S(1)} fusion(bf16[1024,512]{1,0:T(8,128)(2,1)} %bitcast.20, bf16[1024,1024]{1,0:T(8,128)(2,1)S(1)} %bitcast.76, s32[]{:T(128)S(6)} %select_n.116), kind=kOutput, calls=%fused_computation.2 | convolution fusion | flops 537133056 | bytes 2621444 | tf_op jit(solution)/shard_map/dot_general | solution.py:69
  99.7 3.4 %collective-permute-start.5 = (bf16[512,512]{1,0:T(8,128)(2,1)S(1)}, bf16[512,512]{1,0:T(8,128)(2,1)S(1)}, u32[]{:S(2)}, u32[]{:S(2)}) collective-permute-start(bf16[512,512]{1,0:T(8,128)(2,1)S(1)} %convolution_convert_fusion.1), channel_id=1, source_target_pairs={{0,1},{1,0},{2,3},{3,2},{4,5},{5,4},{6,7},{7,6},{8,9},{9,8},{10,11... | collective-permute-start | bytes 1572872 | tf_op jit(solution)/shard_map/ppermute | solution.py:76
  103.1 2.5 %copy.10 = f32[1,512,512]{1,2,0:T(8,128)} copy(f32[1,512,512]{2,1,0:T(8,128)} %param.10) | data formatting | bytes 2097152 | tf_op args[4]
  105.6 2.6 %copy.12 = f32[1,512,512]{1,2,0:T(8,128)} copy(f32[1,512,512]{2,1,0:T(8,128)} %param.11) | data formatting | bytes 2097152 | tf_op args[5]
  108.2 4.9 %collective-permute-done.5 = bf16[512,512]{1,0:T(8,128)(2,1)S(1)} collective-permute-done((bf16[512,512]{1,0:T(8,128)(2,1)S(1)}, bf16[512,512]{1,0:T(8,128)(2,1)S(1)}, u32[]{:S(2)}, u32[]{:S(2)}) %collective-permute-start.5) | collective-permute-done | bytes 524320 | tf_op jit(solution)/shard_map/ppermute | solution.py:76
  113.1 3.1 %fusion.2 = f32[512,512]{1,0:T(8,128)S(1)} fusion(f32[1,512,512]{1,2,0:T(8,128)} %copy.12, bf16[512,512]{1,0:T(8,128)(2,1)S(1)} %collective-permute-done.5, bf16[1024,512]{1,0:T(8,128)(2,1)} %bitcast.20, bf16[1024,1024]{1,0:T(8,128)(2,1)S(1)} %bitcast.77, s32[]{:T(128)S(6)} %select_n.115, f32[1,512,512]{1,2,0:T(8,128)} %copy.10), kind=kOutput, calls=%fused_computation.7 | convolution fusion | flops 540016640 | bytes 5767172 | tf_op jit(solution)/shard_map/dot_general | solution.py:69
  116.2 0.0 copy-start
  116.2 0.0 copy-start.2
  116.3 0.0 copy-start.3
  116.3 0.9 copy-done
  117.2 1.9 %collective-permute-start.6 = (bf16[32,8,512]{2,1,0:T(8,128)(2,1)S(1)}, bf16[32,8,512]{2,1,0:T(8,128)(2,1)S(1)}, u32[]{:S(2)}, u32[]{:S(2)}) collective-permute-start(bf16[32,8,512]{2,1,0:T(8,128)(2,1)S(1)} %fusion.10), channel_id=1, source_target_pairs={{0,8},{8,0},{1,9},{9,1},{2,10},{10,2},{3,11},{11,3},{4,12},{12,4},... | collective-permute-start | bytes 786440 | tf_op jit(solution)/shard_map/ppermute | solution.py:86
  119.2 1.5 %collective-permute-done.6 = bf16[32,8,512]{2,1,0:T(8,128)(2,1)S(1)} collective-permute-done((bf16[32,8,512]{2,1,0:T(8,128)(2,1)S(1)}, bf16[32,8,512]{2,1,0:T(8,128)(2,1)S(1)}, u32[]{:S(2)}, u32[]{:S(2)}) %collective-permute-start.6) | collective-permute-done | bytes 262176 | tf_op jit(solution)/shard_map/ppermute | solution.py:86
  120.7 1.1 fusion.8
  121.8 27.0 %all_to_all.21 = bf16[32,8,512]{2,1,0:T(8,128)(2,1)S(1)} all-to-all(bf16[32,8,512]{2,1,0:T(8,128)(2,1)S(1)} %fusion.8), channel_id=1, replica_groups=mesh['zh'=4,'y'=8,'c'=2,'x'=4,'zl'=2] {'zh','y'}, dimensions={0} | all-to-all | bytes 524288 | tf_op jit(solution)/shard_map/all_to_all | solution.py:22
  148.9 0.0 copy-done.2
  148.9 0.0 copy-done.3
  148.9 0.6 multiply_subtract_fusion
  (3 shorter events, 0.1 us)
Async XLA Ops:
  1.4 5.9 %collective-permute-start.3 = (bf16[8,512]{1,0:T(8,128)(2,1)S(1)}, bf16[8,512]{1,0:T(8,128)(2,1)S(1)}, u32[]{:S(2)}, u32[]{:S(2)}) collective-permute-start(bf16[8,512]{1,0:T(8,128)(2,1)S(1)} %convert_bitcast_fusion), channel_id=1, source_target_pairs={{0,1},{1,0},{2,3},{3,2},{4,5},{5,4},{6,7},{7,6},{8,9},{9,8},{10,11... | collective-permute-start | bytes 24584 | tf_op jit(solution)/shard_map/ppermute | solution.py:55
  8.8 38.0 %all-to-all-start = ((bf16[32,8,1024]{2,1,0:T(8,128)(2,1)}), bf16[32,8,1024]{2,1,0:T(8,128)(2,1)S(1)}, u32[]{:S(2)}, u32[]{:S(2)}) async-start(bf16[32,8,1024]{2,1,0:T(8,128)(2,1)} %broadcast_in_dim.33), calls=%async_computation | async-start | bytes 1048576 | tf_op jit(solution)/shard_map/all_to_all | solution.py:22
  27.0 18.4 %collective-permute-start = (bf16[256,1024]{1,0:T(8,128)(2,1)S(1)}, bf16[256,1024]{1,0:T(8,128)(2,1)}, u32[]{:S(2)}, u32[]{:S(2)}) collective-permute-start(bf16[256,1024]{1,0:T(8,128)(2,1)S(1)} %get-tuple-element.6), channel_id=1, source_target_pairs={{0,4},{2,6},{4,0},{6,2},{1,5},{3,7},{5,1},{7,3},{8,12},{10,14},{12... | collective-permute-start | bytes 1572872 | tf_op jit(solution)/shard_map/ppermute | solution.py:50
  32.0 21.8 %collective-permute-start.1 = (bf16[256,1024]{1,0:T(8,128)(2,1)}, bf16[256,1024]{1,0:T(8,128)(2,1)}, u32[]{:S(2)}, u32[]{:S(2)}) collective-permute-start(bf16[256,1024]{1,0:T(8,128)(2,1)} %get-tuple-element.5), channel_id=1, source_target_pairs={{0,2},{2,4},{4,6},{6,0},{1,3},{3,5},{5,7},{7,1},{8,10},{10,12},{12... | collective-permute-start | bytes 1572872 | tf_op jit(solution)/shard_map/ppermute | solution.py:50
  34.5 20.3 %collective-permute-start.2 = (bf16[256,1024]{1,0:T(8,128)(2,1)S(1)}, bf16[256,1024]{1,0:T(8,128)(2,1)}, u32[]{:S(2)}, u32[]{:S(2)}) collective-permute-start(bf16[256,1024]{1,0:T(8,128)(2,1)S(1)} %get-tuple-element.4), channel_id=1, source_target_pairs={{0,6},{2,0},{4,2},{6,4},{1,7},{3,1},{5,3},{7,5},{8,14},{10,8},{12,... | collective-permute-start | bytes 1572872 | tf_op jit(solution)/shard_map/ppermute | solution.py:50
  46.8 10.2 %collective-permute-start.4 = (bf16[32,8,1024]{2,1,0:T(8,128)(2,1)S(1)}, bf16[32,8,1024]{2,1,0:T(8,128)(2,1)S(1)}, u32[]{:S(2)}, u32[]{:S(2)}) collective-permute-start(bf16[32,8,1024]{2,1,0:T(8,128)(2,1)S(1)} %all-to-all-done), channel_id=1, source_target_pairs={{0,8},{8,0},{1,9},{9,1},{2,10},{10,2},{3,11},{11,3},{4,12},{12,4},... | collective-permute-start | bytes 1572872 | tf_op jit(solution)/shard_map/ppermute | solution.py:57
  58.5 19.7 %copy-start.1 = (bf16[1,256,512]{2,1,0:T(8,128)(2,1)S(1)}, bf16[1,256,512]{2,1,0:T(8,128)(2,1)}, u32[]{:S(2)}) copy-start(bf16[1,256,512]{2,1,0:T(8,128)(2,1)} %param.9) | copy-start | bytes 786436
  79.3 18.4 %all-to-all-start.2 = ((bf16[4,256,512]{2,1,0:T(8,128)(2,1)}), bf16[4,256,512]{2,1,0:T(8,128)(2,1)}, u32[]{:S(2)}, u32[]{:S(2)}) async-start(bf16[4,256,512]{2,1,0:T(8,128)(2,1)} %broadcast_in_dim.35), calls=%async_computation.2 | async-start | bytes 2097152 | tf_op jit(solution)/shard_map/all_to_all | solution.py:22
  99.7 13.4 %collective-permute-start.5 = (bf16[512,512]{1,0:T(8,128)(2,1)S(1)}, bf16[512,512]{1,0:T(8,128)(2,1)S(1)}, u32[]{:S(2)}, u32[]{:S(2)}) collective-permute-start(bf16[512,512]{1,0:T(8,128)(2,1)S(1)} %convolution_convert_fusion.1), channel_id=1, source_target_pairs={{0,1},{1,0},{2,3},{3,2},{4,5},{5,4},{6,7},{7,6},{8,9},{9,8},{10,11... | collective-permute-start | bytes 1572872 | tf_op jit(solution)/shard_map/ppermute | solution.py:76
  116.2 1.0 copy-start
  116.2 32.6 %copy-start.2 = (f32[512,8]{0,1:T(8,128)S(1)}, f32[512,8]{0,1:T(8,128)}, u32[]{:S(2)}) copy-start(f32[512,8]{0,1:T(8,128)} %param.6) | copy-start | bytes 49156
  116.3 32.6 %copy-start.3 = (f32[512,8]{0,1:T(8,128)S(1)}, f32[512,8]{0,1:T(8,128)}, u32[]{:S(2)}) copy-start(f32[512,8]{0,1:T(8,128)} %param.7) | copy-start | bytes 49156
  117.2 3.4 %collective-permute-start.6 = (bf16[32,8,512]{2,1,0:T(8,128)(2,1)S(1)}, bf16[32,8,512]{2,1,0:T(8,128)(2,1)S(1)}, u32[]{:S(2)}, u32[]{:S(2)}) collective-permute-start(bf16[32,8,512]{2,1,0:T(8,128)(2,1)S(1)} %fusion.10), channel_id=1, source_target_pairs={{0,8},{8,0},{1,9},{9,1},{2,10},{10,2},{3,11},{11,3},{4,12},{12,4},... | collective-permute-start | bytes 786440 | tf_op jit(solution)/shard_map/ppermute | solution.py:86

commit v4 on v3

--- a/solution.py
+++ b/solution.py
@@ -38,29 +38,33 @@
     at_x, at_zl, at_c = lax.axis_index("x"), lax.axis_index("zl"), lax.axis_index("c")
     swap = [(0, 1), (1, 0)]
 
-    def ordered(mine, other, at, axis):
-        first = jnp.where(at == 0, mine, other)
-        return jnp.stack([first, jnp.where(at == 0, other, mine)], axis)
+    own = anchor.astype(jnp.bfloat16).T
+    half = spread(own, ("zl",) + FAR).reshape(2, far, owned, rows)
+    other = lax.ppermute(half, "c", swap)
+    first = jnp.where(at_c == 0, half, other)
+    start = jnp.stack([first, jnp.where(at_c == 0, other, half)], 2)
+    start = start.reshape(2, columns, rows)
 
     tok = tokens[0]
     held = jnp.zeros((nx, count, 2 * rows), tok.dtype)
-    for d in (2, 1, 3, 0):
+    for d in (0, 2, 1, 3):
         block = lax.dynamic_slice_in_dim(tok, (at_x + d) % nx * 2 * rows, 2 * rows, 1)
         if d:
             block = lax.ppermute(block, "x", [(i, (i + d) % nx) for i in range(nx)])
         held = lax.dynamic_update_slice_in_dim(held, block[None], (at_x - d) % nx, 0)
     held = held.reshape(nx * count, 2 * rows)
 
-    own = anchor.astype(jnp.bfloat16).T
-    pair = ordered(own, lax.ppermute(own, "zl", swap), at_zl, 1).reshape(owned, 2 * rows)
-    half = spread(pair, FAR)
-    start = ordered(half, lax.ppermute(half, "c", swap), at_c, 1)
-    start = start.reshape(columns, 2 * rows)
+    def project(at):
+        return lax.dot_general(
+            held[:, at * rows : (at + 1) * rows],
+            start[at],
+            (((1,), (1,)), ((), ())),
+            preferred_element_type=jnp.float32,
+        )
 
-    partial = lax.dot_general(
-        held, start, (((1,), (1,)), ((), ())), preferred_element_type=jnp.float32
-    ).astype(jnp.bfloat16)
-    parts = exchange(partial.reshape(nx, count, columns), "x").astype(jnp.float32)
+    partial = (project(0) + project(1)).astype(jnp.bfloat16)
+    partial = partial.reshape(nx, count, columns)
+    parts = exchange(partial, "x").astype(jnp.float32)
     projected = jnp.sum(parts, axis=0) * width ** (-0.5)
     residual = (projected - targets[0].astype(jnp.float32)).astype(jnp.bfloat16)
     residual = spread(residual, "x").reshape(nx * count, columns)
@@ -74,17 +78,22 @@
         )
 
     other = lax.ppermute(term(1 - at_zl).astype(jnp.bfloat16), "zl", swap)
-    summed = term(at_zl) + other.astype(jnp.float32)
-    gradient = summed * (1.0 / (math.sqrt(width) * groups * count))
-    moment_one = beta_one * first_moment[0].T + (1.0 - beta_one) * gradient
-    moment_two = beta_two * second_moment[0].T + (1.0 - beta_two) * gradient * gradient
-    direction = moment_one / (jnp.sqrt(moment_two) + adam_eps)
+    kept = lax.optimization_barrier(term(at_zl))
 
-    direction = direction.reshape(far, 2, owned, rows)
-    given = lax.dynamic_index_in_dim(direction, 1 - at_c, 1, keepdims=False)
-    kept = lax.dynamic_index_in_dim(direction, at_c, 1, keepdims=False)
-    given = lax.ppermute(given.astype(jnp.bfloat16), "c", swap)
-    sent = (kept + given.astype(jnp.float32)).astype(jnp.bfloat16)
+    def direct(at):
+        def of(a):
+            a = a.reshape(far, 2, owned, rows)
+            return lax.dynamic_index_in_dim(a, at, 1, keepdims=False)
+
+        summed = of(kept) + of(other).astype(jnp.float32)
+        gradient = summed * (1.0 / (math.sqrt(width) * groups * count))
+        moment_one = beta_one * of(first_moment[0].T) + (1.0 - beta_one) * gradient
+        squared = (1.0 - beta_two) * gradient * gradient
+        moment_two = beta_two * of(second_moment[0].T) + squared
+        return moment_one / (jnp.sqrt(moment_two) + adam_eps)
+
+    given = lax.ppermute(direct(1 - at_c).astype(jnp.bfloat16), "c", swap)
+    sent = (direct(at_c) + given.astype(jnp.float32)).astype(jnp.bfloat16)
     total = jnp.sum(exchange(sent, FAR).astype(jnp.float32), axis=0).T
 
     begin = anchor.astype(jnp.bfloat16).astype(jnp.float32)

time: 151 us -> 141 us (0.934)
  starting transfers between devices: 43.5 us -> 39.4 us
  local copies, waits for them, and re-layouts: 15 us -> 11 us
    all_to_all x2, waiting for transfers between devices: 14.2 us -> 19.6 us  [exchange(): return lax.all_to_all(blocks, axes, 0, 0)]
    ppermute x3 -> x2, starting transfers between devices: 8.11 us -> 3.83 us  [the longest x1 1.92 us: local(): given = lax.ppermute(direct(1 - at_c).astype(jnp.bfloat16), 'c', swap)]
    ppermute x3, waiting for transfers between devices: 11.3 us -> 7.39 us  [local(): block = lax.ppermute(block, 'x', [(i, (i + d) % nx) for i in range(nx)])]
    dynamic_update_slice x4 -> x3, local copies, waits for them, and re-layouts: 4.33 us -> 2.2 us  [local(): lax.dynamic_update_slice_in_dim(held, block[None], (at_x - d) % nx, 0)]
    convert_element_type x1 -> x2, other arithmetic: 1.11 us -> 2.8 us  [the longest x1 1.5 us: local(): sent = (direct(at_c) + given.astype(jnp.float32)).astype(jnp.bfloat16)]
    ppermute x3 -> x2, waiting for transfers between devices: 3.11 us -> 1.5 us  [the longest x1 1.5 us: local(): given = lax.ppermute(direct(1 - at_c).astype(jnp.bfloat16), 'c', swap)]
    unnamed x10 -> x18, local copies, waits for them, and re-layouts: 6.06 us -> 5.46 us
  transfers between devices with their start and end apart: 9 -> 8, of which waited for: 6 -> 5; matrix products, arithmetic and copies ran while one was open for 8% -> 7% of each run, Pallas kernels for 0% -> 0%
where the time goes in v4:
time: 141 us; the launch traced here: 140 us
  blocking collectives  46.6 us (33%)
  starting transfers between devices  39.4 us (28%)
  waiting for transfers between devices  32.5 us (23%)
  local copies, waits for them, and re-layouts  11 us (8%)
  matrix products  5.1 us (4%)
  other arithmetic  4.59 us (3%)
    all_to_all x2, blocking collectives, exchange(): return lax.all_to_all(blocks, axes, 0, 0)  46.6 us
    all_to_all x2, starting transfers between devices, exchange(): return lax.all_to_all(blocks, axes, 0, 0)  20.1 us
    all_to_all x2, waiting for transfers between devices, exchange(): return lax.all_to_all(blocks, axes, 0, 0)  19.6 us
    ppermute x3, starting transfers between devices, local(): block = lax.ppermute(block, 'x', [(i, (i + d) % nx) for i in range(nx)])  12 us
    ppermute x3, waiting for transfers between devices, local(): block = lax.ppermute(block, 'x', [(i, (i + d) % nx) for i in range(nx)])  7.39 us
    unnamed x18, local copies, waits for them, and re-layouts  5.46 us
    ppermute x1, waiting for transfers between devices, local(): other = lax.ppermute(term(1 - at_zl).astype(jnp.bfloat16), 'zl', swap)  4.01 us
    dot_general x2, matrix products, term(): lax.dot_general(residual, lax.dynamic_slice_in_dim(held, at * rows, rows,...  3.59 us
  transfers between devices with their start and end apart: 8, of which 5 were waited for; matrix products, arithmetic and copies ran while one was open for 7% of the time, Pallas kernels for 0%

profile of v4, /device:TPU:8, one launch (start us, length us, event | category | flops | bytes accessed | tf_op | source)
XLA Modules:
  0.0 140.2 jit_solution(16935747701322239360)
XLA Ops:
  0.6 0.7 convert_bitcast_fusion
  1.4 0.9 broadcast_in_dim.31
  2.2 16.6 %all-to-all-start = ((bf16[64,8,512]{2,1,0:T(8,128)(2,1)}), bf16[64,8,512]{2,1,0:T(8,128)(2,1)S(1)}, u32[]{:S(2)}, u32[]{:S(2)}) async-start(bf16[64,8,512]{2,1,0:T(8,128)(2,1)} %broadcast_in_dim.31), calls=%async_computation | async-start | bytes 1048576 | tf_op jit(solution)/shard_map/all_to_all | solution.py:22
  18.9 0.0 copy-start.2
  18.9 0.3 broadcast_in_dim.27
  19.1 1.3 copy-done.2
  20.5 1.2 dynamic-slice_bitcast_fusion
  21.7 4.9 %collective-permute-start = (bf16[256,1024]{1,0:T(8,128)(2,1)}, bf16[256,1024]{1,0:T(8,128)(2,1)}, u32[]{:S(2)}, u32[]{:S(2)}) collective-permute-start(bf16[256,1024]{1,0:T(8,128)(2,1)} %get-tuple-element.5), channel_id=1, source_target_pairs={{0,4},{2,6},{4,0},{6,2},{1,5},{3,7},{5,1},{7,3},{8,12},{10,14},{12... | collective-permute-start | bytes 1572872 | tf_op jit(solution)/shard_map/ppermute | solution.py:53
  26.6 2.5 %collective-permute-start.1 = (bf16[256,1024]{1,0:T(8,128)(2,1)}, bf16[256,1024]{1,0:T(8,128)(2,1)}, u32[]{:S(2)}, u32[]{:S(2)}) collective-permute-start(bf16[256,1024]{1,0:T(8,128)(2,1)} %get-tuple-element.7), channel_id=1, source_target_pairs={{0,2},{2,4},{4,6},{6,0},{1,3},{3,5},{5,7},{7,1},{8,10},{10,12},{12... | collective-permute-start | bytes 1572872 | tf_op jit(solution)/shard_map/ppermute | solution.py:53
  29.1 4.6 %collective-permute-start.2 = (bf16[256,1024]{1,0:T(8,128)(2,1)}, bf16[256,1024]{1,0:T(8,128)(2,1)S(1)}, u32[]{:S(2)}, u32[]{:S(2)}) collective-permute-start(bf16[256,1024]{1,0:T(8,128)(2,1)} %get-tuple-element.4), channel_id=1, source_target_pairs={{0,6},{2,0},{4,2},{6,4},{1,7},{3,1},{5,3},{7,5},{8,14},{10,8},{12,... | collective-permute-start | bytes 1572872 | tf_op jit(solution)/shard_map/ppermute | solution.py:53
  33.7 5.6 %all-to-all-done = bf16[64,8,512]{2,1,0:T(8,128)(2,1)S(1)} async-done(((bf16[64,8,512]{2,1,0:T(8,128)(2,1)}), bf16[64,8,512]{2,1,0:T(8,128)(2,1)S(1)}, u32[]{:S(2)}, u32[]{:S(2)}) %all-to-all-start) | async-done | bytes 524320 | tf_op jit(solution)/shard_map/all_to_all | solution.py:22
  39.3 1.9 %collective-permute-start.3 = (bf16[2,32,8,512]{3,2,1,0:T(8,128)(2,1)S(1)}, bf16[2,32,8,512]{3,2,1,0:T(8,128)(2,1)S(1)}, u32[]{:S(2)}, u32[]{:S(2)}) collective-permute-start(bf16[2,32,8,512]{3,2,1,0:T(8,128)(2,1)S(1)} %bitcast.160), channel_id=1, source_target_pairs={{0,8},{8,0},{1,9},{9,1},{2,10},{10,2},{3,11},{11,3},{4,12},{12,4},... | collective-permute-start | bytes 1572872 | tf_op jit(solution)/shard_map/ppermute | solution.py:43
  41.2 0.0 collective-permute-done
  41.2 1.1 bitcast_dynamic-update-slice_fusion.2
  42.3 7.4 %collective-permute-done.1 = bf16[256,1024]{1,0:T(8,128)(2,1)} collective-permute-done((bf16[256,1024]{1,0:T(8,128)(2,1)}, bf16[256,1024]{1,0:T(8,128)(2,1)}, u32[]{:S(2)}, u32[]{:S(2)}) %collective-permute-start.1) | collective-permute-done | bytes 524320 | tf_op jit(solution)/shard_map/ppermute | solution.py:53
  49.7 1.1 bitcast_dynamic-update-slice_fusion.1
  50.8 0.0 collective-permute-done.2
  50.8 0.0 collective-permute-done.3
  50.9 0.1 select_bitcast_fusion.1
  50.9 0.1 fusion.6
  51.0 0.7 fusion
  51.8 0.8 add_convert_fusion
  52.6 0.0 copy-start.5
  52.6 19.5 %all_to_all.20 = bf16[4,256,512]{2,1,0:T(8,128)(2,1)S(1)} all-to-all(bf16[4,256,512]{2,1,0:T(8,128)(2,1)S(1)} %bitcast.159), channel_id=1, replica_groups=mesh['zh'=4,'y'=8,'c'=2,'x'=4,'zl'=2] {'x'}, dimensions={0} | all-to-all | bytes 2097152 | tf_op jit(solution)/shard_map/all_to_all | solution.py:22
  72.1 0.1 convert_reduce_fusion
  72.2 0.0 copy-done.5
  72.2 0.1 fusion.22
  72.3 1.1 broadcast_in_dim.33
  73.4 3.5 %all-to-all-start.2 = ((bf16[4,256,512]{2,1,0:T(8,128)(2,1)}), bf16[4,256,512]{2,1,0:T(8,128)(2,1)S(1)}, u32[]{:S(2)}, u32[]{:S(2)}) async-start(bf16[4,256,512]{2,1,0:T(8,128)(2,1)} %broadcast_in_dim.33), calls=%async_computation.2 | async-start | bytes 2097152 | tf_op jit(solution)/shard_map/all_to_all | solution.py:22
  76.9 14.1 %all-to-all-done.2 = bf16[4,256,512]{2,1,0:T(8,128)(2,1)S(1)} async-done(((bf16[4,256,512]{2,1,0:T(8,128)(2,1)}), bf16[4,256,512]{2,1,0:T(8,128)(2,1)S(1)}, u32[]{:S(2)}, u32[]{:S(2)}) %all-to-all-start.2) | async-done | bytes 1048608 | tf_op jit(solution)/shard_map/all_to_all | solution.py:22
  91.0 0.0 copy-start.4
  91.0 1.5 %convolution_convert_fusion = bf16[512,512]{1,0:T(8,128)(2,1)} fusion(bf16[1024,512]{1,0:T(8,128)(2,1)S(1)} %bitcast.166, bf16[1024,1024]{1,0:T(8,128)(2,1)S(1)} %bitcast.153, s32[]{:T(128)S(6)} %select_n.109), kind=kOutput, calls=%fused_computation.2 | convolution fusion | flops 537133056 | bytes 2621444 | tf_op jit(solution)/shard_map/dot_general | solution.py:73
  92.5 3.5 %collective-permute-start.4 = (bf16[512,512]{1,0:T(8,128)(2,1)}, bf16[512,512]{1,0:T(8,128)(2,1)}, u32[]{:S(2)}, u32[]{:S(2)}) collective-permute-start(bf16[512,512]{1,0:T(8,128)(2,1)} %convolution_convert_fusion), channel_id=1, source_target_pairs={{0,1},{1,0},{2,3},{3,2},{4,5},{5,4},{6,7},{7,6},{8,9},{9,8},{10,11... | collective-permute-start | bytes 1572872 | tf_op jit(solution)/shard_map/ppermute | solution.py:80
  96.0 0.0 copy-done.4
  96.0 1.6 %copy.21 = f32[1,512,512]{1,2,0:T(8,128)S(1)} copy(f32[1,512,512]{2,1,0:T(8,128)} %param.10) | data formatting | bytes 2097152 | tf_op args[4]
  97.6 2.5 %copy.26 = f32[1,512,512]{1,2,0:T(8,128)} copy(f32[1,512,512]{2,1,0:T(8,128)} %param.11) | data formatting | bytes 2097152 | tf_op args[5]
  100.1 0.0 copy-start
  100.1 2.0 %fusion.4 = f32[512,512]{1,0:T(8,128)S(1)} fusion(bf16[1024,512]{1,0:T(8,128)(2,1)} %bitcast.167, bf16[1024,1024]{1,0:T(8,128)(2,1)S(1)} %bitcast.154, s32[]{:T(128)S(6)} %select_n.108), kind=kOutput, calls=%fused_computation.9 | convolution fusion | flops 536870912 | bytes 3145732 | tf_op jit(solution)/shard_map/dot_general | solution.py:73
  102.2 0.0 copy-start.3
  102.2 0.0 copy-start.1
  102.2 4.0 %collective-permute-done.4 = bf16[512,512]{1,0:T(8,128)(2,1)} collective-permute-done((bf16[512,512]{1,0:T(8,128)(2,1)}, bf16[512,512]{1,0:T(8,128)(2,1)}, u32[]{:S(2)}, u32[]{:S(2)}) %collective-permute-start.4) | collective-permute-done | bytes 524320 | tf_op jit(solution)/shard_map/ppermute | solution.py:80
  106.2 0.0 copy-done
  106.2 1.3 fusion.23
  107.5 0.0 copy-done.3
  107.5 0.0 copy-start.6
  107.5 0.0 copy-start.7
  107.6 1.9 %collective-permute-start.5 = (bf16[32,8,512]{2,1,0:T(8,128)(2,1)S(1)}, bf16[32,8,512]{2,1,0:T(8,128)(2,1)S(1)}, u32[]{:S(2)}, u32[]{:S(2)}) collective-permute-start(bf16[32,8,512]{2,1,0:T(8,128)(2,1)S(1)} %fusion.23), channel_id=1, source_target_pairs={{0,8},{8,0},{1,9},{9,1},{2,10},{10,2},{3,11},{11,3},{4,12},{12,4},... | collective-permute-start | bytes 786440 | tf_op jit(solution)/shard_map/ppermute | solution.py:95
  109.5 1.5 %collective-permute-done.5 = bf16[32,8,512]{2,1,0:T(8,128)(2,1)S(1)} collective-permute-done((bf16[32,8,512]{2,1,0:T(8,128)(2,1)S(1)}, bf16[32,8,512]{2,1,0:T(8,128)(2,1)S(1)}, u32[]{:S(2)}, u32[]{:S(2)}) %collective-permute-start.5) | collective-permute-done | bytes 262176 | tf_op jit(solution)/shard_map/ppermute | solution.py:95
  111.0 0.0 copy-done.1
  111.0 1.5 %fusion.21 = bf16[32,8,512]{2,1,0:T(8,128)(2,1)S(1)} fusion(bf16[32,8,512]{2,1,0:T(8,128)(2,1)S(1)} %collective-permute-done.5, f32[32,2,8,512]{3,2,1,0:T(8,128)S(1)} %bitcast.158, s32[]{:T(128)S(6)} %select_n.89, f32[32,2,8,512]{3,2,1,0:T(8,128)} %bitcast.165, f32[32,2,8,512]{3,2,1,0:T(8,128)S(1)} %bitcast.156, bf16[32,2,8,512]{3,2,1,0:T(8,128)(2,1)} %bitcast.22), kind=kLoop, calls=%fused_computation.45 | loop fusion | flops 1966080 | bytes 2359300 | tf_op jit(solution)/shard_map/convert_element_type | solution.py:96
  112.5 27.1 %all_to_all.21 = bf16[32,8,512]{2,1,0:T(8,128)(2,1)S(1)} all-to-all(bf16[32,8,512]{2,1,0:T(8,128)(2,1)S(1)} %fusion.21), channel_id=1, replica_groups=mesh['zh'=4,'y'=8,'c'=2,'x'=4,'zl'=2] {'zh','y'}, dimensions={0} | all-to-all | bytes 524288 | tf_op jit(solution)/shard_map/all_to_all | solution.py:22
  139.6 0.0 copy-done.6
  139.6 0.0 copy-done.7
  139.6 0.6 multiply_subtract_fusion
  (2 shorter events, 0.1 us)
Async XLA Ops:
  2.2 37.1 %all-to-all-start = ((bf16[64,8,512]{2,1,0:T(8,128)(2,1)}), bf16[64,8,512]{2,1,0:T(8,128)(2,1)S(1)}, u32[]{:S(2)}, u32[]{:S(2)}) async-start(bf16[64,8,512]{2,1,0:T(8,128)(2,1)} %broadcast_in_dim.31), calls=%async_computation | async-start | bytes 1048576 | tf_op jit(solution)/shard_map/all_to_all | solution.py:22
  18.9 1.6 %copy-start.2 = (bf16[1,256,4096]{2,1,0:T(8,128)(2,1)S(1)}, bf16[1,256,4096]{2,1,0:T(8,128)(2,1)}, u32[]{:S(2)}) copy-start(bf16[1,256,4096]{2,1,0:T(8,128)(2,1)} %param.8) | copy-start | bytes 6291460
  21.7 19.6 %collective-permute-start = (bf16[256,1024]{1,0:T(8,128)(2,1)}, bf16[256,1024]{1,0:T(8,128)(2,1)}, u32[]{:S(2)}, u32[]{:S(2)}) collective-permute-start(bf16[256,1024]{1,0:T(8,128)(2,1)} %get-tuple-element.5), channel_id=1, source_target_pairs={{0,4},{2,6},{4,0},{6,2},{1,5},{3,7},{5,1},{7,3},{8,12},{10,14},{12... | collective-permute-start | bytes 1572872 | tf_op jit(solution)/shard_map/ppermute | solution.py:53
  26.6 23.1 %collective-permute-start.1 = (bf16[256,1024]{1,0:T(8,128)(2,1)}, bf16[256,1024]{1,0:T(8,128)(2,1)}, u32[]{:S(2)}, u32[]{:S(2)}) collective-permute-start(bf16[256,1024]{1,0:T(8,128)(2,1)} %get-tuple-element.7), channel_id=1, source_target_pairs={{0,2},{2,4},{4,6},{6,0},{1,3},{3,5},{5,7},{7,1},{8,10},{10,12},{12... | collective-permute-start | bytes 1572872 | tf_op jit(solution)/shard_map/ppermute | solution.py:53
  29.1 21.7 %collective-permute-start.2 = (bf16[256,1024]{1,0:T(8,128)(2,1)}, bf16[256,1024]{1,0:T(8,128)(2,1)S(1)}, u32[]{:S(2)}, u32[]{:S(2)}) collective-permute-start(bf16[256,1024]{1,0:T(8,128)(2,1)} %get-tuple-element.4), channel_id=1, source_target_pairs={{0,6},{2,0},{4,2},{6,4},{1,7},{3,1},{5,3},{7,5},{8,14},{10,8},{12,... | collective-permute-start | bytes 1572872 | tf_op jit(solution)/shard_map/ppermute | solution.py:53
  39.3 11.5 %collective-permute-start.3 = (bf16[2,32,8,512]{3,2,1,0:T(8,128)(2,1)S(1)}, bf16[2,32,8,512]{3,2,1,0:T(8,128)(2,1)S(1)}, u32[]{:S(2)}, u32[]{:S(2)}) collective-permute-start(bf16[2,32,8,512]{3,2,1,0:T(8,128)(2,1)S(1)} %bitcast.160), channel_id=1, source_target_pairs={{0,8},{8,0},{1,9},{9,1},{2,10},{10,2},{3,11},{11,3},{4,12},{12,4},... | collective-permute-start | bytes 1572872 | tf_op jit(solution)/shard_map/ppermute | solution.py:43
  52.6 19.7 %copy-start.5 = (bf16[1,256,512]{2,1,0:T(8,128)(2,1)S(1)}, bf16[1,256,512]{2,1,0:T(8,128)(2,1)}, u32[]{:S(2)}) copy-start(bf16[1,256,512]{2,1,0:T(8,128)(2,1)} %param.9) | copy-start | bytes 786436
  73.4 17.6 %all-to-all-start.2 = ((bf16[4,256,512]{2,1,0:T(8,128)(2,1)}), bf16[4,256,512]{2,1,0:T(8,128)(2,1)S(1)}, u32[]{:S(2)}, u32[]{:S(2)}) async-start(bf16[4,256,512]{2,1,0:T(8,128)(2,1)} %broadcast_in_dim.33), calls=%async_computation.2 | async-start | bytes 2097152 | tf_op jit(solution)/shard_map/all_to_all | solution.py:22
  91.0 5.0 %copy-start.4 = (bf16[4,256,512]{2,1,0:T(8,128)(2,1)}, bf16[4,256,512]{2,1,0:T(8,128)(2,1)S(1)}, u32[]{:S(2)}) copy-start(bf16[4,256,512]{2,1,0:T(8,128)(2,1)S(1)} %all-to-all-done.2) | copy-start | bytes 3145732
  92.5 13.7 %collective-permute-start.4 = (bf16[512,512]{1,0:T(8,128)(2,1)}, bf16[512,512]{1,0:T(8,128)(2,1)}, u32[]{:S(2)}, u32[]{:S(2)}) collective-permute-start(bf16[512,512]{1,0:T(8,128)(2,1)} %convolution_convert_fusion), channel_id=1, source_target_pairs={{0,1},{1,0},{2,3},{3,2},{4,5},{5,4},{6,7},{7,6},{8,9},{9,8},{10,11... | collective-permute-start | bytes 1572872 | tf_op jit(solution)/shard_map/ppermute | solution.py:80
  100.1 6.1 %copy-start = (f32[1,512,512]{1,2,0:T(8,128)S(1)}, f32[1,512,512]{1,2,0:T(8,128)}, u32[]{:S(2)}) copy-start(f32[1,512,512]{1,2,0:T(8,128)} %copy.26) | copy-start | bytes 3145732
  102.2 5.3 %copy-start.3 = (f32[512,512]{1,0:T(8,128)}, f32[512,512]{1,0:T(8,128)S(1)}, u32[]{:S(2)}) copy-start(f32[512,512]{1,0:T(8,128)S(1)} %fusion.4) | copy-start | bytes 3145732
  102.2 8.8 %copy-start.1 = (f32[1,512,512]{1,2,0:T(8,128)S(1)}, f32[1,512,512]{1,2,0:T(8,128)}, u32[]{:S(2)}) copy-start(f32[1,512,512]{1,2,0:T(8,128)} %copy.26) | copy-start | bytes 3145732
  107.5 32.1 %copy-start.6 = (f32[512,8]{0,1:T(8,128)S(1)}, f32[512,8]{0,1:T(8,128)}, u32[]{:S(2)}) copy-start(f32[512,8]{0,1:T(8,128)} %param.6) | copy-start | bytes 49156
  107.5 32.1 %copy-start.7 = (f32[512,8]{0,1:T(8,128)S(1)}, f32[512,8]{0,1:T(8,128)}, u32[]{:S(2)}) copy-start(f32[512,8]{0,1:T(8,128)} %param.7) | copy-start | bytes 49156
  107.6 3.4 %collective-permute-start.5 = (bf16[32,8,512]{2,1,0:T(8,128)(2,1)S(1)}, bf16[32,8,512]{2,1,0:T(8,128)(2,1)S(1)}, u32[]{:S(2)}, u32[]{:S(2)}) collective-permute-start(bf16[32,8,512]{2,1,0:T(8,128)(2,1)S(1)} %fusion.23), channel_id=1, source_target_pairs={{0,8},{8,0},{1,9},{9,1},{2,10},{10,2},{3,11},{11,3},{4,12},{12,4},... | collective-permute-start | bytes 786440 | tf_op jit(solution)/shard_map/ppermute | solution.py:95

commit v5 on v4

--- a/solution.py
+++ b/solution.py
@@ -46,12 +46,30 @@
     start = start.reshape(2, columns, rows)
 
     tok = tokens[0]
+    right = [(i, (i + 1) % nx) for i in range(nx)]
+    left = [(i, (i - 1) % nx) for i in range(nx)]
+
+    def cut(x, first, size):
+        at = (at_x + x) % nx * 2 * rows + first
+        return lax.dynamic_slice_in_dim(tok, at, size, 1)
+
+    def merge(*parts):
+        return jnp.concatenate(parts, axis=1)
+
+    from_left = lax.ppermute(merge(cut(1, 0, 2 * rows), cut(2, 0, rows)), "x", right)
+    from_right = lax.ppermute(merge(cut(3, 0, 2 * rows), cut(2, rows, rows)), "x", left)
+    far_left = lax.ppermute(from_left[:, 2 * rows :], "x", right)
+    far_right = lax.ppermute(from_right[:, 2 * rows :], "x", left)
+
     held = jnp.zeros((nx, count, 2 * rows), tok.dtype)
-    for d in (0, 2, 1, 3):
-        block = lax.dynamic_slice_in_dim(tok, (at_x + d) % nx * 2 * rows, 2 * rows, 1)
-        if d:
-            block = lax.ppermute(block, "x", [(i, (i + d) % nx) for i in range(nx)])
-        held = lax.dynamic_update_slice_in_dim(held, block[None], (at_x - d) % nx, 0)
+    for d, first, block in (
+        (0, 0, cut(0, 0, 2 * rows)),
+        (3, 0, from_left[:, : 2 * rows]),
+        (1, 0, from_right[:, : 2 * rows]),
+        (2, 0, far_left),
+        (2, rows, far_right),
+    ):
+        held = lax.dynamic_update_slice(held, block[None], ((at_x + d) % nx, 0, first))
     held = held.reshape(nx * count, 2 * rows)
 
     def project(at):

time: 141 us -> 135 us (0.957)
  blocking collectives: 46.6 us -> 37.9 us
  local copies, waits for them, and re-layouts: 11 us -> 13.8 us
    all_to_all x2, blocking collectives: 46.6 us -> 37.9 us  [exchange(): return lax.all_to_all(blocks, axes, 0, 0)]
    ppermute x3 -> x4, waiting for transfers between devices: 7.39 us -> 0.01 us  [the longest x1 0.01 us: local(): lax.ppermute(merge(cut(1, 0, 2 * rows), cut(2, 0, rows)), 'x', right)]
    all_to_all x2, waiting for transfers between devices: 19.6 us -> 24 us  [exchange(): return lax.all_to_all(blocks, axes, 0, 0)]
    slice x0 -> x2, local copies, waits for them, and re-layouts: none -> 2.64 us  [the longest x1 1.67 us: local(): far_left = lax.ppermute(from_left[:, 2 * rows:], 'x', right)]
    ppermute x3 -> x4, starting transfers between devices: 12 us -> 14.1 us  [the longest x1 4.86 us: local(): far_right = lax.ppermute(from_right[:, 2 * rows:], 'x', left)]
    ppermute x1, waiting for transfers between devices: 4.01 us -> 5.59 us  [local(): other = lax.ppermute(term(1 - at_zl).astype(jnp.bfloat16), 'zl', swap)]
    dynamic_update_slice x3 -> x4, local copies, waits for them, and re-layouts: 2.2 us -> 3.17 us  [local(): lax.dynamic_update_slice(held, block[None], ((at_x + d) % nx, 0, first))]
  transfers between devices with their start and end apart: 8 -> 9, of which waited for: 5 -> 4; matrix products, arithmetic and copies ran while one was open for 7% -> 10% of each run, Pallas kernels for 0% -> 0%
where the time goes in v5:
time: 135 us
  starting transfers between devices  40.7 us (30%)
  blocking collectives  37.9 us (28%)
  waiting for transfers between devices  31.1 us (23%)
  local copies, waits for them, and re-layouts  13.8 us (10%)
  matrix products  5.09 us (4%)
  other arithmetic  4.86 us (4%)
    all_to_all x2, blocking collectives, exchange(): return lax.all_to_all(blocks, axes, 0, 0)  37.9 us
    all_to_all x2, waiting for transfers between devices, exchange(): return lax.all_to_all(blocks, axes, 0, 0)  24 us
    all_to_all x2, starting transfers between devices, exchange(): return lax.all_to_all(blocks, axes, 0, 0)  20.1 us
    ppermute x1, waiting for transfers between devices, local(): other = lax.ppermute(term(1 - at_zl).astype(jnp.bfloat16), 'zl', swap)  5.59 us
    ppermute x1, starting transfers between devices, local(): far_right = lax.ppermute(from_right[:, 2 * rows:], 'x', left)  4.86 us
    unnamed x18, local copies, waits for them, and re-layouts  4.4 us
    ppermute x1, starting transfers between devices, local(): lax.ppermute(merge(cut(3, 0, 2 * rows), cut(2, rows, rows)), 'x', left)  3.65 us
    dot_general x2, matrix products, term(): lax.dot_general(residual, lax.dynamic_slice_in_dim(held, at * rows, rows,...  3.58 us
  transfers between devices with their start and end apart: 9, of which 4 were waited for; matrix products, arithmetic and copies ran while one was open for 10% of the time, Pallas kernels for 0%

profile of v5, /device:TPU:8, one launch (start us, length us, event | category | flops | bytes accessed | tf_op | source)
XLA Modules:
  0.0 134.5 jit_solution(5167804247237324400)
XLA Ops:
  0.7 0.0 copy-start.2
  0.7 1.2 dynamic-slice_bitcast_fusion.2
  1.9 0.3 broadcast_in_dim.30
  2.2 0.3 copy-done.2
  2.5 0.2 dynamic-slice_bitcast_fusion
  2.6 0.0 copy-start.6
  2.6 0.9 pad_maximum_fusion
  3.6 3.4 %collective-permute-start = (bf16[256,1536]{1,0:T(8,128)(2,1)}, bf16[256,1536]{1,0:T(8,128)(2,1)}, u32[]{:S(2)}, u32[]{:S(2)}) collective-permute-start(bf16[256,1536]{1,0:T(8,128)(2,1)} %pad_maximum_fusion), channel_id=1, source_target_pairs={{0,2},{2,4},{4,6},{6,0},{1,3},{3,5},{5,7},{7,1},{8,10},{10,12},{12... | collective-permute-start | bytes 2359304 | tf_op jit(solution)/shard_map/ppermute | solution.py:59
  7.0 0.1 pad_maximum_fusion.1
  7.0 3.7 %collective-permute-start.1 = (bf16[256,1536]{1,0:T(8,128)(2,1)S(1)}, bf16[256,1536]{1,0:T(8,128)(2,1)}, u32[]{:S(2)}, u32[]{:S(2)}) collective-permute-start(bf16[256,1536]{1,0:T(8,128)(2,1)S(1)} %pad_maximum_fusion.1), channel_id=1, source_target_pairs={{0,6},{2,0},{4,2},{6,4},{1,7},{3,1},{5,3},{7,5},{8,14},{10,8},{12,... | collective-permute-start | bytes 2359304 | tf_op jit(solution)/shard_map/ppermute | solution.py:60
  10.7 0.0 copy-done.6
  10.7 0.8 broadcast_in_dim.35
  11.6 16.6 %all-to-all-start = ((bf16[64,8,512]{2,1,0:T(8,128)(2,1)}), bf16[64,8,512]{2,1,0:T(8,128)(2,1)S(1)}, u32[]{:S(2)}, u32[]{:S(2)}) async-start(bf16[64,8,512]{2,1,0:T(8,128)(2,1)} %broadcast_in_dim.35), calls=%async_computation | async-start | bytes 1048576 | tf_op jit(solution)/shard_map/all_to_all | solution.py:22
  28.2 0.0 collective-permute-done
  28.2 1.7 %slice.36 = bf16[256,512]{1,0:T(8,128)(2,1)} slice(bf16[256,1536]{1,0:T(8,128)(2,1)} %collective-permute-done), slice={[0:256], [1024:1536]} | slice | bytes 524288 | tf_op jit(solution)/shard_map/slice | solution.py:61
  29.9 2.2 %collective-permute-start.2 = (bf16[256,512]{1,0:T(8,128)(2,1)}, bf16[256,512]{1,0:T(8,128)(2,1)}, u32[]{:S(2)}, u32[]{:S(2)}) collective-permute-start(bf16[256,512]{1,0:T(8,128)(2,1)} %slice.36), channel_id=1, source_target_pairs={{0,2},{2,4},{4,6},{6,0},{1,3},{3,5},{5,7},{7,1},{8,10},{10,12},{12... | collective-permute-start | bytes 786440 | tf_op jit(solution)/shard_map/ppermute | solution.py:61
  32.0 0.0 collective-permute-done.1
  32.1 1.0 slice.37
  33.0 4.9 %collective-permute-start.3 = (bf16[256,512]{1,0:T(8,128)(2,1)S(1)}, bf16[256,512]{1,0:T(8,128)(2,1)S(1)}, u32[]{:S(2)}, u32[]{:S(2)}) collective-permute-start(bf16[256,512]{1,0:T(8,128)(2,1)S(1)} %slice.37), channel_id=1, source_target_pairs={{0,6},{2,0},{4,2},{6,4},{1,7},{3,1},{5,3},{7,5},{8,14},{10,8},{12,... | collective-permute-start | bytes 786440 | tf_op jit(solution)/shard_map/ppermute | solution.py:62
  37.9 1.1 fusion.8
  39.0 9.1 %all-to-all-done = bf16[64,8,512]{2,1,0:T(8,128)(2,1)S(1)} async-done(((bf16[64,8,512]{2,1,0:T(8,128)(2,1)}), bf16[64,8,512]{2,1,0:T(8,128)(2,1)S(1)}, u32[]{:S(2)}, u32[]{:S(2)}) %all-to-all-start) | async-done | bytes 524320 | tf_op jit(solution)/shard_map/all_to_all | solution.py:22
  48.1 1.9 %collective-permute-start.4 = (bf16[2,32,8,512]{3,2,1,0:T(8,128)(2,1)S(1)}, bf16[2,32,8,512]{3,2,1,0:T(8,128)(2,1)S(1)}, u32[]{:S(2)}, u32[]{:S(2)}) collective-permute-start(bf16[2,32,8,512]{3,2,1,0:T(8,128)(2,1)S(1)} %bitcast.168), channel_id=1, source_target_pairs={{0,8},{8,0},{1,9},{9,1},{2,10},{10,2},{3,11},{11,3},{4,12},{12,4},... | collective-permute-start | bytes 1572872 | tf_op jit(solution)/shard_map/ppermute | solution.py:43
  50.0 1.1 fusion.7
  51.1 0.0 collective-permute-done.2
  51.1 1.0 bitcast_dynamic-update-slice_fusion.1
  52.1 0.0 collective-permute-done.3
  52.1 0.0 collective-permute-done.4
  52.1 0.1 select_bitcast_fusion.1
  52.2 0.1 fusion.6
  52.3 0.7 fusion
  53.1 0.8 add_convert_fusion
  53.9 0.0 copy-start.5
  53.9 18.8 %all_to_all.20 = bf16[4,256,512]{2,1,0:T(8,128)(2,1)S(1)} all-to-all(bf16[4,256,512]{2,1,0:T(8,128)(2,1)S(1)} %bitcast.167), channel_id=1, replica_groups=mesh['zh'=4,'y'=8,'c'=2,'x'=4,'zl'=2] {'x'}, dimensions={0} | all-to-all | bytes 2097152 | tf_op jit(solution)/shard_map/all_to_all | solution.py:22
  72.6 0.1 convert_reduce_fusion
  72.8 0.0 copy-done.5
  72.8 0.1 fusion.24
  72.9 1.1 broadcast_in_dim.37
  73.9 3.5 %all-to-all-start.2 = ((bf16[4,256,512]{2,1,0:T(8,128)(2,1)}), bf16[4,256,512]{2,1,0:T(8,128)(2,1)S(1)}, u32[]{:S(2)}, u32[]{:S(2)}) async-start(bf16[4,256,512]{2,1,0:T(8,128)(2,1)} %broadcast_in_dim.37), calls=%async_computation.2 | async-start | bytes 2097152 | tf_op jit(solution)/shard_map/all_to_all | solution.py:22
  77.5 14.9 %all-to-all-done.2 = bf16[4,256,512]{2,1,0:T(8,128)(2,1)S(1)} async-done(((bf16[4,256,512]{2,1,0:T(8,128)(2,1)}), bf16[4,256,512]{2,1,0:T(8,128)(2,1)S(1)}, u32[]{:S(2)}, u32[]{:S(2)}) %all-to-all-start.2) | async-done | bytes 1048608 | tf_op jit(solution)/shard_map/all_to_all | solution.py:22
  92.4 0.0 copy-start.4
  92.4 1.5 %convolution_convert_fusion = bf16[512,512]{1,0:T(8,128)(2,1)} fusion(bf16[1024,512]{1,0:T(8,128)(2,1)S(1)} %bitcast.174, bf16[1024,1024]{1,0:T(8,128)(2,1)S(1)} %bitcast.161, s32[]{:T(128)S(6)} %select_n.109), kind=kOutput, calls=%fused_computation.2 | convolution fusion | flops 537133056 | bytes 2621444 | tf_op jit(solution)/shard_map/dot_general | solution.py:91
  93.9 0.0 copy-done.4
  93.9 2.7 %collective-permute-start.5 = (bf16[512,512]{1,0:T(8,128)(2,1)}, bf16[512,512]{1,0:T(8,128)(2,1)}, u32[]{:S(2)}, u32[]{:S(2)}) collective-permute-start(bf16[512,512]{1,0:T(8,128)(2,1)} %convolution_convert_fusion), channel_id=1, source_target_pairs={{0,1},{1,0},{2,3},{3,2},{4,5},{5,4},{6,7},{7,6},{8,9},{9,8},{10,11... | collective-permute-start | bytes 1572872 | tf_op jit(solution)/shard_map/ppermute | solution.py:98
  96.7 1.6 %copy.21 = f32[1,512,512]{1,2,0:T(8,128)S(1)} copy(f32[1,512,512]{2,1,0:T(8,128)} %param.10) | data formatting | bytes 2097152 | tf_op args[4]
  98.2 2.5 %copy.26 = f32[1,512,512]{1,2,0:T(8,128)} copy(f32[1,512,512]{2,1,0:T(8,128)} %param.11) | data formatting | bytes 2097152 | tf_op args[5]
  100.8 0.0 copy-start
  100.8 2.0 %fusion.4 = f32[512,512]{1,0:T(8,128)S(1)} fusion(bf16[1024,512]{1,0:T(8,128)(2,1)} %bitcast.175, bf16[1024,1024]{1,0:T(8,128)(2,1)S(1)} %bitcast.162, s32[]{:T(128)S(6)} %select_n.108), kind=kOutput, calls=%fused_computation.9 | convolution fusion | flops 536870912 | bytes 3145732 | tf_op jit(solution)/shard_map/dot_general | solution.py:91
  102.8 0.0 copy-start.3
  102.8 0.0 copy-start.1
  102.8 5.6 %collective-permute-done.5 = bf16[512,512]{1,0:T(8,128)(2,1)} collective-permute-done((bf16[512,512]{1,0:T(8,128)(2,1)}, bf16[512,512]{1,0:T(8,128)(2,1)}, u32[]{:S(2)}, u32[]{:S(2)}) %collective-permute-start.5) | collective-permute-done | bytes 524320 | tf_op jit(solution)/shard_map/ppermute | solution.py:98
  108.4 0.0 copy-done
  108.4 1.3 fusion.25
  109.7 0.0 copy-done.3
  109.7 0.0 copy-start.7
  109.8 1.9 %collective-permute-start.6 = (bf16[32,8,512]{2,1,0:T(8,128)(2,1)S(1)}, bf16[32,8,512]{2,1,0:T(8,128)(2,1)S(1)}, u32[]{:S(2)}, u32[]{:S(2)}) collective-permute-start(bf16[32,8,512]{2,1,0:T(8,128)(2,1)S(1)} %fusion.25), channel_id=1, source_target_pairs={{0,8},{8,0},{1,9},{9,1},{2,10},{10,2},{3,11},{11,3},{4,12},{12,4},... | collective-permute-start | bytes 786440 | tf_op jit(solution)/shard_map/ppermute | solution.py:113
  111.7 1.5 %collective-permute-done.6 = bf16[32,8,512]{2,1,0:T(8,128)(2,1)S(1)} collective-permute-done((bf16[32,8,512]{2,1,0:T(8,128)(2,1)S(1)}, bf16[32,8,512]{2,1,0:T(8,128)(2,1)S(1)}, u32[]{:S(2)}, u32[]{:S(2)}) %collective-permute-start.6) | collective-permute-done | bytes 262176 | tf_op jit(solution)/shard_map/ppermute | solution.py:113
  113.2 0.0 copy-done.1
  113.2 1.5 %fusion.23 = bf16[32,8,512]{2,1,0:T(8,128)(2,1)S(1)} fusion(bf16[32,8,512]{2,1,0:T(8,128)(2,1)S(1)} %collective-permute-done.6, f32[32,2,8,512]{3,2,1,0:T(8,128)S(1)} %bitcast.166, s32[]{:T(128)S(6)} %select_n.91, f32[32,2,8,512]{3,2,1,0:T(8,128)} %bitcast.173, f32[32,2,8,512]{3,2,1,0:T(8,128)S(1)} %bitcast.164, bf16[32,2,8,512]{3,2,1,0:T(8,128)(2,1)} %bitcast.24), kind=kLoop, calls=%fused_computation.47 | loop fusion | flops 1966080 | bytes 2359300 | tf_op jit(solution)/shard_map/convert_element_type | solution.py:114
  114.7 19.1 %all_to_all.21 = bf16[32,8,512]{2,1,0:T(8,128)(2,1)S(1)} all-to-all(bf16[32,8,512]{2,1,0:T(8,128)(2,1)S(1)} %fusion.23), channel_id=1, replica_groups=mesh['zh'=4,'y'=8,'c'=2,'x'=4,'zl'=2] {'zh','y'}, dimensions={0} | all-to-all | bytes 524288 | tf_op jit(solution)/shard_map/all_to_all | solution.py:22
  133.9 0.0 copy-done.7
  133.9 0.6 multiply_subtract_fusion
  (3 shorter events, 0.1 us)
Async XLA Ops:
  0.7 1.8 %copy-start.2 = (bf16[1,256,4096]{2,1,0:T(8,128)(2,1)S(1)}, bf16[1,256,4096]{2,1,0:T(8,128)(2,1)}, u32[]{:S(2)}) copy-start(bf16[1,256,4096]{2,1,0:T(8,128)(2,1)} %param.8) | copy-start | bytes 6291460
  2.6 8.1 %copy-start.6 = (f32[512,8]{0,1:T(8,128)S(1)}, f32[512,8]{0,1:T(8,128)}, u32[]{:S(2)}) copy-start(f32[512,8]{0,1:T(8,128)} %param.6) | copy-start | bytes 49156
  3.6 24.6 %collective-permute-start = (bf16[256,1536]{1,0:T(8,128)(2,1)}, bf16[256,1536]{1,0:T(8,128)(2,1)}, u32[]{:S(2)}, u32[]{:S(2)}) collective-permute-start(bf16[256,1536]{1,0:T(8,128)(2,1)} %pad_maximum_fusion), channel_id=1, source_target_pairs={{0,2},{2,4},{4,6},{6,0},{1,3},{3,5},{5,7},{7,1},{8,10},{10,12},{12... | collective-permute-start | bytes 2359304 | tf_op jit(solution)/shard_map/ppermute | solution.py:59
  7.0 25.0 %collective-permute-start.1 = (bf16[256,1536]{1,0:T(8,128)(2,1)S(1)}, bf16[256,1536]{1,0:T(8,128)(2,1)}, u32[]{:S(2)}, u32[]{:S(2)}) collective-permute-start(bf16[256,1536]{1,0:T(8,128)(2,1)S(1)} %pad_maximum_fusion.1), channel_id=1, source_target_pairs={{0,6},{2,0},{4,2},{6,4},{1,7},{3,1},{5,3},{7,5},{8,14},{10,8},{12,... | collective-permute-start | bytes 2359304 | tf_op jit(solution)/shard_map/ppermute | solution.py:60
  11.6 36.5 %all-to-all-start = ((bf16[64,8,512]{2,1,0:T(8,128)(2,1)}), bf16[64,8,512]{2,1,0:T(8,128)(2,1)S(1)}, u32[]{:S(2)}, u32[]{:S(2)}) async-start(bf16[64,8,512]{2,1,0:T(8,128)(2,1)} %broadcast_in_dim.35), calls=%async_computation | async-start | bytes 1048576 | tf_op jit(solution)/shard_map/all_to_all | solution.py:22
  29.9 21.2 %collective-permute-start.2 = (bf16[256,512]{1,0:T(8,128)(2,1)}, bf16[256,512]{1,0:T(8,128)(2,1)}, u32[]{:S(2)}, u32[]{:S(2)}) collective-permute-start(bf16[256,512]{1,0:T(8,128)(2,1)} %slice.36), channel_id=1, source_target_pairs={{0,2},{2,4},{4,6},{6,0},{1,3},{3,5},{5,7},{7,1},{8,10},{10,12},{12... | collective-permute-start | bytes 786440 | tf_op jit(solution)/shard_map/ppermute | solution.py:61
  33.0 19.1 %collective-permute-start.3 = (bf16[256,512]{1,0:T(8,128)(2,1)S(1)}, bf16[256,512]{1,0:T(8,128)(2,1)S(1)}, u32[]{:S(2)}, u32[]{:S(2)}) collective-permute-start(bf16[256,512]{1,0:T(8,128)(2,1)S(1)} %slice.37), channel_id=1, source_target_pairs={{0,6},{2,0},{4,2},{6,4},{1,7},{3,1},{5,3},{7,5},{8,14},{10,8},{12,... | collective-permute-start | bytes 786440 | tf_op jit(solution)/shard_map/ppermute | solution.py:62
  48.1 4.0 %collective-permute-start.4 = (bf16[2,32,8,512]{3,2,1,0:T(8,128)(2,1)S(1)}, bf16[2,32,8,512]{3,2,1,0:T(8,128)(2,1)S(1)}, u32[]{:S(2)}, u32[]{:S(2)}) collective-permute-start(bf16[2,32,8,512]{3,2,1,0:T(8,128)(2,1)S(1)} %bitcast.168), channel_id=1, source_target_pairs={{0,8},{8,0},{1,9},{9,1},{2,10},{10,2},{3,11},{11,3},{4,12},{12,4},... | collective-permute-start | bytes 1572872 | tf_op jit(solution)/shard_map/ppermute | solution.py:43
  53.9 18.9 %copy-start.5 = (bf16[1,256,512]{2,1,0:T(8,128)(2,1)S(1)}, bf16[1,256,512]{2,1,0:T(8,128)(2,1)}, u32[]{:S(2)}) copy-start(bf16[1,256,512]{2,1,0:T(8,128)(2,1)} %param.9) | copy-start | bytes 786436
  73.9 18.4 %all-to-all-start.2 = ((bf16[4,256,512]{2,1,0:T(8,128)(2,1)}), bf16[4,256,512]{2,1,0:T(8,128)(2,1)S(1)}, u32[]{:S(2)}, u32[]{:S(2)}) async-start(bf16[4,256,512]{2,1,0:T(8,128)(2,1)} %broadcast_in_dim.37), calls=%async_computation.2 | async-start | bytes 2097152 | tf_op jit(solution)/shard_map/all_to_all | solution.py:22
  92.4 1.5 %copy-start.4 = (bf16[4,256,512]{2,1,0:T(8,128)(2,1)}, bf16[4,256,512]{2,1,0:T(8,128)(2,1)S(1)}, u32[]{:S(2)}) copy-start(bf16[4,256,512]{2,1,0:T(8,128)(2,1)S(1)} %all-to-all-done.2) | copy-start | bytes 3145732
  93.9 14.5 %collective-permute-start.5 = (bf16[512,512]{1,0:T(8,128)(2,1)}, bf16[512,512]{1,0:T(8,128)(2,1)}, u32[]{:S(2)}, u32[]{:S(2)}) collective-permute-start(bf16[512,512]{1,0:T(8,128)(2,1)} %convolution_convert_fusion), channel_id=1, source_target_pairs={{0,1},{1,0},{2,3},{3,2},{4,5},{5,4},{6,7},{7,6},{8,9},{9,8},{10,11... | collective-permute-start | bytes 1572872 | tf_op jit(solution)/shard_map/ppermute | solution.py:98
  100.8 7.7 %copy-start = (f32[1,512,512]{1,2,0:T(8,128)S(1)}, f32[1,512,512]{1,2,0:T(8,128)}, u32[]{:S(2)}) copy-start(f32[1,512,512]{1,2,0:T(8,128)} %copy.26) | copy-start | bytes 3145732
  102.8 6.9 %copy-start.3 = (f32[512,512]{1,0:T(8,128)}, f32[512,512]{1,0:T(8,128)S(1)}, u32[]{:S(2)}) copy-start(f32[512,512]{1,0:T(8,128)S(1)} %fusion.4) | copy-start | bytes 3145732
  102.8 10.4 %copy-start.1 = (f32[1,512,512]{1,2,0:T(8,128)S(1)}, f32[1,512,512]{1,2,0:T(8,128)}, u32[]{:S(2)}) copy-start(f32[1,512,512]{1,2,0:T(8,128)} %copy.26) | copy-start | bytes 3145732
  109.7 24.1 %copy-start.7 = (f32[512,8]{0,1:T(8,128)S(1)}, f32[512,8]{0,1:T(8,128)}, u32[]{:S(2)}) copy-start(f32[512,8]{0,1:T(8,128)} %param.7) | copy-start | bytes 49156
  109.8 3.4 %collective-permute-start.6 = (bf16[32,8,512]{2,1,0:T(8,128)(2,1)S(1)}, bf16[32,8,512]{2,1,0:T(8,128)(2,1)S(1)}, u32[]{:S(2)}, u32[]{:S(2)}) collective-permute-start(bf16[32,8,512]{2,1,0:T(8,128)(2,1)S(1)} %fusion.25), channel_id=1, source_target_pairs={{0,8},{8,0},{1,9},{9,1},{2,10},{10,2},{3,11},{11,3},{4,12},{12,4},... | collective-permute-start | bytes 786440 | tf_op jit(solution)/shard_map/ppermute | solution.py:113

commit v6 on v5

v6 whole, which is shorter than its diff:
```python
import math

import jax
import jax.numpy as jnp
from jax import lax
from jax.sharding import Mesh, PartitionSpec as P

beta_one = 0.9
beta_two = 0.95
adam_eps = 1e-08
inner_rate = 0.2
decay_rate = 0.1
outer_rate = 0.7
outer_mom = 0.9

REP = ("zh", "y", "c")
FSDP = ("x", "zl")
FAR = ("zh", "y")


def exchange(blocks, axes):
    return lax.all_to_all(blocks, axes, 0, 0)


def spread(block, axes):
    n = lax.axis_size(axes)
    return exchange(jnp.broadcast_to(block[None], (n,) + block.shape), axes)


def local(anchor, momentum, tokens, targets, first_moment, second_moment):
    nx = lax.axis_size("x")
    groups = lax.axis_size(FSDP)
    replicas = lax.axis_size(REP)
    rows, owned = anchor.shape
    count, width = tokens.shape[1:]
    columns = targets.shape[2]
    far = columns // owned // 2
    at_x, at_zl, at_c = lax.axis_index("x"), lax.axis_index("zl"), lax.axis_index("c")
    swap = [(0, 1), (1, 0)]

    def take(a, at, axis):
        start = [0] * a.ndim
        start[axis] = at
        size = [1 if i == axis else n for i, n in enumerate(a.shape)]
        return lax.dynamic_slice(a, start, size, allow_negative_indices=False)

    tok = tokens[0]
    right = [(i, (i + 1) % nx) for i in range(nx)]
    left = [(i, (i - 1) % nx) for i in range(nx)]

    def cut(x, zl):
        at = ((at_x + x) % nx * 2 + (at_zl + zl) % 2) * rows
        return lax.dynamic_slice(tok, (0, at), (count, rows), allow_negative_indices=False)

    def merge(*parts):
        return jnp.concatenate(parts, axis=1)

    from_left = lax.ppermute(merge(cut(1, 0), cut(1, 1), cut(2, 0)), "x", right)
    from_right = lax.ppermute(merge(cut(3, 0), cut(3, 1), cut(2, 1)), "x", left)
    far_left = lax.ppermute(from_left[:, 2 * rows :], "x", right)
    far_right = lax.ppermute(from_right[:, 2 * rows :], "x", left)

    held = jnp.zeros((nx, count, 2 * rows), tok.dtype)
    for d, first, block in (
        (0, 0, merge(cut(0, 0), cut(0, 1))),
        (3, 0, from_left[:, : 2 * rows]),
        (1, 0, from_right[:, : 2 * rows]),
        (2, 0, far_left),
        (2, rows, far_right),
    ):
        at = ((at_x + d) % nx, 0, first)
        held = lax.dynamic_update_slice(held, block[None], at, allow_negative_indices=False)
    held = held.reshape(nx * count, 2 * rows)

    own = anchor.astype(jnp.bfloat16).T
    half = spread(own, ("zl",) + FAR).reshape(2, far, owned, rows)
    swapped = lax.ppermute(half, "c", swap)

    first = jnp.where(at_c == 0, half, swapped)
    start = jnp.stack([first, jnp.where(at_c == 0, swapped, half)], 2)
    start = start.reshape(2, columns, rows)

    def project(first, at):
        return lax.dot_general(
            held[:, first : first + rows], take(start, at, 0)[0], (((1,), (1,)), ((), ())),
            preferred_element_type=jnp.float32,
        )

    partial = project(0, at_zl) + project(rows, 1 - at_zl)
    partial = partial.astype(jnp.bfloat16).reshape(nx, count, columns)
    parts = exchange(partial, "x").astype(jnp.float32)
    projected = jnp.sum(parts, axis=0) * width ** (-0.5)
    residual = (projected - targets[0].astype(jnp.float32)).astype(jnp.bfloat16)
    residual = spread(residual, "x").reshape(nx * count, columns)

    def term(first):
        return lax.dot_general(
            residual, held[:, first : first + rows], (((0,), (0,)), ((), ())),
            preferred_element_type=jnp.float32,
        )

    other = lax.ppermute(term(rows).astype(jnp.bfloat16), "zl", swap)
    kept = lax.optimization_barrier(term(0))

    def direct(at):
        def of(a):
            return take(a.reshape(far, 2, owned, rows), at, 1)[:, 0]

        summed = of(kept) + of(other).astype(jnp.float32)
        gradient = summed * (1.0 / (math.sqrt(width) * groups * count))
        moment_one = beta_one * of(first_moment[0].T) + (1.0 - beta_one) * gradient
        squared = (1.0 - beta_two) * gradient * gradient
        moment_two = beta_two * of(second_moment[0].T) + squared
        return moment_one / (jnp.sqrt(moment_two) + adam_eps)

    given = lax.ppermute(direct(1 - at_c).astype(jnp.bfloat16), "c", swap)
    kept = lax.optimization_barrier(direct(at_c))
    sent = (kept + given.astype(jnp.float32)).astype(jnp.bfloat16)
    total = jnp.sum(exchange(sent, FAR).astype(jnp.float32), axis=0).T

    begin = anchor.astype(jnp.bfloat16).astype(jnp.float32)
    mean_delta = inner_rate * (total / replicas + decay_rate * begin)
    momentum_next = outer_mom * momentum + mean_delta
    anchor_next = anchor - outer_rate * (mean_delta + outer_mom * momentum_next)
    return (anchor_next, momentum_next)


def solution(mesh):
    fine = Mesh(mesh.devices.reshape(4, 8, 2, 4, 2), REP + FSDP)
    outer = P(FSDP, REP)
    inner = P(REP, FSDP, None)
    return jax.shard_map(
        local,
        mesh=fine,
        in_specs=(outer, outer, inner, inner, inner, inner),
        out_specs=(outer, outer),
        check_vma=False,
    )
```

time: 135 us -> 133 us (0.985)
  blocking collectives: 37.9 us -> 56.4 us
  waiting for transfers between devices: 31.1 us -> 14.9 us
  starting transfers between devices: 40.7 us -> 36.7 us
    all_to_all x2 -> x3, blocking collectives: 37.9 us -> 56.4 us  [exchange(): return lax.all_to_all(blocks, axes, 0, 0)]
    all_to_all x2 -> x1, waiting for transfers between devices: 24 us -> 6.4 us  [exchange(): return lax.all_to_all(blocks, axes, 0, 0)]
    all_to_all x2 -> x1, starting transfers between devices: 20.1 us -> 16.6 us  [exchange(): return lax.all_to_all(blocks, axes, 0, 0)]
    ppermute x4, waiting for transfers between devices: 5.59 us -> 8.3 us  [the longest x1 4.9 us: local(): other = lax.ppermute(term(rows).astype(jnp.bfloat16), 'zl', swap)]
    convert_element_type x1, other arithmetic: 1.5 us -> 0.07 us  [local(): sent = (kept + given.astype(jnp.float32)).astype(jnp.bfloat16)]
    unnamed x18 -> x12, local copies, waits for them, and re-layouts: 4.4 us -> 5.14 us
  transfers between devices with their start and end apart: 9 -> 8, of which waited for: 4 -> 5; matrix products, arithmetic and copies ran while one was open for 10% -> 11% of each run, Pallas kernels for 0% -> 0%
where the time goes in v6:
time: 133 us
  blocking collectives  56.4 us (42%)
  starting transfers between devices  36.7 us (28%)
  waiting for transfers between devices  14.9 us (11%)
  local copies, waits for them, and re-layouts  12.8 us (10%)
  other arithmetic  5.72 us (4%)
  matrix products  5.1 us (4%)
    all_to_all x3, blocking collectives, exchange(): return lax.all_to_all(blocks, axes, 0, 0)  56.4 us
    all_to_all x1, starting transfers between devices, exchange(): return lax.all_to_all(blocks, axes, 0, 0)  16.6 us
    all_to_all x1, waiting for transfers between devices, exchange(): return lax.all_to_all(blocks, axes, 0, 0)  6.4 us
    unnamed x12, local copies, waits for them, and re-layouts  5.14 us
    ppermute x1, starting transfers between devices, local(): far_right = lax.ppermute(from_right[:, 2 * rows:], 'x', left)  5.12 us
    ppermute x1, waiting for transfers between devices, local(): other = lax.ppermute(term(rows).astype(jnp.bfloat16), 'zl', swap)  4.9 us
    ppermute x1, starting transfers between devices, local(): from_right = lax.ppermute(merge(cut(3, 0), cut(3, 1), cut(2, 1)), 'x', left)  4.66 us
    dot_general x2, matrix products, term(): lax.dot_general(residual, held[:, first:first + rows], (((0,), (0,)), (()...  3.57 us
  transfers between devices with their start and end apart: 8, of which 5 were waited for; matrix products, arithmetic and copies ran while one was open for 11% of the time, Pallas kernels for 0%

profile of v6, /device:TPU:8, one launch (start us, length us, event | category | flops | bytes accessed | tf_op | source)
XLA Modules:
  0.0 132.6 jit_solution(6962527299541016577)
XLA Ops:
  0.7 1.7 %dynamic-slice_bitcast_fusion.2 = (bf16[256,512]{1,0:T(8,128)(2,1)S(1)}, bf16[256,512]{1,0:T(8,128)(2,1)S(1)}, bf16[256,512]{1,0:T(8,128)(2,1)S(1)}, bf16[256,51...) fusion(bf16[1,256,4096]{2,1,0:T(8,128)(2,1)} %param.8, ...), kind=kLoop, calls=%fused_computation.52 | loop fusion | bytes 4194336 | tf_op jit(solution)/shard_map/dynamic_slice | solution.py:53
  2.4 0.0 copy-start.3
  2.4 1.0 pad_maximum_fusion.2
  3.4 4.7 %collective-permute-start.1 = (bf16[256,1536]{1,0:T(8,128)(2,1)}, bf16[256,1536]{1,0:T(8,128)(2,1)}, u32[]{:S(2)}, u32[]{:S(2)}) collective-permute-start(bf16[256,1536]{1,0:T(8,128)(2,1)} %pad_maximum_fusion.2), channel_id=1, source_target_pairs={{0,6},{2,0},{4,2},{6,4},{1,7},{3,1},{5,3},{7,5},{8,14},{10,8},{12,... | collective-permute-start | bytes 2359304 | tf_op jit(solution)/shard_map/ppermute | solution.py:59
  8.0 0.9 pad_maximum_fusion.1
  9.0 1.9 %collective-permute-start = (bf16[256,1536]{1,0:T(8,128)(2,1)}, bf16[256,1536]{1,0:T(8,128)(2,1)}, u32[]{:S(2)}, u32[]{:S(2)}) collective-permute-start(bf16[256,1536]{1,0:T(8,128)(2,1)} %pad_maximum_fusion.1), channel_id=1, source_target_pairs={{0,2},{2,4},{4,6},{6,0},{1,3},{3,5},{5,7},{7,1},{8,10},{10,12},{12... | collective-permute-start | bytes 2359304 | tf_op jit(solution)/shard_map/ppermute | solution.py:58
  10.9 0.0 copy-done.3
  10.9 0.8 broadcast_in_dim.38
  11.7 16.6 %all-to-all-start = ((bf16[64,8,512]{2,1,0:T(8,128)(2,1)}), bf16[64,8,512]{2,1,0:T(8,128)(2,1)S(1)}, u32[]{:S(2)}, u32[]{:S(2)}) async-start(bf16[64,8,512]{2,1,0:T(8,128)(2,1)} %broadcast_in_dim.38), calls=%async_computation | async-start | bytes 1048576 | tf_op jit(solution)/shard_map/all_to_all | solution.py:22
  28.3 0.3 broadcast_in_dim.32
  28.6 0.1 fusion.8
  28.7 2.7 %collective-permute-done = bf16[256,1536]{1,0:T(8,128)(2,1)} collective-permute-done((bf16[256,1536]{1,0:T(8,128)(2,1)}, bf16[256,1536]{1,0:T(8,128)(2,1)}, u32[]{:S(2)}, u32[]{:S(2)}) %collective-permute-start) | collective-permute-done | bytes 786464 | tf_op jit(solution)/shard_map/ppermute | solution.py:58
  31.4 1.0 slice.28
  32.3 1.9 %collective-permute-start.2 = (bf16[256,512]{1,0:T(8,128)(2,1)S(1)}, bf16[256,512]{1,0:T(8,128)(2,1)S(1)}, u32[]{:S(2)}, u32[]{:S(2)}) collective-permute-start(bf16[256,512]{1,0:T(8,128)(2,1)S(1)} %slice.28), channel_id=1, source_target_pairs={{0,2},{2,4},{4,6},{6,0},{1,3},{3,5},{5,7},{7,1},{8,10},{10,12},{12... | collective-permute-start | bytes 786440 | tf_op jit(solution)/shard_map/ppermute | solution.py:60
  34.3 0.0 collective-permute-done.1
  34.3 1.7 %slice.29 = bf16[256,512]{1,0:T(8,128)(2,1)} slice(bf16[256,1536]{1,0:T(8,128)(2,1)} %collective-permute-done.1), slice={[0:256], [1024:1536]} | slice | bytes 524288 | tf_op jit(solution)/shard_map/slice | solution.py:61
  35.9 5.1 %collective-permute-start.3 = (bf16[256,512]{1,0:T(8,128)(2,1)}, bf16[256,512]{1,0:T(8,128)(2,1)S(1)}, u32[]{:S(2)}, u32[]{:S(2)}) collective-permute-start(bf16[256,512]{1,0:T(8,128)(2,1)} %slice.29), channel_id=1, source_target_pairs={{0,6},{2,0},{4,2},{6,4},{1,7},{3,1},{5,3},{7,5},{8,14},{10,8},{12,... | collective-permute-start | bytes 786440 | tf_op jit(solution)/shard_map/ppermute | solution.py:61
  41.1 1.1 fusion.7
  42.2 6.4 %all-to-all-done = bf16[64,8,512]{2,1,0:T(8,128)(2,1)S(1)} async-done(((bf16[64,8,512]{2,1,0:T(8,128)(2,1)}), bf16[64,8,512]{2,1,0:T(8,128)(2,1)S(1)}, u32[]{:S(2)}, u32[]{:S(2)}) %all-to-all-start) | async-done | bytes 524320 | tf_op jit(solution)/shard_map/all_to_all | solution.py:22
  48.6 1.9 %collective-permute-start.4 = (bf16[2,32,8,512]{3,2,1,0:T(8,128)(2,1)S(1)}, bf16[2,32,8,512]{3,2,1,0:T(8,128)(2,1)S(1)}, u32[]{:S(2)}, u32[]{:S(2)}) collective-permute-start(bf16[2,32,8,512]{3,2,1,0:T(8,128)(2,1)S(1)} %bitcast.173), channel_id=1, source_target_pairs={{0,8},{8,0},{1,9},{9,1},{2,10},{10,2},{3,11},{11,3},{4,12},{12,4},... | collective-permute-start | bytes 1572872 | tf_op jit(solution)/shard_map/ppermute | solution.py:77
  50.5 1.1 fusion.6
  51.6 0.0 collective-permute-done.2
  51.6 0.0 collective-permute-done.3
  51.7 0.7 collective-permute-done.4
  52.4 0.1 select_bitcast_fusion.1
  52.4 0.1 pad_maximum_fusion
  52.5 0.8 fusion.1
  53.3 0.8 add_convert_fusion
  54.1 0.0 copy-start.2
  54.1 19.5 %all_to_all.20 = bf16[4,256,512]{2,1,0:T(8,128)(2,1)S(1)} all-to-all(bf16[4,256,512]{2,1,0:T(8,128)(2,1)S(1)} %bitcast.170), channel_id=1, replica_groups=mesh['zh'=4,'y'=8,'c'=2,'x'=4,'zl'=2] {'x'}, dimensions={0} | all-to-all | bytes 2097152 | tf_op jit(solution)/shard_map/all_to_all | solution.py:22
  73.6 0.1 convert_reduce_fusion
  73.8 0.0 copy-done.2
  73.8 0.1 fusion.26
  73.9 0.1 broadcast_in_dim.40
  73.9 16.7 %all_to_all.21 = bf16[4,256,512]{2,1,0:T(8,128)(2,1)S(1)} all-to-all(bf16[4,256,512]{2,1,0:T(8,128)(2,1)S(1)} %broadcast_in_dim.40), channel_id=1, replica_groups=mesh['zh'=4,'y'=8,'c'=2,'x'=4,'zl'=2] {'x'}, dimensions={0} | all-to-all | bytes 2097152 | tf_op jit(solution)/shard_map/all_to_all | solution.py:22
  90.6 0.0 copy-start.1
  90.6 1.0 copy-done.1
  91.6 1.5 %convolution_convert_fusion = bf16[512,512]{1,0:T(8,128)(2,1)} fusion(bf16[1024,512]{1,0:T(8,128)(2,1)S(1)} %bitcast.177, bf16[1024,1024]{1,0:T(8,128)(2,1)S(1)} %bitcast.164), kind=kOutput, calls=%fused_computation.2 | convolution fusion | flops 537133056 | bytes 2621440 | tf_op jit(solution)/shard_map/dot_general | solution.py:97
  93.1 2.7 %collective-permute-start.5 = (bf16[512,512]{1,0:T(8,128)(2,1)}, bf16[512,512]{1,0:T(8,128)(2,1)}, u32[]{:S(2)}, u32[]{:S(2)}) collective-permute-start(bf16[512,512]{1,0:T(8,128)(2,1)} %convolution_convert_fusion), channel_id=1, source_target_pairs={{0,1},{1,0},{2,3},{3,2},{4,5},{5,4},{6,7},{7,6},{8,9},{9,8},{10,11... | collective-permute-start | bytes 1572872 | tf_op jit(solution)/shard_map/ppermute | solution.py:102
  95.8 1.6 %copy.21 = f32[1,512,512]{1,2,0:T(8,128)S(1)} copy(f32[1,512,512]{2,1,0:T(8,128)} %param.10) | data formatting | bytes 2097152 | tf_op args[4]
  97.4 2.6 %copy.26 = f32[1,512,512]{1,2,0:T(8,128)} copy(f32[1,512,512]{2,1,0:T(8,128)} %param.11) | data formatting | bytes 2097152 | tf_op args[5]
  100.0 0.0 copy-start
  100.0 2.0 %fusion.3 = f32[512,512]{1,0:T(8,128)S(1)} fusion(bf16[1024,512]{1,0:T(8,128)(2,1)} %bitcast.178, bf16[1024,1024]{1,0:T(8,128)(2,1)S(1)} %bitcast.165), kind=kOutput, calls=%fused_computation.7 | convolution fusion | flops 536870912 | bytes 3145728 | tf_op jit(solution)/shard_map/dot_general | solution.py:97
  102.0 4.9 %collective-permute-done.5 = bf16[512,512]{1,0:T(8,128)(2,1)} collective-permute-done((bf16[512,512]{1,0:T(8,128)(2,1)}, bf16[512,512]{1,0:T(8,128)(2,1)}, u32[]{:S(2)}, u32[]{:S(2)}) %collective-permute-start.5) | collective-permute-done | bytes 524320 | tf_op jit(solution)/shard_map/ppermute | solution.py:102
  106.9 0.0 copy-done
  106.9 1.3 fusion.27
  108.2 0.0 copy-start.4
  108.2 1.9 %collective-permute-start.6 = (bf16[32,8,512]{2,1,0:T(8,128)(2,1)S(1)}, bf16[32,8,512]{2,1,0:T(8,128)(2,1)S(1)}, u32[]{:S(2)}, u32[]{:S(2)}) collective-permute-start(bf16[32,8,512]{2,1,0:T(8,128)(2,1)S(1)} %fusion.27), channel_id=1, source_target_pairs={{0,8},{8,0},{1,9},{9,1},{2,10},{10,2},{3,11},{11,3},{4,12},{12,4},... | collective-permute-start | bytes 786440 | tf_op jit(solution)/shard_map/ppermute | solution.py:116
  110.2 1.3 fusion.18
  111.5 0.2 collective-permute-done.6
  111.7 0.1 add_convert_fusion.1
  111.7 20.2 %all_to_all.22 = bf16[32,8,512]{2,1,0:T(8,128)(2,1)S(1)} all-to-all(bf16[32,8,512]{2,1,0:T(8,128)(2,1)S(1)} %add_convert_fusion.1), channel_id=1, replica_groups=mesh['zh'=4,'y'=8,'c'=2,'x'=4,'zl'=2] {'zh','y'}, dimensions={0} | all-to-all | bytes 524288 | tf_op jit(solution)/shard_map/all_to_all | solution.py:22
  132.0 0.0 copy-done.4
  132.0 0.6 multiply_subtract_fusion
  (4 shorter events, 0.1 us)
Async XLA Ops:
  2.4 8.5 %copy-start.3 = (f32[512,8]{0,1:T(8,128)S(1)}, f32[512,8]{0,1:T(8,128)}, u32[]{:S(2)}) copy-start(f32[512,8]{0,1:T(8,128)} %param.6) | copy-start | bytes 49156
  3.4 30.9 %collective-permute-start.1 = (bf16[256,1536]{1,0:T(8,128)(2,1)}, bf16[256,1536]{1,0:T(8,128)(2,1)}, u32[]{:S(2)}, u32[]{:S(2)}) collective-permute-start(bf16[256,1536]{1,0:T(8,128)(2,1)} %pad_maximum_fusion.2), channel_id=1, source_target_pairs={{0,6},{2,0},{4,2},{6,4},{1,7},{3,1},{5,3},{7,5},{8,14},{10,8},{12,... | collective-permute-start | bytes 2359304 | tf_op jit(solution)/shard_map/ppermute | solution.py:59
  9.0 22.4 %collective-permute-start = (bf16[256,1536]{1,0:T(8,128)(2,1)}, bf16[256,1536]{1,0:T(8,128)(2,1)}, u32[]{:S(2)}, u32[]{:S(2)}) collective-permute-start(bf16[256,1536]{1,0:T(8,128)(2,1)} %pad_maximum_fusion.1), channel_id=1, source_target_pairs={{0,2},{2,4},{4,6},{6,0},{1,3},{3,5},{5,7},{7,1},{8,10},{10,12},{12... | collective-permute-start | bytes 2359304 | tf_op jit(solution)/shard_map/ppermute | solution.py:58
  11.7 36.8 %all-to-all-start = ((bf16[64,8,512]{2,1,0:T(8,128)(2,1)}), bf16[64,8,512]{2,1,0:T(8,128)(2,1)S(1)}, u32[]{:S(2)}, u32[]{:S(2)}) async-start(bf16[64,8,512]{2,1,0:T(8,128)(2,1)} %broadcast_in_dim.38), calls=%async_computation | async-start | bytes 1048576 | tf_op jit(solution)/shard_map/all_to_all | solution.py:22
  32.3 19.2 %collective-permute-start.2 = (bf16[256,512]{1,0:T(8,128)(2,1)S(1)}, bf16[256,512]{1,0:T(8,128)(2,1)S(1)}, u32[]{:S(2)}, u32[]{:S(2)}) collective-permute-start(bf16[256,512]{1,0:T(8,128)(2,1)S(1)} %slice.28), channel_id=1, source_target_pairs={{0,2},{2,4},{4,6},{6,0},{1,3},{3,5},{5,7},{7,1},{8,10},{10,12},{12... | collective-permute-start | bytes 786440 | tf_op jit(solution)/shard_map/ppermute | solution.py:60
  35.9 15.7 %collective-permute-start.3 = (bf16[256,512]{1,0:T(8,128)(2,1)}, bf16[256,512]{1,0:T(8,128)(2,1)S(1)}, u32[]{:S(2)}, u32[]{:S(2)}) collective-permute-start(bf16[256,512]{1,0:T(8,128)(2,1)} %slice.29), channel_id=1, source_target_pairs={{0,6},{2,0},{4,2},{6,4},{1,7},{3,1},{5,3},{7,5},{8,14},{10,8},{12,... | collective-permute-start | bytes 786440 | tf_op jit(solution)/shard_map/ppermute | solution.py:61
  48.6 3.8 %collective-permute-start.4 = (bf16[2,32,8,512]{3,2,1,0:T(8,128)(2,1)S(1)}, bf16[2,32,8,512]{3,2,1,0:T(8,128)(2,1)S(1)}, u32[]{:S(2)}, u32[]{:S(2)}) collective-permute-start(bf16[2,32,8,512]{3,2,1,0:T(8,128)(2,1)S(1)} %bitcast.173), channel_id=1, source_target_pairs={{0,8},{8,0},{1,9},{9,1},{2,10},{10,2},{3,11},{11,3},{4,12},{12,4},... | collective-permute-start | bytes 1572872 | tf_op jit(solution)/shard_map/ppermute | solution.py:77
  54.1 19.7 %copy-start.2 = (bf16[1,256,512]{2,1,0:T(8,128)(2,1)S(1)}, bf16[1,256,512]{2,1,0:T(8,128)(2,1)}, u32[]{:S(2)}) copy-start(bf16[1,256,512]{2,1,0:T(8,128)(2,1)} %param.9) | copy-start | bytes 786436
  90.6 1.0 copy-start.1
  93.1 13.8 %collective-permute-start.5 = (bf16[512,512]{1,0:T(8,128)(2,1)}, bf16[512,512]{1,0:T(8,128)(2,1)}, u32[]{:S(2)}, u32[]{:S(2)}) collective-permute-start(bf16[512,512]{1,0:T(8,128)(2,1)} %convolution_convert_fusion), channel_id=1, source_target_pairs={{0,1},{1,0},{2,3},{3,2},{4,5},{5,4},{6,7},{7,6},{8,9},{9,8},{10,11... | collective-permute-start | bytes 1572872 | tf_op jit(solution)/shard_map/ppermute | solution.py:102
  100.0 6.9 %copy-start = (f32[1,512,512]{1,2,0:T(8,128)S(1)}, f32[1,512,512]{1,2,0:T(8,128)}, u32[]{:S(2)}) copy-start(f32[1,512,512]{1,2,0:T(8,128)} %copy.26) | copy-start | bytes 3145732
  108.2 23.7 %copy-start.4 = (f32[512,8]{0,1:T(8,128)S(1)}, f32[512,8]{0,1:T(8,128)}, u32[]{:S(2)}) copy-start(f32[512,8]{0,1:T(8,128)} %param.7) | copy-start | bytes 49156
  108.2 3.4 %collective-permute-start.6 = (bf16[32,8,512]{2,1,0:T(8,128)(2,1)S(1)}, bf16[32,8,512]{2,1,0:T(8,128)(2,1)S(1)}, u32[]{:S(2)}, u32[]{:S(2)}) collective-permute-start(bf16[32,8,512]{2,1,0:T(8,128)(2,1)S(1)} %fusion.27), channel_id=1, source_target_pairs={{0,8},{8,0},{1,9},{9,1},{2,10},{10,2},{3,11},{11,3},{4,12},{12,4},... | collective-permute-start | bytes 786440 | tf_op jit(solution)/shard_map/ppermute | solution.py:116

commit v7 on v6

--- a/solution.py
+++ b/solution.py
@@ -99,22 +99,28 @@
             preferred_element_type=jnp.float32,
         )
 
-    other = lax.ppermute(term(rows).astype(jnp.bfloat16), "zl", swap)
+    def of(a, at):
+        return take(a.reshape(far, 2, owned, rows), at, 1)[:, 0]
+
+    lent = lax.optimization_barrier(term(rows))
+    others = [
+        lax.ppermute(of(lent, at).astype(jnp.bfloat16), "zl", swap)
+        for at in (1 - at_c, at_c)
+    ]
     kept = lax.optimization_barrier(term(0))
 
-    def direct(at):
-        def of(a):
-            return take(a.reshape(far, 2, owned, rows), at, 1)[:, 0]
-
-        summed = of(kept) + of(other).astype(jnp.float32)
+    def direct(at, other):
+        summed = of(kept, at) + other.astype(jnp.float32)
         gradient = summed * (1.0 / (math.sqrt(width) * groups * count))
-        moment_one = beta_one * of(first_moment[0].T) + (1.0 - beta_one) * gradient
+        moment_one = beta_one * of(first_moment[0].T, at) + (1.0 - beta_one) * gradient
         squared = (1.0 - beta_two) * gradient * gradient
-        moment_two = beta_two * of(second_moment[0].T) + squared
+        moment_two = beta_two * of(second_moment[0].T, at) + squared
         return moment_one / (jnp.sqrt(moment_two) + adam_eps)
 
-    given = lax.ppermute(direct(1 - at_c).astype(jnp.bfloat16), "c", swap)
-    kept = lax.optimization_barrier(direct(at_c))
+    given = direct(1 - at_c, others[0]).astype(jnp.bfloat16)
+    later, _ = lax.optimization_barrier((others[1], given))
+    given = lax.ppermute(given, "c", swap)
+    kept = lax.optimization_barrier(direct(at_c, later))
     sent = (kept + given.astype(jnp.float32)).astype(jnp.bfloat16)
     total = jnp.sum(exchange(sent, FAR).astype(jnp.float32), axis=0).T
 

time: 133 us -> 132 us (level)
  blocking collectives: 56.4 us -> 40 us
  waiting for transfers between devices: 14.9 us -> 23.8 us
  starting transfers between devices: 36.7 us -> 44.2 us
  other arithmetic: 5.72 us -> 3.8 us
    all_to_all x3 -> x2, blocking collectives: 56.4 us -> 40 us  [exchange(): return lax.all_to_all(blocks, axes, 0, 0)]
    all_to_all x1 -> x2, waiting for transfers between devices: 6.4 us -> 16.6 us  [exchange(): return lax.all_to_all(blocks, axes, 0, 0)]
    all_to_all x1 -> x2, starting transfers between devices: 16.6 us -> 20.8 us  [exchange(): return lax.all_to_all(blocks, axes, 0, 0)]
    ppermute x2 -> x3, starting transfers between devices: 4.62 us -> 7.89 us  [the longest x2 5.97 us: local(): lax.ppermute(of(lent, at).astype(jnp.bfloat16), 'zl', swap)]
    ppermute x2 -> x3, waiting for transfers between devices: 5.09 us -> 3.88 us  [the longest x2 3.24 us: local(): lax.ppermute(of(lent, at).astype(jnp.bfloat16), 'zl', swap)]
    unnamed x12 -> x10, local copies, waits for them, and re-layouts: 5.14 us -> 4.14 us
  transfers between devices with their start and end apart: 8 -> 10, of which waited for: 5 -> 7; matrix products, arithmetic and copies ran while one was open for 11% -> 10% of each run, Pallas kernels for 0% -> 0%
where the time goes in v7:
time: 132 us; the launch traced here: 131 us
  starting transfers between devices  44.2 us (33%)
  blocking collectives  40 us (30%)
  waiting for transfers between devices  23.8 us (18%)
  local copies, waits for them, and re-layouts  12.9 us (10%)
  matrix products  5.43 us (4%)
  other arithmetic  3.8 us (3%)
    all_to_all x2, blocking collectives, exchange(): return lax.all_to_all(blocks, axes, 0, 0)  40 us
    all_to_all x2, starting transfers between devices, exchange(): return lax.all_to_all(blocks, axes, 0, 0)  20.8 us
    all_to_all x2, waiting for transfers between devices, exchange(): return lax.all_to_all(blocks, axes, 0, 0)  16.6 us
    ppermute x2, starting transfers between devices, local(): lax.ppermute(of(lent, at).astype(jnp.bfloat16), 'zl', swap)  5.97 us
    ppermute x1, starting transfers between devices, local(): far_right = lax.ppermute(from_right[:, 2 * rows:], 'x', left)  5.12 us
    ppermute x1, starting transfers between devices, local(): from_right = lax.ppermute(merge(cut(3, 0), cut(3, 1), cut(2, 1)), 'x', left)  4.66 us
    unnamed x10, local copies, waits for them, and re-layouts  4.14 us
    dot_general x2, matrix products, term(): lax.dot_general(residual, held[:, first:first + rows], (((0,), (0,)), (()...  3.9 us
  transfers between devices with their start and end apart: 10, of which 7 were waited for; matrix products, arithmetic and copies ran while one was open for 10% of the time, Pallas kernels for 0%

profile of v7, /device:TPU:8, one launch (start us, length us, event | category | flops | bytes accessed | tf_op | source)
XLA Modules:
  0.0 131.2 jit_solution(5327775586821524129)
XLA Ops:
  0.7 1.7 %dynamic-slice_bitcast_fusion.2 = (bf16[256,512]{1,0:T(8,128)(2,1)S(1)}, bf16[256,512]{1,0:T(8,128)(2,1)S(1)}, bf16[256,512]{1,0:T(8,128)(2,1)S(1)}, bf16[256,51...) fusion(bf16[1,256,4096]{2,1,0:T(8,128)(2,1)} %param.8, ...), kind=kLoop, calls=%fused_computation.57 | loop fusion | bytes 4194336 | tf_op jit(solution)/shard_map/dynamic_slice | solution.py:53
  2.4 0.0 copy-start.2
  2.4 1.0 pad_maximum_fusion.2
  3.4 4.7 %collective-permute-start.1 = (bf16[256,1536]{1,0:T(8,128)(2,1)}, bf16[256,1536]{1,0:T(8,128)(2,1)}, u32[]{:S(2)}, u32[]{:S(2)}) collective-permute-start(bf16[256,1536]{1,0:T(8,128)(2,1)} %pad_maximum_fusion.2), channel_id=1, source_target_pairs={{0,6},{2,0},{4,2},{6,4},{1,7},{3,1},{5,3},{7,5},{8,14},{10,8},{12,... | collective-permute-start | bytes 2359304 | tf_op jit(solution)/shard_map/ppermute | solution.py:59
  8.0 0.9 pad_maximum_fusion.1
  9.0 1.9 %collective-permute-start = (bf16[256,1536]{1,0:T(8,128)(2,1)}, bf16[256,1536]{1,0:T(8,128)(2,1)}, u32[]{:S(2)}, u32[]{:S(2)}) collective-permute-start(bf16[256,1536]{1,0:T(8,128)(2,1)} %pad_maximum_fusion.1), channel_id=1, source_target_pairs={{0,2},{2,4},{4,6},{6,0},{1,3},{3,5},{5,7},{7,1},{8,10},{10,12},{12... | collective-permute-start | bytes 2359304 | tf_op jit(solution)/shard_map/ppermute | solution.py:58
  10.9 0.0 copy-done.2
  10.9 0.8 broadcast_in_dim.38
  11.7 16.6 %all-to-all-start = ((bf16[64,8,512]{2,1,0:T(8,128)(2,1)}), bf16[64,8,512]{2,1,0:T(8,128)(2,1)S(1)}, u32[]{:S(2)}, u32[]{:S(2)}) async-start(bf16[64,8,512]{2,1,0:T(8,128)(2,1)} %broadcast_in_dim.38), calls=%async_computation | async-start | bytes 1048576 | tf_op jit(solution)/shard_map/all_to_all | solution.py:22
  28.3 0.3 broadcast_in_dim.32
  28.6 0.1 fusion.9
  28.7 2.7 %collective-permute-done = bf16[256,1536]{1,0:T(8,128)(2,1)} collective-permute-done((bf16[256,1536]{1,0:T(8,128)(2,1)}, bf16[256,1536]{1,0:T(8,128)(2,1)}, u32[]{:S(2)}, u32[]{:S(2)}) %collective-permute-start) | collective-permute-done | bytes 786464 | tf_op jit(solution)/shard_map/ppermute | solution.py:58
  31.4 1.0 slice.28
  32.3 1.9 %collective-permute-start.2 = (bf16[256,512]{1,0:T(8,128)(2,1)S(1)}, bf16[256,512]{1,0:T(8,128)(2,1)S(1)}, u32[]{:S(2)}, u32[]{:S(2)}) collective-permute-start(bf16[256,512]{1,0:T(8,128)(2,1)S(1)} %slice.28), channel_id=1, source_target_pairs={{0,2},{2,4},{4,6},{6,0},{1,3},{3,5},{5,7},{7,1},{8,10},{10,12},{12... | collective-permute-start | bytes 786440 | tf_op jit(solution)/shard_map/ppermute | solution.py:60
  34.3 0.0 collective-permute-done.1
  34.3 1.7 %slice.29 = bf16[256,512]{1,0:T(8,128)(2,1)} slice(bf16[256,1536]{1,0:T(8,128)(2,1)} %collective-permute-done.1), slice={[0:256], [1024:1536]} | slice | bytes 524288 | tf_op jit(solution)/shard_map/slice | solution.py:61
  36.0 5.1 %collective-permute-start.3 = (bf16[256,512]{1,0:T(8,128)(2,1)}, bf16[256,512]{1,0:T(8,128)(2,1)S(1)}, u32[]{:S(2)}, u32[]{:S(2)}) collective-permute-start(bf16[256,512]{1,0:T(8,128)(2,1)} %slice.29), channel_id=1, source_target_pairs={{0,6},{2,0},{4,2},{6,4},{1,7},{3,1},{5,3},{7,5},{8,14},{10,8},{12,... | collective-permute-start | bytes 786440 | tf_op jit(solution)/shard_map/ppermute | solution.py:61
  41.1 1.1 fusion.8
  42.2 6.4 %all-to-all-done = bf16[64,8,512]{2,1,0:T(8,128)(2,1)S(1)} async-done(((bf16[64,8,512]{2,1,0:T(8,128)(2,1)}), bf16[64,8,512]{2,1,0:T(8,128)(2,1)S(1)}, u32[]{:S(2)}, u32[]{:S(2)}) %all-to-all-start) | async-done | bytes 524320 | tf_op jit(solution)/shard_map/all_to_all | solution.py:22
  48.6 1.9 %collective-permute-start.4 = (bf16[2,32,8,512]{3,2,1,0:T(8,128)(2,1)S(1)}, bf16[2,32,8,512]{3,2,1,0:T(8,128)(2,1)S(1)}, u32[]{:S(2)}, u32[]{:S(2)}) collective-permute-start(bf16[2,32,8,512]{3,2,1,0:T(8,128)(2,1)S(1)} %bitcast.189), channel_id=1, source_target_pairs={{0,8},{8,0},{1,9},{9,1},{2,10},{10,2},{3,11},{11,3},{4,12},{12,4},... | collective-permute-start | bytes 1572872 | tf_op jit(solution)/shard_map/ppermute | solution.py:77
  50.5 1.1 fusion.7
  51.6 0.0 collective-permute-done.2
  51.6 0.0 collective-permute-done.3
  51.7 0.7 collective-permute-done.4
  52.4 0.1 select_bitcast_fusion.1
  52.4 0.1 pad_maximum_fusion
  52.5 0.8 fusion.2
  53.3 0.8 add_convert_fusion
  54.1 0.0 copy-start.1
  54.1 19.5 %all_to_all.20 = bf16[4,256,512]{2,1,0:T(8,128)(2,1)S(1)} all-to-all(bf16[4,256,512]{2,1,0:T(8,128)(2,1)S(1)} %bitcast.186), channel_id=1, replica_groups=mesh['zh'=4,'y'=8,'c'=2,'x'=4,'zl'=2] {'x'}, dimensions={0} | all-to-all | bytes 2097152 | tf_op jit(solution)/shard_map/all_to_all | solution.py:22
  73.6 0.1 convert_reduce_fusion
  73.8 0.0 copy-done.1
  73.8 0.1 fusion.28
  73.9 1.1 broadcast_in_dim.40
  74.9 4.2 %all-to-all-start.2 = ((bf16[4,256,512]{2,1,0:T(8,128)(2,1)}), bf16[4,256,512]{2,1,0:T(8,128)(2,1)}, u32[]{:S(2)}, u32[]{:S(2)}) async-start(bf16[4,256,512]{2,1,0:T(8,128)(2,1)} %broadcast_in_dim.40), calls=%async_computation.2 | async-start | bytes 2097152 | tf_op jit(solution)/shard_map/all_to_all | solution.py:22
  79.2 1.6 %copy.13 = f32[1,512,512]{1,2,0:T(8,128)S(1)} copy(f32[1,512,512]{2,1,0:T(8,128)} %param.10) | data formatting | bytes 2097152 | tf_op args[4]
  80.7 2.6 %copy.19 = f32[1,512,512]{1,2,0:T(8,128)} copy(f32[1,512,512]{2,1,0:T(8,128)} %param.11) | data formatting | bytes 2097152 | tf_op args[5]
  83.3 10.2 %all-to-all-done.2 = bf16[4,256,512]{2,1,0:T(8,128)(2,1)} async-done(((bf16[4,256,512]{2,1,0:T(8,128)(2,1)}), bf16[4,256,512]{2,1,0:T(8,128)(2,1)}, u32[]{:S(2)}, u32[]{:S(2)}) %all-to-all-start.2) | async-done | bytes 1048608 | tf_op jit(solution)/shard_map/all_to_all | solution.py:22
  93.5 1.9 %fusion = bf16[512,512]{1,0:T(8,128)(2,1)S(1)} fusion(bf16[1024,512]{1,0:T(8,128)(2,1)} %bitcast.29, bf16[1024,1024]{1,0:T(8,128)(2,1)S(1)} %bitcast.180), kind=kOutput, calls=%fused_computation.3 | convolution fusion | flops 536870912 | bytes 2621440 | tf_op jit(solution)/shard_map/dot_general | solution.py:97
  95.5 2.7 %collective-permute-start.6 = (bf16[32,8,512]{2,1,0:T(8,128)(2,1)S(1)}, bf16[32,8,512]{2,1,0:T(8,128)(2,1)S(1)}, u32[]{:S(2)}, u32[]{:S(2)}) collective-permute-start(bf16[32,8,512]{2,1,0:T(8,128)(2,1)S(1)} %get-tuple-element.16), channel_id=1, source_target_pairs={{0,1},{1,0},{2,3},{3,2},{4,5},{5,4},{6,7},{7,6},{8,9},{9,8},{10,11... | collective-permute-start | bytes 786440 | tf_op jit(solution)/shard_map/ppermute | solution.py:107
  98.2 0.0 copy-start
  98.2 3.3 %collective-permute-start.5 = (bf16[32,8,512]{2,1,0:T(8,128)(2,1)S(1)}, bf16[32,8,512]{2,1,0:T(8,128)(2,1)S(1)}, u32[]{:S(2)}, u32[]{:S(2)}) collective-permute-start(bf16[32,8,512]{2,1,0:T(8,128)(2,1)S(1)} %get-tuple-element.17), channel_id=1, source_target_pairs={{0,1},{1,0},{2,3},{3,2},{4,5},{5,4},{6,7},{7,6},{8,9},{9,8},{10,11... | collective-permute-start | bytes 786440 | tf_op jit(solution)/shard_map/ppermute | solution.py:107
  101.5 2.0 %fusion.4 = f32[512,512]{1,0:T(8,128)S(1)} fusion(bf16[1024,512]{1,0:T(8,128)(2,1)} %bitcast.29, bf16[1024,1024]{1,0:T(8,128)(2,1)S(1)} %bitcast.181), kind=kOutput, calls=%fused_computation.7 | convolution fusion | flops 536870912 | bytes 3145728 | tf_op jit(solution)/shard_map/dot_general | solution.py:97
  103.4 2.7 %collective-permute-done.6 = bf16[32,8,512]{2,1,0:T(8,128)(2,1)S(1)} collective-permute-done((bf16[32,8,512]{2,1,0:T(8,128)(2,1)S(1)}, bf16[32,8,512]{2,1,0:T(8,128)(2,1)S(1)}, u32[]{:S(2)}, u32[]{:S(2)}) %collective-permute-start.6) | collective-permute-done | bytes 262176 | tf_op jit(solution)/shard_map/ppermute | solution.py:107
  106.2 0.0 copy-done
  106.2 0.4 fusion.27
  106.5 0.0 copy-start.3
  106.5 1.9 %collective-permute-start.7 = (bf16[32,8,512]{2,1,0:T(8,128)(2,1)S(1)}, bf16[32,8,512]{2,1,0:T(8,128)(2,1)S(1)}, u32[]{:S(2)}, u32[]{:S(2)}) collective-permute-start(bf16[32,8,512]{2,1,0:T(8,128)(2,1)S(1)} %fusion.27), channel_id=1, source_target_pairs={{0,8},{8,0},{1,9},{9,1},{2,10},{10,2},{3,11},{11,3},{4,12},{12,4},... | collective-permute-start | bytes 786440 | tf_op jit(solution)/shard_map/ppermute | solution.py:122
  108.5 0.5 collective-permute-done.5
  109.0 0.4 fusion.14
  109.3 0.6 collective-permute-done.7
  110.0 0.1 add_convert_fusion.1
  110.0 20.4 %all_to_all.21 = bf16[32,8,512]{2,1,0:T(8,128)(2,1)S(1)} all-to-all(bf16[32,8,512]{2,1,0:T(8,128)(2,1)S(1)} %add_convert_fusion.1), channel_id=1, replica_groups=mesh['zh'=4,'y'=8,'c'=2,'x'=4,'zl'=2] {'zh','y'}, dimensions={0} | all-to-all | bytes 524288 | tf_op jit(solution)/shard_map/all_to_all | solution.py:22
  130.5 0.0 copy-done.3
  130.5 0.6 multiply_subtract_fusion
  (5 shorter events, 0.2 us)
Async XLA Ops:
  2.4 8.5 %copy-start.2 = (f32[512,8]{0,1:T(8,128)S(1)}, f32[512,8]{0,1:T(8,128)}, u32[]{:S(2)}) copy-start(f32[512,8]{0,1:T(8,128)} %param.6) | copy-start | bytes 49156
  3.4 30.9 %collective-permute-start.1 = (bf16[256,1536]{1,0:T(8,128)(2,1)}, bf16[256,1536]{1,0:T(8,128)(2,1)}, u32[]{:S(2)}, u32[]{:S(2)}) collective-permute-start(bf16[256,1536]{1,0:T(8,128)(2,1)} %pad_maximum_fusion.2), channel_id=1, source_target_pairs={{0,6},{2,0},{4,2},{6,4},{1,7},{3,1},{5,3},{7,5},{8,14},{10,8},{12,... | collective-permute-start | bytes 2359304 | tf_op jit(solution)/shard_map/ppermute | solution.py:59
  9.0 22.4 %collective-permute-start = (bf16[256,1536]{1,0:T(8,128)(2,1)}, bf16[256,1536]{1,0:T(8,128)(2,1)}, u32[]{:S(2)}, u32[]{:S(2)}) collective-permute-start(bf16[256,1536]{1,0:T(8,128)(2,1)} %pad_maximum_fusion.1), channel_id=1, source_target_pairs={{0,2},{2,4},{4,6},{6,0},{1,3},{3,5},{5,7},{7,1},{8,10},{10,12},{12... | collective-permute-start | bytes 2359304 | tf_op jit(solution)/shard_map/ppermute | solution.py:58
  11.7 36.8 %all-to-all-start = ((bf16[64,8,512]{2,1,0:T(8,128)(2,1)}), bf16[64,8,512]{2,1,0:T(8,128)(2,1)S(1)}, u32[]{:S(2)}, u32[]{:S(2)}) async-start(bf16[64,8,512]{2,1,0:T(8,128)(2,1)} %broadcast_in_dim.38), calls=%async_computation | async-start | bytes 1048576 | tf_op jit(solution)/shard_map/all_to_all | solution.py:22
  32.3 19.2 %collective-permute-start.2 = (bf16[256,512]{1,0:T(8,128)(2,1)S(1)}, bf16[256,512]{1,0:T(8,128)(2,1)S(1)}, u32[]{:S(2)}, u32[]{:S(2)}) collective-permute-start(bf16[256,512]{1,0:T(8,128)(2,1)S(1)} %slice.28), channel_id=1, source_target_pairs={{0,2},{2,4},{4,6},{6,0},{1,3},{3,5},{5,7},{7,1},{8,10},{10,12},{12... | collective-permute-start | bytes 786440 | tf_op jit(solution)/shard_map/ppermute | solution.py:60
  36.0 15.7 %collective-permute-start.3 = (bf16[256,512]{1,0:T(8,128)(2,1)}, bf16[256,512]{1,0:T(8,128)(2,1)S(1)}, u32[]{:S(2)}, u32[]{:S(2)}) collective-permute-start(bf16[256,512]{1,0:T(8,128)(2,1)} %slice.29), channel_id=1, source_target_pairs={{0,6},{2,0},{4,2},{6,4},{1,7},{3,1},{5,3},{7,5},{8,14},{10,8},{12,... | collective-permute-start | bytes 786440 | tf_op jit(solution)/shard_map/ppermute | solution.py:61
  48.6 3.8 %collective-permute-start.4 = (bf16[2,32,8,512]{3,2,1,0:T(8,128)(2,1)S(1)}, bf16[2,32,8,512]{3,2,1,0:T(8,128)(2,1)S(1)}, u32[]{:S(2)}, u32[]{:S(2)}) collective-permute-start(bf16[2,32,8,512]{3,2,1,0:T(8,128)(2,1)S(1)} %bitcast.189), channel_id=1, source_target_pairs={{0,8},{8,0},{1,9},{9,1},{2,10},{10,2},{3,11},{11,3},{4,12},{12,4},... | collective-permute-start | bytes 1572872 | tf_op jit(solution)/shard_map/ppermute | solution.py:77
  54.1 19.7 %copy-start.1 = (bf16[1,256,512]{2,1,0:T(8,128)(2,1)S(1)}, bf16[1,256,512]{2,1,0:T(8,128)(2,1)}, u32[]{:S(2)}) copy-start(bf16[1,256,512]{2,1,0:T(8,128)(2,1)} %param.9) | copy-start | bytes 786436
  74.9 18.5 %all-to-all-start.2 = ((bf16[4,256,512]{2,1,0:T(8,128)(2,1)}), bf16[4,256,512]{2,1,0:T(8,128)(2,1)}, u32[]{:S(2)}, u32[]{:S(2)}) async-start(bf16[4,256,512]{2,1,0:T(8,128)(2,1)} %broadcast_in_dim.40), calls=%async_computation.2 | async-start | bytes 2097152 | tf_op jit(solution)/shard_map/all_to_all | solution.py:22
  95.5 10.7 %collective-permute-start.6 = (bf16[32,8,512]{2,1,0:T(8,128)(2,1)S(1)}, bf16[32,8,512]{2,1,0:T(8,128)(2,1)S(1)}, u32[]{:S(2)}, u32[]{:S(2)}) collective-permute-start(bf16[32,8,512]{2,1,0:T(8,128)(2,1)S(1)} %get-tuple-element.16), channel_id=1, source_target_pairs={{0,1},{1,0},{2,3},{3,2},{4,5},{5,4},{6,7},{7,6},{8,9},{9,8},{10,11... | collective-permute-start | bytes 786440 | tf_op jit(solution)/shard_map/ppermute | solution.py:107
  98.2 8.0 %copy-start = (f32[1,512,512]{1,2,0:T(8,128)S(1)}, f32[1,512,512]{1,2,0:T(8,128)}, u32[]{:S(2)}) copy-start(f32[1,512,512]{1,2,0:T(8,128)} %copy.19) | copy-start | bytes 3145732
  98.2 10.8 %collective-permute-start.5 = (bf16[32,8,512]{2,1,0:T(8,128)(2,1)S(1)}, bf16[32,8,512]{2,1,0:T(8,128)(2,1)S(1)}, u32[]{:S(2)}, u32[]{:S(2)}) collective-permute-start(bf16[32,8,512]{2,1,0:T(8,128)(2,1)S(1)} %get-tuple-element.17), channel_id=1, source_target_pairs={{0,1},{1,0},{2,3},{3,2},{4,5},{5,4},{6,7},{7,6},{8,9},{9,8},{10,11... | collective-permute-start | bytes 786440 | tf_op jit(solution)/shard_map/ppermute | solution.py:107
  106.5 24.0 %copy-start.3 = (f32[512,8]{0,1:T(8,128)S(1)}, f32[512,8]{0,1:T(8,128)}, u32[]{:S(2)}) copy-start(f32[512,8]{0,1:T(8,128)} %param.7) | copy-start | bytes 49156
  106.5 3.4 %collective-permute-start.7 = (bf16[32,8,512]{2,1,0:T(8,128)(2,1)S(1)}, bf16[32,8,512]{2,1,0:T(8,128)(2,1)S(1)}, u32[]{:S(2)}, u32[]{:S(2)}) collective-permute-start(bf16[32,8,512]{2,1,0:T(8,128)(2,1)S(1)} %fusion.27), channel_id=1, source_target_pairs={{0,8},{8,0},{1,9},{9,1},{2,10},{10,2},{3,11},{11,3},{4,12},{12,4},... | collective-permute-start | bytes 786440 | tf_op jit(solution)/shard_map/ppermute | solution.py:122

commit v8 on v7

--- a/solution.py
+++ b/solution.py
@@ -55,30 +55,27 @@
     def merge(*parts):
         return jnp.concatenate(parts, axis=1)
 
-    from_left = lax.ppermute(merge(cut(1, 0), cut(1, 1), cut(2, 0)), "x", right)
-    from_right = lax.ppermute(merge(cut(3, 0), cut(3, 1), cut(2, 1)), "x", left)
-    far_left = lax.ppermute(from_left[:, 2 * rows :], "x", right)
-    far_right = lax.ppermute(from_right[:, 2 * rows :], "x", left)
+    from_left = lax.ppermute(merge(cut(1, 0), cut(1, 1)), "x", right)
+    from_right = lax.ppermute(merge(cut(3, 0), cut(3, 1)), "x", left)
+    after = 0 * (from_left[0, 0] + from_right[0, 0])
+    across = merge(cut(2, 0), cut(2, 1)) + after
+    across = lax.ppermute(across, "x", [(i, (i + 2) % nx) for i in range(nx)])
 
     held = jnp.zeros((nx, count, 2 * rows), tok.dtype)
-    for d, first, block in (
-        (0, 0, merge(cut(0, 0), cut(0, 1))),
-        (3, 0, from_left[:, : 2 * rows]),
-        (1, 0, from_right[:, : 2 * rows]),
-        (2, 0, far_left),
-        (2, rows, far_right),
+    for d, block in (
+        (0, merge(cut(0, 0), cut(0, 1))),
+        (3, from_left),
+        (1, from_right),
+        (2, across),
     ):
-        at = ((at_x + d) % nx, 0, first)
+        at = ((at_x + d) % nx, 0, 0)
         held = lax.dynamic_update_slice(held, block[None], at, allow_negative_indices=False)
     held = held.reshape(nx * count, 2 * rows)
 
     own = anchor.astype(jnp.bfloat16).T
     half = spread(own, ("zl",) + FAR).reshape(2, far, owned, rows)
-    swapped = lax.ppermute(half, "c", swap)
-
-    first = jnp.where(at_c == 0, half, swapped)
-    start = jnp.stack([first, jnp.where(at_c == 0, swapped, half)], 2)
-    start = start.reshape(2, columns, rows)
+    start = [lax.all_gather(half[i], "c", axis=1).reshape(columns, rows) for i in (0, 1)]
+    start = jnp.stack(start)
 
     def project(first, at):
         return lax.dot_general(

time: 132 us -> 132 us (level)
  starting transfers between devices: 44.2 us -> 39.5 us
  blocking collectives: 40 us -> 41.9 us
  waiting for transfers between devices: 23.8 us -> 22.2 us
  other arithmetic: 3.8 us -> 5.31 us
  local copies, waits for them, and re-layouts: 12.9 us -> 14.4 us
    ppermute x5 -> x3, starting transfers between devices: 15.5 us -> 10.7 us  [the longest x1 3.71 us: local(): across = lax.ppermute(across, 'x', [(i, (i + 2) % nx) for i in range(nx)])]
    all_gather x0 -> x2, blocking collectives: none -> 4.35 us  [local(): lax.all_gather(half[i], 'c', axis=1).reshape(columns, rows)]
    ppermute x5 -> x3, waiting for transfers between devices: 3.4 us -> 0.01 us  [the longest x1 0.01 us: local(): from_right = lax.ppermute(merge(cut(3, 0), cut(3, 1)), 'x', left)]
    all_to_all x2, blocking collectives: 40 us -> 37.5 us  [exchange(): return lax.all_to_all(blocks, axes, 0, 0)]
    all_to_all x2, waiting for transfers between devices: 16.6 us -> 18.3 us  [exchange(): return lax.all_to_all(blocks, axes, 0, 0)]
    dynamic_update_slice x4 -> x3, local copies, waits for them, and re-layouts: 2.22 us -> 3.24 us  [local(): lax.dynamic_update_slice(held, block[None], at, allow_negative_indices=Fa...]
    slice x2 -> x3, local copies, waits for them, and re-layouts: 2.65 us -> 2.39 us  [the longest x2 2.35 us: local(): after = 0 * (from_left[0, 0] + from_right[0, 0])]
  transfers between devices with their start and end apart: 10 -> 8, of which waited for: 7 -> 5; matrix products, arithmetic and copies ran while one was open for 10% -> 12% of each run, Pallas kernels for 0% -> 0%
where the time goes in v8:
time: 132 us; the launch traced here: 131 us
  blocking collectives  41.9 us (32%)
  starting transfers between devices  39.5 us (30%)
  waiting for transfers between devices  22.2 us (17%)
  local copies, waits for them, and re-layouts  14.4 us (11%)
  matrix products  5.52 us (4%)
  other arithmetic  5.31 us (4%)
  between operations  2.25 us (2%)
    all_to_all x2, blocking collectives, exchange(): return lax.all_to_all(blocks, axes, 0, 0)  37.5 us
    all_to_all x2, starting transfers between devices, exchange(): return lax.all_to_all(blocks, axes, 0, 0)  20.8 us
    all_to_all x2, waiting for transfers between devices, exchange(): return lax.all_to_all(blocks, axes, 0, 0)  18.3 us
    ppermute x2, starting transfers between devices, local(): lax.ppermute(of(lent, at).astype(jnp.bfloat16), 'zl', swap)  5.97 us
    all_gather x2, blocking collectives, local(): lax.all_gather(half[i], 'c', axis=1).reshape(columns, rows)  4.35 us
    unnamed x10, local copies, waits for them, and re-layouts  4.14 us
    dot_general x2, matrix products, term(): lax.dot_general(residual, held[:, first:first + rows], (((0,), (0,)), (()...  3.91 us
    ppermute x1, starting transfers between devices, local(): across = lax.ppermute(across, 'x', [(i, (i + 2) % nx) for i in range(nx)])  3.71 us
  transfers between devices with their start and end apart: 8, of which 5 were waited for; matrix products, arithmetic and copies ran while one was open for 12% of the time, Pallas kernels for 0%

profile of v8, /device:TPU:8, one launch (start us, length us, event | category | flops | bytes accessed | tf_op | source)
XLA Modules:
  0.0 131.1 jit_solution(14477222509365464426)
XLA Ops:
  0.7 2.4 %dynamic-slice_bitcast_fusion.1 = (bf16[256,512]{1,0:T(8,128)(2,1)S(1)}, bf16[256,512]{1,0:T(8,128)(2,1)S(1)}, bf16[256,512]{1,0:T(8,128)(2,1)S(1)}, bf16[256,51...) fusion(bf16[1,256,4096]{2,1,0:T(8,128)(2,1)} %param.8, ...), kind=kLoop, calls=%fused_computation.55 | loop fusion | bytes 4194336 | tf_op jit(solution)/shard_map/dynamic_slice | solution.py:53
  3.1 0.0 copy-start.2
  3.1 0.9 pad_maximum_fusion
  4.0 3.4 %collective-permute-start = (bf16[256,1024]{1,0:T(8,128)(2,1)}, bf16[256,1024]{1,0:T(8,128)(2,1)}, u32[]{:S(2)}, u32[]{:S(2)}) collective-permute-start(bf16[256,1024]{1,0:T(8,128)(2,1)} %pad_maximum_fusion), channel_id=1, source_target_pairs={{0,2},{2,4},{4,6},{6,0},{1,3},{3,5},{5,7},{7,1},{8,10},{10,12},{12... | collective-permute-start | bytes 1572872 | tf_op jit(solution)/shard_map/ppermute | solution.py:58
  7.4 0.9 pad_maximum_fusion.1
  8.2 3.6 %collective-permute-start.1 = (bf16[256,1024]{1,0:T(8,128)(2,1)}, bf16[256,1024]{1,0:T(8,128)(2,1)}, u32[]{:S(2)}, u32[]{:S(2)}) collective-permute-start(bf16[256,1024]{1,0:T(8,128)(2,1)} %pad_maximum_fusion.1), channel_id=1, source_target_pairs={{0,6},{2,0},{4,2},{6,4},{1,7},{3,1},{5,3},{7,5},{8,14},{10,8},{12,... | collective-permute-start | bytes 1572872 | tf_op jit(solution)/shard_map/ppermute | solution.py:59
  11.9 0.0 copy-done.2
  11.9 0.9 broadcast_in_dim.34
  12.8 16.6 %all-to-all-start = ((bf16[64,8,512]{2,1,0:T(8,128)(2,1)}), bf16[64,8,512]{2,1,0:T(8,128)(2,1)S(1)}, u32[]{:S(2)}, u32[]{:S(2)}) async-start(bf16[64,8,512]{2,1,0:T(8,128)(2,1)} %broadcast_in_dim.34), calls=%async_computation | async-start | bytes 1048576 | tf_op jit(solution)/shard_map/all_to_all | solution.py:22
  29.4 0.3 broadcast_in_dim.29
  29.6 1.0 fusion.13
  30.6 0.0 collective-permute-done
  30.6 1.2 slice.28
  31.8 0.0 collective-permute-done.1
  31.8 1.2 slice.29
  34.3 0.9 maximum_add_fusion
  35.2 3.7 %collective-permute-start.2 = (bf16[256,1024]{1,0:T(8,128)(2,1)}, bf16[256,1024]{1,0:T(8,128)(2,1)}, u32[]{:S(2)}, u32[]{:S(2)}) collective-permute-start(bf16[256,1024]{1,0:T(8,128)(2,1)} %maximum_add_fusion), channel_id=1, source_target_pairs={{0,4},{2,6},{4,0},{6,2},{1,5},{3,7},{5,1},{7,3},{8,12},{10,14},{12... | collective-permute-start | bytes 1572872 | tf_op jit(solution)/shard_map/ppermute | solution.py:62
  38.9 1.1 bitcast_dynamic-update-slice_fusion.2
  40.0 1.1 bitcast_dynamic-update-slice_fusion.1
  41.1 8.2 %all-to-all-done = bf16[64,8,512]{2,1,0:T(8,128)(2,1)S(1)} async-done(((bf16[64,8,512]{2,1,0:T(8,128)(2,1)}), bf16[64,8,512]{2,1,0:T(8,128)(2,1)S(1)}, u32[]{:S(2)}, u32[]{:S(2)}) %all-to-all-start) | async-done | bytes 524320 | tf_op jit(solution)/shard_map/all_to_all | solution.py:22
  49.3 2.2 %all-gather = bf16[32,16,512]{2,1,0:T(8,128)(2,1)S(1)} all-gather(bf16[32,8,512]{2,1,0:T(8,128)(2,1)S(1)} %get-tuple-element.17), channel_id=2, replica_groups=mesh['zh'=4,'y'=8,'c'=2,'x'=4,'zl'=2] {'c'}, dimensions={1}, use_global_device_ids=true | all-gather | bytes 786432 | tf_op jit(solution)/shard_map/all_gather | solution.py:77
  51.5 2.2 %all-gather.1 = bf16[32,16,512]{2,1,0:T(8,128)(2,1)S(1)} all-gather(bf16[32,8,512]{2,1,0:T(8,128)(2,1)S(1)} %get-tuple-element.16), channel_id=3, replica_groups=mesh['zh'=4,'y'=8,'c'=2,'x'=4,'zl'=2] {'c'}, dimensions={1}, use_global_device_ids=true | all-gather | bytes 786432 | tf_op jit(solution)/shard_map/all_gather | solution.py:77
  53.7 0.0 collective-permute-done.2
  53.7 1.1 bitcast_dynamic-update-slice_fusion
  54.8 0.8 fusion.2
  55.6 0.8 add_convert_fusion
  56.4 0.0 copy-start.1
  56.4 18.4 %all_to_all.20 = bf16[4,256,512]{2,1,0:T(8,128)(2,1)S(1)} all-to-all(bf16[4,256,512]{2,1,0:T(8,128)(2,1)S(1)} %bitcast.179), channel_id=1, replica_groups=mesh['zh'=4,'y'=8,'c'=2,'x'=4,'zl'=2] {'x'}, dimensions={0} | all-to-all | bytes 2097152 | tf_op jit(solution)/shard_map/all_to_all | solution.py:22
  74.8 0.1 convert_reduce_fusion
  75.0 0.0 copy-done.1
  75.0 0.1 fusion.28
  75.1 1.1 broadcast_in_dim.36
  76.1 4.2 %all-to-all-start.2 = ((bf16[4,256,512]{2,1,0:T(8,128)(2,1)}), bf16[4,256,512]{2,1,0:T(8,128)(2,1)}, u32[]{:S(2)}, u32[]{:S(2)}) async-start(bf16[4,256,512]{2,1,0:T(8,128)(2,1)} %broadcast_in_dim.36), calls=%async_computation.2 | async-start | bytes 2097152 | tf_op jit(solution)/shard_map/all_to_all | solution.py:22
  80.4 1.6 %copy.13 = f32[1,512,512]{1,2,0:T(8,128)S(1)} copy(f32[1,512,512]{2,1,0:T(8,128)} %param.10) | data formatting | bytes 2097152 | tf_op args[4]
  82.0 2.6 %copy.18 = f32[1,512,512]{1,2,0:T(8,128)} copy(f32[1,512,512]{2,1,0:T(8,128)} %param.11) | data formatting | bytes 2097152 | tf_op args[5]
  84.5 10.2 %all-to-all-done.2 = bf16[4,256,512]{2,1,0:T(8,128)(2,1)} async-done(((bf16[4,256,512]{2,1,0:T(8,128)(2,1)}), bf16[4,256,512]{2,1,0:T(8,128)(2,1)}, u32[]{:S(2)}, u32[]{:S(2)}) %all-to-all-start.2) | async-done | bytes 1048608 | tf_op jit(solution)/shard_map/all_to_all | solution.py:22
  94.7 2.0 %fusion = bf16[512,512]{1,0:T(8,128)(2,1)S(1)} fusion(bf16[1024,512]{1,0:T(8,128)(2,1)} %bitcast.26, bf16[1024,1024]{1,0:T(8,128)(2,1)S(1)} %bitcast.169), kind=kOutput, calls=%fused_computation.6 | convolution fusion | flops 536870912 | bytes 2621440 | tf_op jit(solution)/shard_map/dot_general | solution.py:94
  96.7 2.7 %collective-permute-start.4 = (bf16[32,8,512]{2,1,0:T(8,128)(2,1)S(1)}, bf16[32,8,512]{2,1,0:T(8,128)(2,1)S(1)}, u32[]{:S(2)}, u32[]{:S(2)}) collective-permute-start(bf16[32,8,512]{2,1,0:T(8,128)(2,1)S(1)} %get-tuple-element.14), channel_id=1, source_target_pairs={{0,1},{1,0},{2,3},{3,2},{4,5},{5,4},{6,7},{7,6},{8,9},{9,8},{10,11... | collective-permute-start | bytes 786440 | tf_op jit(solution)/shard_map/ppermute | solution.py:104
  99.4 0.0 copy-start
  99.4 3.3 %collective-permute-start.3 = (bf16[32,8,512]{2,1,0:T(8,128)(2,1)S(1)}, bf16[32,8,512]{2,1,0:T(8,128)(2,1)S(1)}, u32[]{:S(2)}, u32[]{:S(2)}) collective-permute-start(bf16[32,8,512]{2,1,0:T(8,128)(2,1)S(1)} %get-tuple-element.15), channel_id=1, source_target_pairs={{0,1},{1,0},{2,3},{3,2},{4,5},{5,4},{6,7},{7,6},{8,9},{9,8},{10,11... | collective-permute-start | bytes 786440 | tf_op jit(solution)/shard_map/ppermute | solution.py:104
  102.7 2.0 %fusion.4 = f32[512,512]{1,0:T(8,128)S(1)} fusion(bf16[1024,512]{1,0:T(8,128)(2,1)} %bitcast.26, bf16[1024,1024]{1,0:T(8,128)(2,1)S(1)} %bitcast.170), kind=kOutput, calls=%fused_computation.10 | convolution fusion | flops 536870912 | bytes 3145728 | tf_op jit(solution)/shard_map/dot_general | solution.py:94
  104.7 2.7 %collective-permute-done.4 = bf16[32,8,512]{2,1,0:T(8,128)(2,1)S(1)} collective-permute-done((bf16[32,8,512]{2,1,0:T(8,128)(2,1)S(1)}, bf16[32,8,512]{2,1,0:T(8,128)(2,1)S(1)}, u32[]{:S(2)}, u32[]{:S(2)}) %collective-permute-start.4) | collective-permute-done | bytes 262176 | tf_op jit(solution)/shard_map/ppermute | solution.py:104
  107.4 0.0 copy-done
  107.4 0.4 fusion.27
  107.8 0.0 copy-start.3
  107.8 1.9 %collective-permute-start.5 = (bf16[32,8,512]{2,1,0:T(8,128)(2,1)S(1)}, bf16[32,8,512]{2,1,0:T(8,128)(2,1)S(1)}, u32[]{:S(2)}, u32[]{:S(2)}) collective-permute-start(bf16[32,8,512]{2,1,0:T(8,128)(2,1)S(1)} %fusion.27), channel_id=1, source_target_pairs={{0,8},{8,0},{1,9},{9,1},{2,10},{10,2},{3,11},{11,3},{4,12},{12,4},... | collective-permute-start | bytes 786440 | tf_op jit(solution)/shard_map/ppermute | solution.py:119
  109.7 0.5 collective-permute-done.3
  110.2 0.4 fusion.18
  110.6 0.6 collective-permute-done.5
  111.2 0.1 add_convert_fusion.1
  111.3 19.1 %all_to_all.21 = bf16[32,8,512]{2,1,0:T(8,128)(2,1)S(1)} all-to-all(bf16[32,8,512]{2,1,0:T(8,128)(2,1)S(1)} %add_convert_fusion.1), channel_id=1, replica_groups=mesh['zh'=4,'y'=8,'c'=2,'x'=4,'zl'=2] {'zh','y'}, dimensions={0} | all-to-all | bytes 524288 | tf_op jit(solution)/shard_map/all_to_all | solution.py:22
  130.5 0.0 copy-done.3
  130.5 0.6 multiply_subtract_fusion
  (4 shorter events, 0.1 us)
Async XLA Ops:
  3.1 8.8 %copy-start.2 = (f32[512,8]{0,1:T(8,128)S(1)}, f32[512,8]{0,1:T(8,128)}, u32[]{:S(2)}) copy-start(f32[512,8]{0,1:T(8,128)} %param.6) | copy-start | bytes 49156
  4.0 26.7 %collective-permute-start = (bf16[256,1024]{1,0:T(8,128)(2,1)}, bf16[256,1024]{1,0:T(8,128)(2,1)}, u32[]{:S(2)}, u32[]{:S(2)}) collective-permute-start(bf16[256,1024]{1,0:T(8,128)(2,1)} %pad_maximum_fusion), channel_id=1, source_target_pairs={{0,2},{2,4},{4,6},{6,0},{1,3},{3,5},{5,7},{7,1},{8,10},{10,12},{12... | collective-permute-start | bytes 1572872 | tf_op jit(solution)/shard_map/ppermute | solution.py:58
  8.2 23.6 %collective-permute-start.1 = (bf16[256,1024]{1,0:T(8,128)(2,1)}, bf16[256,1024]{1,0:T(8,128)(2,1)}, u32[]{:S(2)}, u32[]{:S(2)}) collective-permute-start(bf16[256,1024]{1,0:T(8,128)(2,1)} %pad_maximum_fusion.1), channel_id=1, source_target_pairs={{0,6},{2,0},{4,2},{6,4},{1,7},{3,1},{5,3},{7,5},{8,14},{10,8},{12,... | collective-permute-start | bytes 1572872 | tf_op jit(solution)/shard_map/ppermute | solution.py:59
  12.8 36.5 %all-to-all-start = ((bf16[64,8,512]{2,1,0:T(8,128)(2,1)}), bf16[64,8,512]{2,1,0:T(8,128)(2,1)S(1)}, u32[]{:S(2)}, u32[]{:S(2)}) async-start(bf16[64,8,512]{2,1,0:T(8,128)(2,1)} %broadcast_in_dim.34), calls=%async_computation | async-start | bytes 1048576 | tf_op jit(solution)/shard_map/all_to_all | solution.py:22
  35.2 18.5 %collective-permute-start.2 = (bf16[256,1024]{1,0:T(8,128)(2,1)}, bf16[256,1024]{1,0:T(8,128)(2,1)}, u32[]{:S(2)}, u32[]{:S(2)}) collective-permute-start(bf16[256,1024]{1,0:T(8,128)(2,1)} %maximum_add_fusion), channel_id=1, source_target_pairs={{0,4},{2,6},{4,0},{6,2},{1,5},{3,7},{5,1},{7,3},{8,12},{10,14},{12... | collective-permute-start | bytes 1572872 | tf_op jit(solution)/shard_map/ppermute | solution.py:62
  56.4 18.6 %copy-start.1 = (bf16[1,256,512]{2,1,0:T(8,128)(2,1)S(1)}, bf16[1,256,512]{2,1,0:T(8,128)(2,1)}, u32[]{:S(2)}) copy-start(bf16[1,256,512]{2,1,0:T(8,128)(2,1)} %param.9) | copy-start | bytes 786436
  76.1 18.6 %all-to-all-start.2 = ((bf16[4,256,512]{2,1,0:T(8,128)(2,1)}), bf16[4,256,512]{2,1,0:T(8,128)(2,1)}, u32[]{:S(2)}, u32[]{:S(2)}) async-start(bf16[4,256,512]{2,1,0:T(8,128)(2,1)} %broadcast_in_dim.36), calls=%async_computation.2 | async-start | bytes 2097152 | tf_op jit(solution)/shard_map/all_to_all | solution.py:22
  96.7 10.7 %collective-permute-start.4 = (bf16[32,8,512]{2,1,0:T(8,128)(2,1)S(1)}, bf16[32,8,512]{2,1,0:T(8,128)(2,1)S(1)}, u32[]{:S(2)}, u32[]{:S(2)}) collective-permute-start(bf16[32,8,512]{2,1,0:T(8,128)(2,1)S(1)} %get-tuple-element.14), channel_id=1, source_target_pairs={{0,1},{1,0},{2,3},{3,2},{4,5},{5,4},{6,7},{7,6},{8,9},{9,8},{10,11... | collective-permute-start | bytes 786440 | tf_op jit(solution)/shard_map/ppermute | solution.py:104
  99.4 8.0 %copy-start = (f32[1,512,512]{1,2,0:T(8,128)S(1)}, f32[1,512,512]{1,2,0:T(8,128)}, u32[]{:S(2)}) copy-start(f32[1,512,512]{1,2,0:T(8,128)} %copy.18) | copy-start | bytes 3145732
  99.4 10.8 %collective-permute-start.3 = (bf16[32,8,512]{2,1,0:T(8,128)(2,1)S(1)}, bf16[32,8,512]{2,1,0:T(8,128)(2,1)S(1)}, u32[]{:S(2)}, u32[]{:S(2)}) collective-permute-start(bf16[32,8,512]{2,1,0:T(8,128)(2,1)S(1)} %get-tuple-element.15), channel_id=1, source_target_pairs={{0,1},{1,0},{2,3},{3,2},{4,5},{5,4},{6,7},{7,6},{8,9},{9,8},{10,11... | collective-permute-start | bytes 786440 | tf_op jit(solution)/shard_map/ppermute | solution.py:104
  107.8 22.7 %copy-start.3 = (f32[512,8]{0,1:T(8,128)S(1)}, f32[512,8]{0,1:T(8,128)}, u32[]{:S(2)}) copy-start(f32[512,8]{0,1:T(8,128)} %param.7) | copy-start | bytes 49156
  107.8 3.4 %collective-permute-start.5 = (bf16[32,8,512]{2,1,0:T(8,128)(2,1)S(1)}, bf16[32,8,512]{2,1,0:T(8,128)(2,1)S(1)}, u32[]{:S(2)}, u32[]{:S(2)}) collective-permute-start(bf16[32,8,512]{2,1,0:T(8,128)(2,1)S(1)} %fusion.27), channel_id=1, source_target_pairs={{0,8},{8,0},{1,9},{9,1},{2,10},{10,2},{3,11},{11,3},{4,12},{12,4},... | collective-permute-start | bytes 786440 | tf_op jit(solution)/shard_map/ppermute | solution.py:119

commit v9 on v8

--- a/solution.py
+++ b/solution.py
@@ -45,29 +45,21 @@
         return lax.dynamic_slice(a, start, size, allow_negative_indices=False)
 
     tok = tokens[0]
-    right = [(i, (i + 1) % nx) for i in range(nx)]
-    left = [(i, (i - 1) % nx) for i in range(nx)]
 
-    def cut(x, zl):
-        at = ((at_x + x) % nx * 2 + (at_zl + zl) % 2) * rows
-        return lax.dynamic_slice(tok, (0, at), (count, rows), allow_negative_indices=False)
+    def cut(d):
+        at = (at_x + d) % nx * 2 * rows
+        size = (count, 2 * rows)
+        return lax.dynamic_slice(tok, (0, at), size, allow_negative_indices=False)
 
-    def merge(*parts):
-        return jnp.concatenate(parts, axis=1)
+    def shift(block, d):
+        return lax.ppermute(block, "x", [(i, (i + d) % nx) for i in range(nx)])
 
-    from_left = lax.ppermute(merge(cut(1, 0), cut(1, 1)), "x", right)
-    from_right = lax.ppermute(merge(cut(3, 0), cut(3, 1)), "x", left)
-    after = 0 * (from_left[0, 0] + from_right[0, 0])
-    across = merge(cut(2, 0), cut(2, 1)) + after
-    across = lax.ppermute(across, "x", [(i, (i + 2) % nx) for i in range(nx)])
+    from_left = shift(cut(1), 1)
+    from_right = shift(cut(3), 3)
+    across = shift(cut(2) + 0 * (from_left + from_right), 2)
 
     held = jnp.zeros((nx, count, 2 * rows), tok.dtype)
-    for d, block in (
-        (0, merge(cut(0, 0), cut(0, 1))),
-        (3, from_left),
-        (1, from_right),
-        (2, across),
-    ):
+    for d, block in ((0, cut(0)), (3, from_left), (1, from_right), (2, across)):
         at = ((at_x + d) % nx, 0, 0)
         held = lax.dynamic_update_slice(held, block[None], at, allow_negative_indices=False)
     held = held.reshape(nx * count, 2 * rows)
@@ -75,36 +67,36 @@
     own = anchor.astype(jnp.bfloat16).T
     half = spread(own, ("zl",) + FAR).reshape(2, far, owned, rows)
     start = [lax.all_gather(half[i], "c", axis=1).reshape(columns, rows) for i in (0, 1)]
-    start = jnp.stack(start)
 
-    def project(first, at):
+    def project(i):
         return lax.dot_general(
-            held[:, first : first + rows], take(start, at, 0)[0], (((1,), (1,)), ((), ())),
+            held[:, i * rows : (i + 1) * rows], start[i], (((1,), (1,)), ((), ())),
             preferred_element_type=jnp.float32,
         )
 
-    partial = project(0, at_zl) + project(rows, 1 - at_zl)
+    partial = project(0) + project(1)
     partial = partial.astype(jnp.bfloat16).reshape(nx, count, columns)
     parts = exchange(partial, "x").astype(jnp.float32)
     projected = jnp.sum(parts, axis=0) * width ** (-0.5)
     residual = (projected - targets[0].astype(jnp.float32)).astype(jnp.bfloat16)
     residual = spread(residual, "x").reshape(nx * count, columns)
 
-    def term(first):
+    def term(zl):
+        met = (nx * count, rows)
+        met = lax.dynamic_slice(held, (0, zl * rows), met, allow_negative_indices=False)
         return lax.dot_general(
-            residual, held[:, first : first + rows], (((0,), (0,)), ((), ())),
-            preferred_element_type=jnp.float32,
+            residual, met, (((0,), (0,)), ((), ())), preferred_element_type=jnp.float32
         )
 
     def of(a, at):
         return take(a.reshape(far, 2, owned, rows), at, 1)[:, 0]
 
-    lent = lax.optimization_barrier(term(rows))
+    lent = lax.optimization_barrier(term(1 - at_zl))
     others = [
         lax.ppermute(of(lent, at).astype(jnp.bfloat16), "zl", swap)
         for at in (1 - at_c, at_c)
     ]
-    kept = lax.optimization_barrier(term(0))
+    kept = lax.optimization_barrier(term(at_zl))
 
     def direct(at, other):
         summed = of(kept, at) + other.astype(jnp.float32)

time: 132 us -> 132 us (level)
  waiting for transfers between devices: 22.2 us -> 28.1 us
  local copies, waits for them, and re-layouts: 14.4 us -> 11.1 us
  other arithmetic: 5.31 us -> 3.81 us
  between operations: 2.25 us -> 0.92 us
    all_to_all x2, waiting for transfers between devices: 18.3 us -> 24 us  [exchange(): return lax.all_to_all(blocks, axes, 0, 0)]
    slice x2 -> x0, local copies, waits for them, and re-layouts: 2.35 us -> none  [local(): after = 0 * (from_left[0, 0] + from_right[0, 0])]
    dynamic_update_slice x3, local copies, waits for them, and re-layouts: 3.24 us -> 1.16 us  [local(): lax.dynamic_update_slice(held, block[None], at, allow_negative_indices=Fa...]
    concatenate x2 -> x0, other arithmetic: 1.72 us -> none  [merge(): return jnp.concatenate(parts, axis=1)]
    unnamed x10 -> x12, local copies, waits for them, and re-layouts: 4.14 us -> 5.47 us
  transfers between devices with their start and end apart: 8 -> 8, of which waited for: 5 -> 5; matrix products, arithmetic and copies ran while one was open for 12% -> 8% of each run, Pallas kernels for 0% -> 0%
where the time goes in v9:
time: 132 us; the launch traced here: 131 us
  blocking collectives  41.9 us (32%)
  starting transfers between devices  39.7 us (30%)
  waiting for transfers between devices  28.1 us (21%)
  local copies, waits for them, and re-layouts  11.1 us (8%)
  matrix products  5.41 us (4%)
  other arithmetic  3.81 us (3%)
    all_to_all x2, blocking collectives, exchange(): return lax.all_to_all(blocks, axes, 0, 0)  37.5 us
    all_to_all x2, waiting for transfers between devices, exchange(): return lax.all_to_all(blocks, axes, 0, 0)  24 us
    all_to_all x2, starting transfers between devices, exchange(): return lax.all_to_all(blocks, axes, 0, 0)  21 us
    ppermute x3, starting transfers between devices, shift(): return lax.ppermute(block, 'x', [(i, (i + d) % nx) for i in range(nx)])  10.8 us
    ppermute x2, starting transfers between devices, local(): lax.ppermute(of(lent, at).astype(jnp.bfloat16), 'zl', swap)  5.97 us
    unnamed x12, local copies, waits for them, and re-layouts  5.47 us
    all_gather x2, blocking collectives, local(): lax.all_gather(half[i], 'c', axis=1).reshape(columns, rows)  4.35 us
    dot_general x2, matrix products, term(): lax.dot_general(residual, met, (((0,), (0,)), ((), ())), preferred_elemen...  3.91 us
  transfers between devices with their start and end apart: 8, of which 5 were waited for; matrix products, arithmetic and copies ran while one was open for 8% of the time, Pallas kernels for 0%

profile of v9, /device:TPU:8, one launch (start us, length us, event | category | flops | bytes accessed | tf_op | source)
XLA Modules:
  0.0 130.8 jit_solution(11509415964289088766)
XLA Ops:
  0.7 0.0 copy-start.1
  0.7 0.3 broadcast_in_dim.27
  0.9 1.3 %copy-done.1 = bf16[1,256,4096]{2,1,0:T(8,128)(2,1)S(1)} copy-done((bf16[1,256,4096]{2,1,0:T(8,128)(2,1)S(1)}, bf16[1,256,4096]{2,1,0:T(8,128)(2,1)}, u32[]{:S(2)}) %copy-start.1) | copy-done | bytes 2097176
  2.3 0.0 copy-start.3
  2.3 1.2 dynamic-slice_bitcast_fusion
  3.4 3.4 %collective-permute-start = (bf16[256,1024]{1,0:T(8,128)(2,1)}, bf16[256,1024]{1,0:T(8,128)(2,1)S(1)}, u32[]{:S(2)}, u32[]{:S(2)}) collective-permute-start(bf16[256,1024]{1,0:T(8,128)(2,1)} %get-tuple-element.7), channel_id=1, source_target_pairs={{0,2},{2,4},{4,6},{6,0},{1,3},{3,5},{5,7},{7,1},{8,10},{10,12},{12... | collective-permute-start | bytes 1572872 | tf_op jit(solution)/shard_map/ppermute | solution.py:55
  6.8 3.7 %collective-permute-start.1 = (bf16[256,1024]{1,0:T(8,128)(2,1)}, bf16[256,1024]{1,0:T(8,128)(2,1)S(1)}, u32[]{:S(2)}, u32[]{:S(2)}) collective-permute-start(bf16[256,1024]{1,0:T(8,128)(2,1)} %get-tuple-element.6), channel_id=1, source_target_pairs={{0,6},{2,0},{4,2},{6,4},{1,7},{3,1},{5,3},{7,5},{8,14},{10,8},{12,... | collective-permute-start | bytes 1572872 | tf_op jit(solution)/shard_map/ppermute | solution.py:55
  10.5 0.0 copy-done.3
  10.5 0.8 broadcast_in_dim.31
  11.3 16.8 %all-to-all-start = ((bf16[64,8,512]{2,1,0:T(8,128)(2,1)}), bf16[64,8,512]{2,1,0:T(8,128)(2,1)}, u32[]{:S(2)}, u32[]{:S(2)}) async-start(bf16[64,8,512]{2,1,0:T(8,128)(2,1)} %broadcast_in_dim.31), calls=%async_computation | async-start | bytes 1048576 | tf_op jit(solution)/shard_map/all_to_all | solution.py:22
  28.1 0.0 collective-permute-done
  28.1 0.0 collective-permute-done.1
  28.2 2.1 %bitcast_add_fusion.3 = bf16[256,1024]{1,0:T(8,128)(2,1)} fusion(bf16[256,1024]{1,0:T(8,128)(2,1)S(1)} %collective-permute-done, bf16[256,1024]{1,0:T(8,128)(2,1)S(1)} %collective-permute-done.1, bf16[1,256,4096]{2,1,0:T(8,128)(2,1)} %param.8, s32[]{:T(128)S(6)} %mul.125), kind=kLoop, calls=%fused_computation.33 | loop fusion | flops 2097152 | bytes 2097156 | tf_op jit(solution)/shard_map/add | solution.py:59
  30.3 3.7 %collective-permute-start.2 = (bf16[256,1024]{1,0:T(8,128)(2,1)}, bf16[256,1024]{1,0:T(8,128)(2,1)}, u32[]{:S(2)}, u32[]{:S(2)}) collective-permute-start(bf16[256,1024]{1,0:T(8,128)(2,1)} %bitcast_add_fusion.3), channel_id=1, source_target_pairs={{0,4},{2,6},{4,0},{6,2},{1,5},{3,7},{5,1},{7,3},{8,12},{10,14},{12... | collective-permute-start | bytes 1572872 | tf_op jit(solution)/shard_map/ppermute | solution.py:55
  34.1 13.9 %all-to-all-done = bf16[64,8,512]{2,1,0:T(8,128)(2,1)} async-done(((bf16[64,8,512]{2,1,0:T(8,128)(2,1)}), bf16[64,8,512]{2,1,0:T(8,128)(2,1)}, u32[]{:S(2)}, u32[]{:S(2)}) %all-to-all-start) | async-done | bytes 524320 | tf_op jit(solution)/shard_map/all_to_all | solution.py:22
  48.0 1.1 fusion.27
  49.1 2.2 %all-gather.1 = bf16[32,16,512]{2,1,0:T(8,128)(2,1)S(1)} all-gather(bf16[32,8,512]{2,1,0:T(8,128)(2,1)S(1)} %get-tuple-element.12), channel_id=3, replica_groups=mesh['zh'=4,'y'=8,'c'=2,'x'=4,'zl'=2] {'c'}, dimensions={1}, use_global_device_ids=true | all-gather | bytes 786432 | tf_op jit(solution)/shard_map/all_gather | solution.py:69
  51.2 2.2 %all-gather = bf16[32,16,512]{2,1,0:T(8,128)(2,1)S(1)} all-gather(bf16[32,8,512]{2,1,0:T(8,128)(2,1)S(1)} %get-tuple-element.11), channel_id=2, replica_groups=mesh['zh'=4,'y'=8,'c'=2,'x'=4,'zl'=2] {'c'}, dimensions={1}, use_global_device_ids=true | all-gather | bytes 786432 | tf_op jit(solution)/shard_map/all_gather | solution.py:69
  53.4 0.0 collective-permute-done.2
  53.4 1.1 bitcast_dynamic-update-slice_fusion
  54.5 0.7 fusion
  55.2 0.8 add_convert_fusion
  56.0 0.0 copy-start.2
  56.0 18.4 %all_to_all.20 = bf16[4,256,512]{2,1,0:T(8,128)(2,1)S(1)} all-to-all(bf16[4,256,512]{2,1,0:T(8,128)(2,1)S(1)} %bitcast.156), channel_id=1, replica_groups=mesh['zh'=4,'y'=8,'c'=2,'x'=4,'zl'=2] {'x'}, dimensions={0} | all-to-all | bytes 2097152 | tf_op jit(solution)/shard_map/all_to_all | solution.py:22
  74.4 0.1 convert_reduce_fusion
  74.6 0.0 copy-done.2
  74.6 0.1 fusion.21
  74.7 1.1 broadcast_in_dim.33
  75.7 4.2 %all-to-all-start.2 = ((bf16[4,256,512]{2,1,0:T(8,128)(2,1)}), bf16[4,256,512]{2,1,0:T(8,128)(2,1)}, u32[]{:S(2)}, u32[]{:S(2)}) async-start(bf16[4,256,512]{2,1,0:T(8,128)(2,1)} %broadcast_in_dim.33), calls=%async_computation.2 | async-start | bytes 2097152 | tf_op jit(solution)/shard_map/all_to_all | solution.py:22
  80.0 1.6 %copy.13 = f32[1,512,512]{1,2,0:T(8,128)S(1)} copy(f32[1,512,512]{2,1,0:T(8,128)} %param.10) | data formatting | bytes 2097152 | tf_op args[4]
  81.6 2.6 %copy.18 = f32[1,512,512]{1,2,0:T(8,128)} copy(f32[1,512,512]{2,1,0:T(8,128)} %param.11) | data formatting | bytes 2097152 | tf_op args[5]
  84.1 10.2 %all-to-all-done.2 = bf16[4,256,512]{2,1,0:T(8,128)(2,1)} async-done(((bf16[4,256,512]{2,1,0:T(8,128)(2,1)}), bf16[4,256,512]{2,1,0:T(8,128)(2,1)}, u32[]{:S(2)}, u32[]{:S(2)}) %all-to-all-start.2) | async-done | bytes 1048608 | tf_op jit(solution)/shard_map/all_to_all | solution.py:22
  94.3 2.0 %fusion.3 = bf16[512,512]{1,0:T(8,128)(2,1)S(1)} fusion(bf16[1024,512]{1,0:T(8,128)(2,1)} %bitcast.17, bf16[1024,1024]{1,0:T(8,128)(2,1)S(1)} %bitcast.150, s32[]{:T(128)S(6)} %mul.132), kind=kOutput, calls=%fused_computation.5 | convolution fusion | flops 536870912 | bytes 2621444 | tf_op jit(solution)/shard_map/dot_general | solution.py:87
  96.2 0.0 copy-start
  96.3 2.8 %collective-permute-start.4 = (bf16[32,8,512]{2,1,0:T(8,128)(2,1)S(1)}, bf16[32,8,512]{2,1,0:T(8,128)(2,1)S(1)}, u32[]{:S(2)}, u32[]{:S(2)}) collective-permute-start(bf16[32,8,512]{2,1,0:T(8,128)(2,1)S(1)} %get-tuple-element.9), channel_id=1, source_target_pairs={{0,1},{1,0},{2,3},{3,2},{4,5},{5,4},{6,7},{7,6},{8,9},{9,8},{10,11... | collective-permute-start | bytes 786440 | tf_op jit(solution)/shard_map/ppermute | solution.py:96
  99.2 3.1 %collective-permute-start.3 = (bf16[32,8,512]{2,1,0:T(8,128)(2,1)S(1)}, bf16[32,8,512]{2,1,0:T(8,128)(2,1)S(1)}, u32[]{:S(2)}, u32[]{:S(2)}) collective-permute-start(bf16[32,8,512]{2,1,0:T(8,128)(2,1)S(1)} %get-tuple-element.10), channel_id=1, source_target_pairs={{0,1},{1,0},{2,3},{3,2},{4,5},{5,4},{6,7},{7,6},{8,9},{9,8},{10,11... | collective-permute-start | bytes 786440 | tf_op jit(solution)/shard_map/ppermute | solution.py:96
  102.3 2.0 %fusion.5 = f32[512,512]{1,0:T(8,128)S(1)} fusion(bf16[1024,512]{1,0:T(8,128)(2,1)} %bitcast.17, bf16[1024,1024]{1,0:T(8,128)(2,1)S(1)} %bitcast.151, s32[]{:T(128)S(6)} %mul.131), kind=kOutput, calls=%fused_computation.7 | convolution fusion | flops 536870912 | bytes 3145732 | tf_op jit(solution)/shard_map/dot_general | solution.py:87
  104.3 2.9 %collective-permute-done.4 = bf16[32,8,512]{2,1,0:T(8,128)(2,1)S(1)} collective-permute-done((bf16[32,8,512]{2,1,0:T(8,128)(2,1)S(1)}, bf16[32,8,512]{2,1,0:T(8,128)(2,1)S(1)}, u32[]{:S(2)}, u32[]{:S(2)}) %collective-permute-start.4) | collective-permute-done | bytes 262176 | tf_op jit(solution)/shard_map/ppermute | solution.py:96
  107.1 0.0 copy-done
  107.1 0.4 fusion.20
  107.5 0.0 copy-start.4
  107.5 1.9 %collective-permute-start.5 = (bf16[32,8,512]{2,1,0:T(8,128)(2,1)S(1)}, bf16[32,8,512]{2,1,0:T(8,128)(2,1)S(1)}, u32[]{:S(2)}, u32[]{:S(2)}) collective-permute-start(bf16[32,8,512]{2,1,0:T(8,128)(2,1)S(1)} %fusion.20), channel_id=1, source_target_pairs={{0,8},{8,0},{1,9},{9,1},{2,10},{10,2},{3,11},{11,3},{4,12},{12,4},... | collective-permute-start | bytes 786440 | tf_op jit(solution)/shard_map/ppermute | solution.py:111
  109.4 0.5 collective-permute-done.3
  109.9 0.4 fusion.11
  110.3 0.6 collective-permute-done.5
  110.9 0.1 add_convert_fusion.1
  111.0 19.1 %all_to_all.21 = bf16[32,8,512]{2,1,0:T(8,128)(2,1)S(1)} all-to-all(bf16[32,8,512]{2,1,0:T(8,128)(2,1)S(1)} %add_convert_fusion.1), channel_id=1, replica_groups=mesh['zh'=4,'y'=8,'c'=2,'x'=4,'zl'=2] {'zh','y'}, dimensions={0} | all-to-all | bytes 524288 | tf_op jit(solution)/shard_map/all_to_all | solution.py:22
  130.2 0.0 copy-done.4
  130.2 0.6 multiply_subtract_fusion
  (5 shorter events, 0.2 us)
Async XLA Ops:
  0.7 1.6 %copy-start.1 = (bf16[1,256,4096]{2,1,0:T(8,128)(2,1)S(1)}, bf16[1,256,4096]{2,1,0:T(8,128)(2,1)}, u32[]{:S(2)}) copy-start(bf16[1,256,4096]{2,1,0:T(8,128)(2,1)} %param.8) | copy-start | bytes 6291460
  2.3 8.2 %copy-start.3 = (f32[512,8]{0,1:T(8,128)S(1)}, f32[512,8]{0,1:T(8,128)}, u32[]{:S(2)}) copy-start(f32[512,8]{0,1:T(8,128)} %param.6) | copy-start | bytes 49156
  3.4 24.7 %collective-permute-start = (bf16[256,1024]{1,0:T(8,128)(2,1)}, bf16[256,1024]{1,0:T(8,128)(2,1)S(1)}, u32[]{:S(2)}, u32[]{:S(2)}) collective-permute-start(bf16[256,1024]{1,0:T(8,128)(2,1)} %get-tuple-element.7), channel_id=1, source_target_pairs={{0,2},{2,4},{4,6},{6,0},{1,3},{3,5},{5,7},{7,1},{8,10},{10,12},{12... | collective-permute-start | bytes 1572872 | tf_op jit(solution)/shard_map/ppermute | solution.py:55
  6.8 21.3 %collective-permute-start.1 = (bf16[256,1024]{1,0:T(8,128)(2,1)}, bf16[256,1024]{1,0:T(8,128)(2,1)S(1)}, u32[]{:S(2)}, u32[]{:S(2)}) collective-permute-start(bf16[256,1024]{1,0:T(8,128)(2,1)} %get-tuple-element.6), channel_id=1, source_target_pairs={{0,6},{2,0},{4,2},{6,4},{1,7},{3,1},{5,3},{7,5},{8,14},{10,8},{12,... | collective-permute-start | bytes 1572872 | tf_op jit(solution)/shard_map/ppermute | solution.py:55
  11.3 36.6 %all-to-all-start = ((bf16[64,8,512]{2,1,0:T(8,128)(2,1)}), bf16[64,8,512]{2,1,0:T(8,128)(2,1)}, u32[]{:S(2)}, u32[]{:S(2)}) async-start(bf16[64,8,512]{2,1,0:T(8,128)(2,1)} %broadcast_in_dim.31), calls=%async_computation | async-start | bytes 1048576 | tf_op jit(solution)/shard_map/all_to_all | solution.py:22
  30.3 23.1 %collective-permute-start.2 = (bf16[256,1024]{1,0:T(8,128)(2,1)}, bf16[256,1024]{1,0:T(8,128)(2,1)}, u32[]{:S(2)}, u32[]{:S(2)}) collective-permute-start(bf16[256,1024]{1,0:T(8,128)(2,1)} %bitcast_add_fusion.3), channel_id=1, source_target_pairs={{0,4},{2,6},{4,0},{6,2},{1,5},{3,7},{5,1},{7,3},{8,12},{10,14},{12... | collective-permute-start | bytes 1572872 | tf_op jit(solution)/shard_map/ppermute | solution.py:55
  56.0 18.6 %copy-start.2 = (bf16[1,256,512]{2,1,0:T(8,128)(2,1)S(1)}, bf16[1,256,512]{2,1,0:T(8,128)(2,1)}, u32[]{:S(2)}) copy-start(bf16[1,256,512]{2,1,0:T(8,128)(2,1)} %param.9) | copy-start | bytes 786436
  75.7 18.6 %all-to-all-start.2 = ((bf16[4,256,512]{2,1,0:T(8,128)(2,1)}), bf16[4,256,512]{2,1,0:T(8,128)(2,1)}, u32[]{:S(2)}, u32[]{:S(2)}) async-start(bf16[4,256,512]{2,1,0:T(8,128)(2,1)} %broadcast_in_dim.33), calls=%async_computation.2 | async-start | bytes 2097152 | tf_op jit(solution)/shard_map/all_to_all | solution.py:22
  96.2 10.9 %copy-start = (f32[1,512,512]{1,2,0:T(8,128)S(1)}, f32[1,512,512]{1,2,0:T(8,128)}, u32[]{:S(2)}) copy-start(f32[1,512,512]{1,2,0:T(8,128)} %copy.18) | copy-start | bytes 3145732
  96.3 10.8 %collective-permute-start.4 = (bf16[32,8,512]{2,1,0:T(8,128)(2,1)S(1)}, bf16[32,8,512]{2,1,0:T(8,128)(2,1)S(1)}, u32[]{:S(2)}, u32[]{:S(2)}) collective-permute-start(bf16[32,8,512]{2,1,0:T(8,128)(2,1)S(1)} %get-tuple-element.9), channel_id=1, source_target_pairs={{0,1},{1,0},{2,3},{3,2},{4,5},{5,4},{6,7},{7,6},{8,9},{9,8},{10,11... | collective-permute-start | bytes 786440 | tf_op jit(solution)/shard_map/ppermute | solution.py:96
  99.2 10.8 %collective-permute-start.3 = (bf16[32,8,512]{2,1,0:T(8,128)(2,1)S(1)}, bf16[32,8,512]{2,1,0:T(8,128)(2,1)S(1)}, u32[]{:S(2)}, u32[]{:S(2)}) collective-permute-start(bf16[32,8,512]{2,1,0:T(8,128)(2,1)S(1)} %get-tuple-element.10), channel_id=1, source_target_pairs={{0,1},{1,0},{2,3},{3,2},{4,5},{5,4},{6,7},{7,6},{8,9},{9,8},{10,11... | collective-permute-start | bytes 786440 | tf_op jit(solution)/shard_map/ppermute | solution.py:96
  107.5 22.7 %copy-start.4 = (f32[512,8]{0,1:T(8,128)S(1)}, f32[512,8]{0,1:T(8,128)}, u32[]{:S(2)}) copy-start(f32[512,8]{0,1:T(8,128)} %param.7) | copy-start | bytes 49156
  107.5 3.4 %collective-permute-start.5 = (bf16[32,8,512]{2,1,0:T(8,128)(2,1)S(1)}, bf16[32,8,512]{2,1,0:T(8,128)(2,1)S(1)}, u32[]{:S(2)}, u32[]{:S(2)}) collective-permute-start(bf16[32,8,512]{2,1,0:T(8,128)(2,1)S(1)} %fusion.20), channel_id=1, source_target_pairs={{0,8},{8,0},{1,9},{9,1},{2,10},{10,2},{3,11},{11,3},{4,12},{12,4},... | collective-permute-start | bytes 786440 | tf_op jit(solution)/shard_map/ppermute | solution.py:111

commit v10 on v9

--- a/solution.py
+++ b/solution.py
@@ -68,6 +68,8 @@
     half = spread(own, ("zl",) + FAR).reshape(2, far, owned, rows)
     start = [lax.all_gather(half[i], "c", axis=1).reshape(columns, rows) for i in (0, 1)]
 
+    turned = [first_moment[0].T, second_moment[0].T]
+
     def project(i):
         return lax.dot_general(
             held[:, i * rows : (i + 1) * rows], start[i], (((1,), (1,)), ((), ())),
@@ -75,15 +77,18 @@
         )
 
     partial = project(0) + project(1)
+    offsets = (at_zl * rows, (1 - at_zl) * rows, 1 - at_c)
+    first, second, offsets, partial = lax.optimization_barrier((*turned, offsets, partial))
+    at_mine, at_other, not_c = offsets
     partial = partial.astype(jnp.bfloat16).reshape(nx, count, columns)
     parts = exchange(partial, "x").astype(jnp.float32)
     projected = jnp.sum(parts, axis=0) * width ** (-0.5)
     residual = (projected - targets[0].astype(jnp.float32)).astype(jnp.bfloat16)
     residual = spread(residual, "x").reshape(nx * count, columns)
 
-    def term(zl):
+    def term(at):
         met = (nx * count, rows)
-        met = lax.dynamic_slice(held, (0, zl * rows), met, allow_negative_indices=False)
+        met = lax.dynamic_slice(held, (0, at), met, allow_negative_indices=False)
         return lax.dot_general(
             residual, met, (((0,), (0,)), ((), ())), preferred_element_type=jnp.float32
         )
@@ -91,22 +96,22 @@
     def of(a, at):
         return take(a.reshape(far, 2, owned, rows), at, 1)[:, 0]
 
-    lent = lax.optimization_barrier(term(1 - at_zl))
+    lent = lax.optimization_barrier(term(at_other))
     others = [
         lax.ppermute(of(lent, at).astype(jnp.bfloat16), "zl", swap)
-        for at in (1 - at_c, at_c)
+        for at in (not_c, at_c)
     ]
-    kept = lax.optimization_barrier(term(at_zl))
+    kept = lax.optimization_barrier(term(at_mine))
 
     def direct(at, other):
         summed = of(kept, at) + other.astype(jnp.float32)
         gradient = summed * (1.0 / (math.sqrt(width) * groups * count))
-        moment_one = beta_one * of(first_moment[0].T, at) + (1.0 - beta_one) * gradient
+        moment_one = beta_one * of(first, at) + (1.0 - beta_one) * gradient
         squared = (1.0 - beta_two) * gradient * gradient
-        moment_two = beta_two * of(second_moment[0].T, at) + squared
+        moment_two = beta_two * of(second, at) + squared
         return moment_one / (jnp.sqrt(moment_two) + adam_eps)
 
-    given = direct(1 - at_c, others[0]).astype(jnp.bfloat16)
+    given = direct(not_c, others[0]).astype(jnp.bfloat16)
     later, _ = lax.optimization_barrier((others[1], given))
     given = lax.ppermute(given, "c", swap)
     kept = lax.optimization_barrier(direct(at_c, later))

time: 132 us -> 128 us (0.970)
  blocking collectives: 41.9 us -> 58.5 us
  waiting for transfers between devices: 28.1 us -> 12.5 us
  starting transfers between devices: 39.7 us -> 35.4 us
  matrix products: 5.41 us -> 3.26 us
    all_to_all x2 -> x3, blocking collectives: 37.5 us -> 54.2 us  [exchange(): return lax.all_to_all(blocks, axes, 0, 0)]
    all_to_all x2 -> x1, waiting for transfers between devices: 24 us -> 7.4 us  [exchange(): return lax.all_to_all(blocks, axes, 0, 0)]
    all_to_all x2 -> x1, starting transfers between devices: 21 us -> 16.8 us  [exchange(): return lax.all_to_all(blocks, axes, 0, 0)]
    dot_general x2, matrix products: 3.91 us -> 1.76 us  [term(): lax.dot_general(residual, met, (((0,), (0,)), ((), ())), preferred_elemen...]
    dynamic_update_slice x3, local copies, waits for them, and re-layouts: 1.16 us -> 3.24 us  [local(): lax.dynamic_update_slice(held, block[None], at, allow_negative_indices=Fa...]
  transfers between devices with their start and end apart: 8 -> 7, of which waited for: 5 -> 4; matrix products, arithmetic and copies ran while one was open for 8% -> 10% of each run, Pallas kernels for 0% -> 0%
where the time goes in v10:
time: 128 us; the launch traced here: 127 us
  blocking collectives  58.5 us (46%)
  starting transfers between devices  35.4 us (28%)
  waiting for transfers between devices  12.5 us (10%)
  local copies, waits for them, and re-layouts  12.1 us (9%)
  other arithmetic  4.11 us (3%)
  matrix products  3.26 us (3%)
    all_to_all x3, blocking collectives, exchange(): return lax.all_to_all(blocks, axes, 0, 0)  54.2 us
    all_to_all x1, starting transfers between devices, exchange(): return lax.all_to_all(blocks, axes, 0, 0)  16.8 us
    ppermute x3, starting transfers between devices, shift(): return lax.ppermute(block, 'x', [(i, (i + d) % nx) for i in range(nx)])  10.8 us
    all_to_all x1, waiting for transfers between devices, exchange(): return lax.all_to_all(blocks, axes, 0, 0)  7.4 us
    ppermute x2, starting transfers between devices, local(): lax.ppermute(of(lent, at).astype(jnp.bfloat16), 'zl', swap)  5.97 us
    unnamed x12, local copies, waits for them, and re-layouts  5.44 us
    ppermute x2, waiting for transfers between devices, local(): lax.ppermute(of(lent, at).astype(jnp.bfloat16), 'zl', swap)  4.45 us
    all_gather x2, blocking collectives, local(): lax.all_gather(half[i], 'c', axis=1).reshape(columns, rows)  4.35 us
  transfers between devices with their start and end apart: 7, of which 4 were waited for; matrix products, arithmetic and copies ran while one was open for 10% of the time, Pallas kernels for 0%

profile of v10, /device:TPU:8, one launch (start us, length us, event | category | flops | bytes accessed | tf_op | source)
XLA Modules:
  0.0 126.9 jit_solution(8843457481649328225)
XLA Ops:
  0.7 0.0 copy-start.1
  0.7 0.3 broadcast_in_dim.27
  0.9 1.3 %copy-done.1 = bf16[1,256,4096]{2,1,0:T(8,128)(2,1)S(1)} copy-done((bf16[1,256,4096]{2,1,0:T(8,128)(2,1)S(1)}, bf16[1,256,4096]{2,1,0:T(8,128)(2,1)}, u32[]{:S(2)}) %copy-start.1) | copy-done | bytes 2097176
  2.3 0.0 copy-start.3
  2.3 1.2 dynamic-slice_bitcast_fusion
  3.4 3.4 %collective-permute-start = (bf16[256,1024]{1,0:T(8,128)(2,1)}, bf16[256,1024]{1,0:T(8,128)(2,1)}, u32[]{:S(2)}, u32[]{:S(2)}) collective-permute-start(bf16[256,1024]{1,0:T(8,128)(2,1)} %get-tuple-element.19), channel_id=1, source_target_pairs={{0,2},{2,4},{4,6},{6,0},{1,3},{3,5},{5,7},{7,1},{8,10},{10,12},{12... | collective-permute-start | bytes 1572872 | tf_op jit(solution)/shard_map/ppermute | solution.py:55
  6.8 3.7 %collective-permute-start.1 = (bf16[256,1024]{1,0:T(8,128)(2,1)}, bf16[256,1024]{1,0:T(8,128)(2,1)}, u32[]{:S(2)}, u32[]{:S(2)}) collective-permute-start(bf16[256,1024]{1,0:T(8,128)(2,1)} %get-tuple-element.18), channel_id=1, source_target_pairs={{0,6},{2,0},{4,2},{6,4},{1,7},{3,1},{5,3},{7,5},{8,14},{10,8},{12,... | collective-permute-start | bytes 1572872 | tf_op jit(solution)/shard_map/ppermute | solution.py:55
  10.5 0.0 copy-done.3
  10.5 0.8 broadcast_in_dim.31
  11.3 16.8 %all-to-all-start = ((bf16[64,8,512]{2,1,0:T(8,128)(2,1)}), bf16[64,8,512]{2,1,0:T(8,128)(2,1)}, u32[]{:S(2)}, u32[]{:S(2)}) async-start(bf16[64,8,512]{2,1,0:T(8,128)(2,1)} %broadcast_in_dim.31), calls=%async_computation | async-start | bytes 1048576 | tf_op jit(solution)/shard_map/all_to_all | solution.py:22
  28.1 1.6 %copy.13 = f32[1,512,512]{1,2,0:T(8,128)S(1)} copy(f32[1,512,512]{2,1,0:T(8,128)} %param.10) | data formatting | bytes 2097152 | tf_op args[4]
  29.7 2.5 %copy.14 = f32[1,512,512]{1,2,0:T(8,128)} copy(f32[1,512,512]{2,1,0:T(8,128)} %param.11) | data formatting | bytes 2097152 | tf_op args[5]
  32.2 0.0 collective-permute-done
  32.2 0.0 collective-permute-done.1
  32.2 2.4 %bitcast_add_fusion.3 = bf16[256,1024]{1,0:T(8,128)(2,1)} fusion(bf16[256,1024]{1,0:T(8,128)(2,1)} %collective-permute-done, bf16[256,1024]{1,0:T(8,128)(2,1)} %collective-permute-done.1, bf16[1,256,4096]{2,1,0:T(8,128)(2,1)} %param.8, s32[]{:T(128)S(6)} %mul.125), kind=kLoop, calls=%fused_computation.33 | loop fusion | flops 2097152 | bytes 2097156 | tf_op jit(solution)/shard_map/add | solution.py:59
  34.7 3.7 %collective-permute-start.2 = (bf16[256,1024]{1,0:T(8,128)(2,1)}, bf16[256,1024]{1,0:T(8,128)(2,1)}, u32[]{:S(2)}, u32[]{:S(2)}) collective-permute-start(bf16[256,1024]{1,0:T(8,128)(2,1)} %bitcast_add_fusion.3), channel_id=1, source_target_pairs={{0,4},{2,6},{4,0},{6,2},{1,5},{3,7},{5,1},{7,3},{8,12},{10,14},{12... | collective-permute-start | bytes 1572872 | tf_op jit(solution)/shard_map/ppermute | solution.py:55
  38.4 1.1 bitcast_dynamic-update-slice_fusion.2
  39.5 1.1 bitcast_dynamic-update-slice_fusion.1
  40.6 7.4 %all-to-all-done = bf16[64,8,512]{2,1,0:T(8,128)(2,1)} async-done(((bf16[64,8,512]{2,1,0:T(8,128)(2,1)}), bf16[64,8,512]{2,1,0:T(8,128)(2,1)}, u32[]{:S(2)}, u32[]{:S(2)}) %all-to-all-start) | async-done | bytes 524320 | tf_op jit(solution)/shard_map/all_to_all | solution.py:22
  48.0 1.1 fusion.27
  49.0 2.2 %all-gather.1 = bf16[32,16,512]{2,1,0:T(8,128)(2,1)S(1)} all-gather(bf16[32,8,512]{2,1,0:T(8,128)(2,1)S(1)} %get-tuple-element.24), channel_id=3, replica_groups=mesh['zh'=4,'y'=8,'c'=2,'x'=4,'zl'=2] {'c'}, dimensions={1}, use_global_device_ids=true | all-gather | bytes 786432 | tf_op jit(solution)/shard_map/all_gather | solution.py:69
  51.2 2.2 %all-gather = bf16[32,16,512]{2,1,0:T(8,128)(2,1)S(1)} all-gather(bf16[32,8,512]{2,1,0:T(8,128)(2,1)S(1)} %get-tuple-element.23), channel_id=2, replica_groups=mesh['zh'=4,'y'=8,'c'=2,'x'=4,'zl'=2] {'c'}, dimensions={1}, use_global_device_ids=true | all-gather | bytes 786432 | tf_op jit(solution)/shard_map/all_gather | solution.py:69
  53.4 0.0 collective-permute-done.2
  53.4 1.1 bitcast_dynamic-update-slice_fusion
  54.5 0.7 fusion
  55.2 0.8 convolution_add_fusion
  56.0 0.0 copy-start.2
  56.0 18.4 %all_to_all.20 = bf16[4,256,512]{2,1,0:T(8,128)(2,1)S(1)} all-to-all(bf16[4,256,512]{2,1,0:T(8,128)(2,1)S(1)} %bitcast.154), channel_id=1, replica_groups=mesh['zh'=4,'y'=8,'c'=2,'x'=4,'zl'=2] {'x'}, dimensions={0} | all-to-all | bytes 2097152 | tf_op jit(solution)/shard_map/all_to_all | solution.py:22
  74.4 0.1 convert_reduce_fusion
  74.6 0.0 copy-done.2
  74.6 0.1 fusion.21
  74.7 0.1 broadcast_in_dim.33
  74.7 16.6 %all_to_all.21 = bf16[4,256,512]{2,1,0:T(8,128)(2,1)S(1)} all-to-all(bf16[4,256,512]{2,1,0:T(8,128)(2,1)S(1)} %broadcast_in_dim.33), channel_id=1, replica_groups=mesh['zh'=4,'y'=8,'c'=2,'x'=4,'zl'=2] {'x'}, dimensions={0} | all-to-all | bytes 2097152 | tf_op jit(solution)/shard_map/all_to_all | solution.py:22
  91.4 0.9 fusion.3
  92.3 0.0 copy-start
  92.3 2.9 %collective-permute-start.4 = (bf16[32,8,512]{2,1,0:T(8,128)(2,1)S(1)}, bf16[32,8,512]{2,1,0:T(8,128)(2,1)S(1)}, u32[]{:S(2)}, u32[]{:S(2)}) collective-permute-start(bf16[32,8,512]{2,1,0:T(8,128)(2,1)S(1)} %get-tuple-element.21), channel_id=1, source_target_pairs={{0,1},{1,0},{2,3},{3,2},{4,5},{5,4},{6,7},{7,6},{8,9},{9,8},{10,11... | collective-permute-start | bytes 786440 | tf_op jit(solution)/shard_map/ppermute | solution.py:101
  95.2 3.1 %collective-permute-start.3 = (bf16[32,8,512]{2,1,0:T(8,128)(2,1)S(1)}, bf16[32,8,512]{2,1,0:T(8,128)(2,1)S(1)}, u32[]{:S(2)}, u32[]{:S(2)}) collective-permute-start(bf16[32,8,512]{2,1,0:T(8,128)(2,1)S(1)} %get-tuple-element.22), channel_id=1, source_target_pairs={{0,1},{1,0},{2,3},{3,2},{4,5},{5,4},{6,7},{7,6},{8,9},{9,8},{10,11... | collective-permute-start | bytes 786440 | tf_op jit(solution)/shard_map/ppermute | solution.py:101
  98.3 0.9 fusion.5
  99.2 3.9 %collective-permute-done.4 = bf16[32,8,512]{2,1,0:T(8,128)(2,1)S(1)} collective-permute-done((bf16[32,8,512]{2,1,0:T(8,128)(2,1)S(1)}, bf16[32,8,512]{2,1,0:T(8,128)(2,1)S(1)}, u32[]{:S(2)}, u32[]{:S(2)}) %collective-permute-start.4) | collective-permute-done | bytes 262176 | tf_op jit(solution)/shard_map/ppermute | solution.py:101
  103.2 0.0 copy-done
  103.2 0.4 fusion.20
  103.5 0.0 copy-start.4
  103.5 1.9 %collective-permute-start.5 = (bf16[32,8,512]{2,1,0:T(8,128)(2,1)S(1)}, bf16[32,8,512]{2,1,0:T(8,128)(2,1)S(1)}, u32[]{:S(2)}, u32[]{:S(2)}) collective-permute-start(bf16[32,8,512]{2,1,0:T(8,128)(2,1)S(1)} %fusion.20), channel_id=1, source_target_pairs={{0,8},{8,0},{1,9},{9,1},{2,10},{10,2},{3,11},{11,3},{4,12},{12,4},... | collective-permute-start | bytes 786440 | tf_op jit(solution)/shard_map/ppermute | solution.py:116
  105.5 0.5 collective-permute-done.3
  106.0 0.4 fusion.11
  106.3 0.6 collective-permute-done.5
  107.0 0.1 add_convert_fusion
  107.0 19.1 %all_to_all.22 = bf16[32,8,512]{2,1,0:T(8,128)(2,1)S(1)} all-to-all(bf16[32,8,512]{2,1,0:T(8,128)(2,1)S(1)} %add_convert_fusion), channel_id=1, replica_groups=mesh['zh'=4,'y'=8,'c'=2,'x'=4,'zl'=2] {'zh','y'}, dimensions={0} | all-to-all | bytes 524288 | tf_op jit(solution)/shard_map/all_to_all | solution.py:22
  126.2 0.0 copy-done.4
  126.2 0.6 multiply_subtract_fusion
  (3 shorter events, 0.1 us)
Async XLA Ops:
  0.7 1.6 %copy-start.1 = (bf16[1,256,4096]{2,1,0:T(8,128)(2,1)S(1)}, bf16[1,256,4096]{2,1,0:T(8,128)(2,1)}, u32[]{:S(2)}) copy-start(bf16[1,256,4096]{2,1,0:T(8,128)(2,1)} %param.8) | copy-start | bytes 6291460
  2.3 8.2 %copy-start.3 = (f32[512,8]{0,1:T(8,128)S(1)}, f32[512,8]{0,1:T(8,128)}, u32[]{:S(2)}) copy-start(f32[512,8]{0,1:T(8,128)} %param.6) | copy-start | bytes 49156
  3.4 28.8 %collective-permute-start = (bf16[256,1024]{1,0:T(8,128)(2,1)}, bf16[256,1024]{1,0:T(8,128)(2,1)}, u32[]{:S(2)}, u32[]{:S(2)}) collective-permute-start(bf16[256,1024]{1,0:T(8,128)(2,1)} %get-tuple-element.19), channel_id=1, source_target_pairs={{0,2},{2,4},{4,6},{6,0},{1,3},{3,5},{5,7},{7,1},{8,10},{10,12},{12... | collective-permute-start | bytes 1572872 | tf_op jit(solution)/shard_map/ppermute | solution.py:55
  6.8 25.4 %collective-permute-start.1 = (bf16[256,1024]{1,0:T(8,128)(2,1)}, bf16[256,1024]{1,0:T(8,128)(2,1)}, u32[]{:S(2)}, u32[]{:S(2)}) collective-permute-start(bf16[256,1024]{1,0:T(8,128)(2,1)} %get-tuple-element.18), channel_id=1, source_target_pairs={{0,6},{2,0},{4,2},{6,4},{1,7},{3,1},{5,3},{7,5},{8,14},{10,8},{12,... | collective-permute-start | bytes 1572872 | tf_op jit(solution)/shard_map/ppermute | solution.py:55
  11.3 36.6 %all-to-all-start = ((bf16[64,8,512]{2,1,0:T(8,128)(2,1)}), bf16[64,8,512]{2,1,0:T(8,128)(2,1)}, u32[]{:S(2)}, u32[]{:S(2)}) async-start(bf16[64,8,512]{2,1,0:T(8,128)(2,1)} %broadcast_in_dim.31), calls=%async_computation | async-start | bytes 1048576 | tf_op jit(solution)/shard_map/all_to_all | solution.py:22
  34.7 18.7 %collective-permute-start.2 = (bf16[256,1024]{1,0:T(8,128)(2,1)}, bf16[256,1024]{1,0:T(8,128)(2,1)}, u32[]{:S(2)}, u32[]{:S(2)}) collective-permute-start(bf16[256,1024]{1,0:T(8,128)(2,1)} %bitcast_add_fusion.3), channel_id=1, source_target_pairs={{0,4},{2,6},{4,0},{6,2},{1,5},{3,7},{5,1},{7,3},{8,12},{10,14},{12... | collective-permute-start | bytes 1572872 | tf_op jit(solution)/shard_map/ppermute | solution.py:55
  56.0 18.6 %copy-start.2 = (bf16[1,256,512]{2,1,0:T(8,128)(2,1)S(1)}, bf16[1,256,512]{2,1,0:T(8,128)(2,1)}, u32[]{:S(2)}) copy-start(bf16[1,256,512]{2,1,0:T(8,128)(2,1)} %param.9) | copy-start | bytes 786436
  92.3 10.9 %copy-start = (f32[1,512,512]{1,2,0:T(8,128)S(1)}, f32[1,512,512]{1,2,0:T(8,128)}, u32[]{:S(2)}) copy-start(f32[1,512,512]{1,2,0:T(8,128)} %copy.14) | copy-start | bytes 3145732
  92.3 10.8 %collective-permute-start.4 = (bf16[32,8,512]{2,1,0:T(8,128)(2,1)S(1)}, bf16[32,8,512]{2,1,0:T(8,128)(2,1)S(1)}, u32[]{:S(2)}, u32[]{:S(2)}) collective-permute-start(bf16[32,8,512]{2,1,0:T(8,128)(2,1)S(1)} %get-tuple-element.21), channel_id=1, source_target_pairs={{0,1},{1,0},{2,3},{3,2},{4,5},{5,4},{6,7},{7,6},{8,9},{9,8},{10,11... | collective-permute-start | bytes 786440 | tf_op jit(solution)/shard_map/ppermute | solution.py:101
  95.2 10.8 %collective-permute-start.3 = (bf16[32,8,512]{2,1,0:T(8,128)(2,1)S(1)}, bf16[32,8,512]{2,1,0:T(8,128)(2,1)S(1)}, u32[]{:S(2)}, u32[]{:S(2)}) collective-permute-start(bf16[32,8,512]{2,1,0:T(8,128)(2,1)S(1)} %get-tuple-element.22), channel_id=1, source_target_pairs={{0,1},{1,0},{2,3},{3,2},{4,5},{5,4},{6,7},{7,6},{8,9},{9,8},{10,11... | collective-permute-start | bytes 786440 | tf_op jit(solution)/shard_map/ppermute | solution.py:101
  103.5 22.7 %copy-start.4 = (f32[512,8]{0,1:T(8,128)S(1)}, f32[512,8]{0,1:T(8,128)}, u32[]{:S(2)}) copy-start(f32[512,8]{0,1:T(8,128)} %param.7) | copy-start | bytes 49156
  103.5 3.4 %collective-permute-start.5 = (bf16[32,8,512]{2,1,0:T(8,128)(2,1)S(1)}, bf16[32,8,512]{2,1,0:T(8,128)(2,1)S(1)}, u32[]{:S(2)}, u32[]{:S(2)}) collective-permute-start(bf16[32,8,512]{2,1,0:T(8,128)(2,1)S(1)} %fusion.20), channel_id=1, source_target_pairs={{0,8},{8,0},{1,9},{9,1},{2,10},{10,2},{3,11},{11,3},{4,12},{12,4},... | collective-permute-start | bytes 786440 | tf_op jit(solution)/shard_map/ppermute | solution.py:116

commit v11 on v10

--- a/solution.py
+++ b/solution.py
@@ -56,7 +56,8 @@
 
     from_left = shift(cut(1), 1)
     from_right = shift(cut(3), 3)
-    across = shift(cut(2) + 0 * (from_left + from_right), 2)
+    from_left, from_right = lax.optimization_barrier((from_left, from_right))
+    across = shift(cut(2) + 0 * from_right, 2)
 
     held = jnp.zeros((nx, count, 2 * rows), tok.dtype)
     for d, block in ((0, cut(0)), (3, from_left), (1, from_right), (2, across)):

time: 128 us -> 128 us (level)
  transfers between devices with their start and end apart: 7 -> 7, of which waited for: 4 -> 4; matrix products, arithmetic and copies ran while one was open for 10% -> 9% of each run, Pallas kernels for 0% -> 0%
where the time goes in v11:
time: 128 us; the launch traced here: 127 us
  blocking collectives  58.5 us (46%)
  starting transfers between devices  35.4 us (28%)
  waiting for transfers between devices  12.7 us (10%)
  local copies, waits for them, and re-layouts  12.1 us (9%)
  other arithmetic  3.88 us (3%)
  matrix products  3.26 us (3%)
    all_to_all x3, blocking collectives, exchange(): return lax.all_to_all(blocks, axes, 0, 0)  54.2 us
    all_to_all x1, starting transfers between devices, exchange(): return lax.all_to_all(blocks, axes, 0, 0)  16.8 us
    ppermute x3, starting transfers between devices, shift(): return lax.ppermute(block, 'x', [(i, (i + d) % nx) for i in range(nx)])  10.8 us
    all_to_all x1, waiting for transfers between devices, exchange(): return lax.all_to_all(blocks, axes, 0, 0)  7.63 us
    ppermute x2, starting transfers between devices, local(): lax.ppermute(of(lent, at).astype(jnp.bfloat16), 'zl', swap)  5.97 us
    unnamed x12, local copies, waits for them, and re-layouts  5.44 us
    ppermute x2, waiting for transfers between devices, local(): lax.ppermute(of(lent, at).astype(jnp.bfloat16), 'zl', swap)  4.45 us
    all_gather x2, blocking collectives, local(): lax.all_gather(half[i], 'c', axis=1).reshape(columns, rows)  4.35 us
  transfers between devices with their start and end apart: 7, of which 4 were waited for; matrix products, arithmetic and copies ran while one was open for 9% of the time, Pallas kernels for 0%

profile of v11, /device:TPU:8, one launch (start us, length us, event | category | flops | bytes accessed | tf_op | source)
XLA Modules:
  0.0 126.9 jit_solution(1706732208946758555)
XLA Ops:
  0.7 0.0 copy-start.1
  0.7 0.3 broadcast_in_dim.27
  0.9 1.3 %copy-done.1 = bf16[1,256,4096]{2,1,0:T(8,128)(2,1)S(1)} copy-done((bf16[1,256,4096]{2,1,0:T(8,128)(2,1)S(1)}, bf16[1,256,4096]{2,1,0:T(8,128)(2,1)}, u32[]{:S(2)}) %copy-start.1) | copy-done | bytes 2097176
  2.3 0.0 copy-start.3
  2.3 1.2 dynamic-slice_bitcast_fusion
  3.4 3.4 %collective-permute-start = (bf16[256,1024]{1,0:T(8,128)(2,1)}, bf16[256,1024]{1,0:T(8,128)(2,1)}, u32[]{:S(2)}, u32[]{:S(2)}) collective-permute-start(bf16[256,1024]{1,0:T(8,128)(2,1)} %get-tuple-element.23), channel_id=1, source_target_pairs={{0,2},{2,4},{4,6},{6,0},{1,3},{3,5},{5,7},{7,1},{8,10},{10,12},{12... | collective-permute-start | bytes 1572872 | tf_op jit(solution)/shard_map/ppermute | solution.py:55
  6.8 3.7 %collective-permute-start.1 = (bf16[256,1024]{1,0:T(8,128)(2,1)}, bf16[256,1024]{1,0:T(8,128)(2,1)}, u32[]{:S(2)}, u32[]{:S(2)}) collective-permute-start(bf16[256,1024]{1,0:T(8,128)(2,1)} %get-tuple-element.22), channel_id=1, source_target_pairs={{0,6},{2,0},{4,2},{6,4},{1,7},{3,1},{5,3},{7,5},{8,14},{10,8},{12,... | collective-permute-start | bytes 1572872 | tf_op jit(solution)/shard_map/ppermute | solution.py:55
  10.5 0.0 copy-done.3
  10.5 0.8 broadcast_in_dim.31
  11.3 16.8 %all-to-all-start = ((bf16[64,8,512]{2,1,0:T(8,128)(2,1)}), bf16[64,8,512]{2,1,0:T(8,128)(2,1)}, u32[]{:S(2)}, u32[]{:S(2)}) async-start(bf16[64,8,512]{2,1,0:T(8,128)(2,1)} %broadcast_in_dim.31), calls=%async_computation | async-start | bytes 1048576 | tf_op jit(solution)/shard_map/all_to_all | solution.py:22
  28.1 1.6 %copy.13 = f32[1,512,512]{1,2,0:T(8,128)S(1)} copy(f32[1,512,512]{2,1,0:T(8,128)} %param.10) | data formatting | bytes 2097152 | tf_op args[4]
  29.7 2.5 %copy.14 = f32[1,512,512]{1,2,0:T(8,128)} copy(f32[1,512,512]{2,1,0:T(8,128)} %param.11) | data formatting | bytes 2097152 | tf_op args[5]
  32.2 0.0 collective-permute-done
  32.2 0.0 collective-permute-done.1
  32.2 2.2 %bitcast_add_fusion.3 = bf16[256,1024]{1,0:T(8,128)(2,1)} fusion(bf16[256,1024]{1,0:T(8,128)(2,1)} %collective-permute-done.1, bf16[1,256,4096]{2,1,0:T(8,128)(2,1)} %param.8, s32[]{:T(128)S(6)} %mul.125), kind=kLoop, calls=%fused_computation.33 | loop fusion | flops 1572864 | bytes 1572868 | tf_op jit(solution)/shard_map/add | solution.py:60
  34.5 3.7 %collective-permute-start.2 = (bf16[256,1024]{1,0:T(8,128)(2,1)}, bf16[256,1024]{1,0:T(8,128)(2,1)}, u32[]{:S(2)}, u32[]{:S(2)}) collective-permute-start(bf16[256,1024]{1,0:T(8,128)(2,1)} %bitcast_add_fusion.3), channel_id=1, source_target_pairs={{0,4},{2,6},{4,0},{6,2},{1,5},{3,7},{5,1},{7,3},{8,12},{10,14},{12... | collective-permute-start | bytes 1572872 | tf_op jit(solution)/shard_map/ppermute | solution.py:55
  38.2 1.1 bitcast_dynamic-update-slice_fusion.2
  39.3 1.1 bitcast_dynamic-update-slice_fusion.1
  40.3 7.6 %all-to-all-done = bf16[64,8,512]{2,1,0:T(8,128)(2,1)} async-done(((bf16[64,8,512]{2,1,0:T(8,128)(2,1)}), bf16[64,8,512]{2,1,0:T(8,128)(2,1)}, u32[]{:S(2)}, u32[]{:S(2)}) %all-to-all-start) | async-done | bytes 524320 | tf_op jit(solution)/shard_map/all_to_all | solution.py:22
  48.0 1.1 fusion.27
  49.0 2.2 %all-gather.1 = bf16[32,16,512]{2,1,0:T(8,128)(2,1)S(1)} all-gather(bf16[32,8,512]{2,1,0:T(8,128)(2,1)S(1)} %get-tuple-element.28), channel_id=3, replica_groups=mesh['zh'=4,'y'=8,'c'=2,'x'=4,'zl'=2] {'c'}, dimensions={1}, use_global_device_ids=true | all-gather | bytes 786432 | tf_op jit(solution)/shard_map/all_gather | solution.py:70
  51.2 2.2 %all-gather = bf16[32,16,512]{2,1,0:T(8,128)(2,1)S(1)} all-gather(bf16[32,8,512]{2,1,0:T(8,128)(2,1)S(1)} %get-tuple-element.27), channel_id=2, replica_groups=mesh['zh'=4,'y'=8,'c'=2,'x'=4,'zl'=2] {'c'}, dimensions={1}, use_global_device_ids=true | all-gather | bytes 786432 | tf_op jit(solution)/shard_map/all_gather | solution.py:70
  53.4 0.0 collective-permute-done.2
  53.4 1.1 bitcast_dynamic-update-slice_fusion
  54.5 0.7 fusion
  55.2 0.8 convolution_add_fusion
  56.0 0.0 copy-start.2
  56.0 18.4 %all_to_all.20 = bf16[4,256,512]{2,1,0:T(8,128)(2,1)S(1)} all-to-all(bf16[4,256,512]{2,1,0:T(8,128)(2,1)S(1)} %bitcast.154), channel_id=1, replica_groups=mesh['zh'=4,'y'=8,'c'=2,'x'=4,'zl'=2] {'x'}, dimensions={0} | all-to-all | bytes 2097152 | tf_op jit(solution)/shard_map/all_to_all | solution.py:22
  74.4 0.1 convert_reduce_fusion
  74.6 0.0 copy-done.2
  74.6 0.1 fusion.21
  74.7 0.1 broadcast_in_dim.33
  74.7 16.6 %all_to_all.21 = bf16[4,256,512]{2,1,0:T(8,128)(2,1)S(1)} all-to-all(bf16[4,256,512]{2,1,0:T(8,128)(2,1)S(1)} %broadcast_in_dim.33), channel_id=1, replica_groups=mesh['zh'=4,'y'=8,'c'=2,'x'=4,'zl'=2] {'x'}, dimensions={0} | all-to-all | bytes 2097152 | tf_op jit(solution)/shard_map/all_to_all | solution.py:22
  91.4 0.9 fusion.3
  92.3 0.0 copy-start
  92.3 2.9 %collective-permute-start.4 = (bf16[32,8,512]{2,1,0:T(8,128)(2,1)S(1)}, bf16[32,8,512]{2,1,0:T(8,128)(2,1)S(1)}, u32[]{:S(2)}, u32[]{:S(2)}) collective-permute-start(bf16[32,8,512]{2,1,0:T(8,128)(2,1)S(1)} %get-tuple-element.25), channel_id=1, source_target_pairs={{0,1},{1,0},{2,3},{3,2},{4,5},{5,4},{6,7},{7,6},{8,9},{9,8},{10,11... | collective-permute-start | bytes 786440 | tf_op jit(solution)/shard_map/ppermute | solution.py:102
  95.2 3.1 %collective-permute-start.3 = (bf16[32,8,512]{2,1,0:T(8,128)(2,1)S(1)}, bf16[32,8,512]{2,1,0:T(8,128)(2,1)S(1)}, u32[]{:S(2)}, u32[]{:S(2)}) collective-permute-start(bf16[32,8,512]{2,1,0:T(8,128)(2,1)S(1)} %get-tuple-element.26), channel_id=1, source_target_pairs={{0,1},{1,0},{2,3},{3,2},{4,5},{5,4},{6,7},{7,6},{8,9},{9,8},{10,11... | collective-permute-start | bytes 786440 | tf_op jit(solution)/shard_map/ppermute | solution.py:102
  98.3 0.9 fusion.5
  99.2 3.9 %collective-permute-done.4 = bf16[32,8,512]{2,1,0:T(8,128)(2,1)S(1)} collective-permute-done((bf16[32,8,512]{2,1,0:T(8,128)(2,1)S(1)}, bf16[32,8,512]{2,1,0:T(8,128)(2,1)S(1)}, u32[]{:S(2)}, u32[]{:S(2)}) %collective-permute-start.4) | collective-permute-done | bytes 262176 | tf_op jit(solution)/shard_map/ppermute | solution.py:102
  103.2 0.0 copy-done
  103.2 0.4 fusion.20
  103.5 0.0 copy-start.4
  103.5 1.9 %collective-permute-start.5 = (bf16[32,8,512]{2,1,0:T(8,128)(2,1)S(1)}, bf16[32,8,512]{2,1,0:T(8,128)(2,1)S(1)}, u32[]{:S(2)}, u32[]{:S(2)}) collective-permute-start(bf16[32,8,512]{2,1,0:T(8,128)(2,1)S(1)} %fusion.20), channel_id=1, source_target_pairs={{0,8},{8,0},{1,9},{9,1},{2,10},{10,2},{3,11},{11,3},{4,12},{12,4},... | collective-permute-start | bytes 786440 | tf_op jit(solution)/shard_map/ppermute | solution.py:117
  105.5 0.5 collective-permute-done.3
  106.0 0.4 fusion.11
  106.3 0.6 collective-permute-done.5
  107.0 0.1 add_convert_fusion
  107.0 19.1 %all_to_all.22 = bf16[32,8,512]{2,1,0:T(8,128)(2,1)S(1)} all-to-all(bf16[32,8,512]{2,1,0:T(8,128)(2,1)S(1)} %add_convert_fusion), channel_id=1, replica_groups=mesh['zh'=4,'y'=8,'c'=2,'x'=4,'zl'=2] {'zh','y'}, dimensions={0} | all-to-all | bytes 524288 | tf_op jit(solution)/shard_map/all_to_all | solution.py:22
  126.2 0.0 copy-done.4
  126.2 0.6 multiply_subtract_fusion
  (3 shorter events, 0.1 us)
Async XLA Ops:
  0.7 1.6 %copy-start.1 = (bf16[1,256,4096]{2,1,0:T(8,128)(2,1)S(1)}, bf16[1,256,4096]{2,1,0:T(8,128)(2,1)}, u32[]{:S(2)}) copy-start(bf16[1,256,4096]{2,1,0:T(8,128)(2,1)} %param.8) | copy-start | bytes 6291460
  2.3 8.2 %copy-start.3 = (f32[512,8]{0,1:T(8,128)S(1)}, f32[512,8]{0,1:T(8,128)}, u32[]{:S(2)}) copy-start(f32[512,8]{0,1:T(8,128)} %param.6) | copy-start | bytes 49156
  3.4 28.8 %collective-permute-start = (bf16[256,1024]{1,0:T(8,128)(2,1)}, bf16[256,1024]{1,0:T(8,128)(2,1)}, u32[]{:S(2)}, u32[]{:S(2)}) collective-permute-start(bf16[256,1024]{1,0:T(8,128)(2,1)} %get-tuple-element.23), channel_id=1, source_target_pairs={{0,2},{2,4},{4,6},{6,0},{1,3},{3,5},{5,7},{7,1},{8,10},{10,12},{12... | collective-permute-start | bytes 1572872 | tf_op jit(solution)/shard_map/ppermute | solution.py:55
  6.8 25.4 %collective-permute-start.1 = (bf16[256,1024]{1,0:T(8,128)(2,1)}, bf16[256,1024]{1,0:T(8,128)(2,1)}, u32[]{:S(2)}, u32[]{:S(2)}) collective-permute-start(bf16[256,1024]{1,0:T(8,128)(2,1)} %get-tuple-element.22), channel_id=1, source_target_pairs={{0,6},{2,0},{4,2},{6,4},{1,7},{3,1},{5,3},{7,5},{8,14},{10,8},{12,... | collective-permute-start | bytes 1572872 | tf_op jit(solution)/shard_map/ppermute | solution.py:55
  11.3 36.6 %all-to-all-start = ((bf16[64,8,512]{2,1,0:T(8,128)(2,1)}), bf16[64,8,512]{2,1,0:T(8,128)(2,1)}, u32[]{:S(2)}, u32[]{:S(2)}) async-start(bf16[64,8,512]{2,1,0:T(8,128)(2,1)} %broadcast_in_dim.31), calls=%async_computation | async-start | bytes 1048576 | tf_op jit(solution)/shard_map/all_to_all | solution.py:22
  34.5 18.9 %collective-permute-start.2 = (bf16[256,1024]{1,0:T(8,128)(2,1)}, bf16[256,1024]{1,0:T(8,128)(2,1)}, u32[]{:S(2)}, u32[]{:S(2)}) collective-permute-start(bf16[256,1024]{1,0:T(8,128)(2,1)} %bitcast_add_fusion.3), channel_id=1, source_target_pairs={{0,4},{2,6},{4,0},{6,2},{1,5},{3,7},{5,1},{7,3},{8,12},{10,14},{12... | collective-permute-start | bytes 1572872 | tf_op jit(solution)/shard_map/ppermute | solution.py:55
  56.0 18.6 %copy-start.2 = (bf16[1,256,512]{2,1,0:T(8,128)(2,1)S(1)}, bf16[1,256,512]{2,1,0:T(8,128)(2,1)}, u32[]{:S(2)}) copy-start(bf16[1,256,512]{2,1,0:T(8,128)(2,1)} %param.9) | copy-start | bytes 786436
  92.3 10.9 %copy-start = (f32[1,512,512]{1,2,0:T(8,128)S(1)}, f32[1,512,512]{1,2,0:T(8,128)}, u32[]{:S(2)}) copy-start(f32[1,512,512]{1,2,0:T(8,128)} %copy.14) | copy-start | bytes 3145732
  92.3 10.8 %collective-permute-start.4 = (bf16[32,8,512]{2,1,0:T(8,128)(2,1)S(1)}, bf16[32,8,512]{2,1,0:T(8,128)(2,1)S(1)}, u32[]{:S(2)}, u32[]{:S(2)}) collective-permute-start(bf16[32,8,512]{2,1,0:T(8,128)(2,1)S(1)} %get-tuple-element.25), channel_id=1, source_target_pairs={{0,1},{1,0},{2,3},{3,2},{4,5},{5,4},{6,7},{7,6},{8,9},{9,8},{10,11... | collective-permute-start | bytes 786440 | tf_op jit(solution)/shard_map/ppermute | solution.py:102
  95.2 10.8 %collective-permute-start.3 = (bf16[32,8,512]{2,1,0:T(8,128)(2,1)S(1)}, bf16[32,8,512]{2,1,0:T(8,128)(2,1)S(1)}, u32[]{:S(2)}, u32[]{:S(2)}) collective-permute-start(bf16[32,8,512]{2,1,0:T(8,128)(2,1)S(1)} %get-tuple-element.26), channel_id=1, source_target_pairs={{0,1},{1,0},{2,3},{3,2},{4,5},{5,4},{6,7},{7,6},{8,9},{9,8},{10,11... | collective-permute-start | bytes 786440 | tf_op jit(solution)/shard_map/ppermute | solution.py:102
  103.5 22.7 %copy-start.4 = (f32[512,8]{0,1:T(8,128)S(1)}, f32[512,8]{0,1:T(8,128)}, u32[]{:S(2)}) copy-start(f32[512,8]{0,1:T(8,128)} %param.7) | copy-start | bytes 49156
  103.5 3.4 %collective-permute-start.5 = (bf16[32,8,512]{2,1,0:T(8,128)(2,1)S(1)}, bf16[32,8,512]{2,1,0:T(8,128)(2,1)S(1)}, u32[]{:S(2)}, u32[]{:S(2)}) collective-permute-start(bf16[32,8,512]{2,1,0:T(8,128)(2,1)S(1)} %fusion.20), channel_id=1, source_target_pairs={{0,8},{8,0},{1,9},{9,1},{2,10},{10,2},{3,11},{11,3},{4,12},{12,4},... | collective-permute-start | bytes 786440 | tf_op jit(solution)/shard_map/ppermute | solution.py:117

commit v12 on v10

--- a/solution.py
+++ b/solution.py
@@ -66,7 +66,13 @@
 
     own = anchor.astype(jnp.bfloat16).T
     half = spread(own, ("zl",) + FAR).reshape(2, far, owned, rows)
-    start = [lax.all_gather(half[i], "c", axis=1).reshape(columns, rows) for i in (0, 1)]
+    other = lax.ppermute(half[0], "c", swap)
+    first = jnp.where(at_c == 0, half[0], other)
+    second = jnp.where(at_c == 0, other, half[0])
+    start = [
+        jnp.stack([first, second], 1).reshape(columns, rows),
+        lax.all_gather(half[1], "c", axis=1).reshape(columns, rows),
+    ]
 
     turned = [first_moment[0].T, second_moment[0].T]
 

time: 128 us -> 133 us (1.039)
  starting transfers between devices: 35.4 us -> 37.3 us
    all_to_all x3, blocking collectives: 54.2 us -> 56.7 us  [exchange(): return lax.all_to_all(blocks, axes, 0, 0)]
    all_gather x2 -> x1, blocking collectives: 4.35 us -> 2.31 us  [local(): lax.all_gather(half[1], 'c', axis=1).reshape(columns, rows)]
    ppermute x0 -> x1, starting transfers between devices: none -> 1.92 us  [local(): other = lax.ppermute(half[0], 'c', swap)]
    unnamed x12 -> x16, local copies, waits for them, and re-layouts: 5.44 us -> 5.45 us
  transfers between devices with their start and end apart: 7 -> 8, of which waited for: 4 -> 4; matrix products, arithmetic and copies ran while one was open for 10% -> 10% of each run, Pallas kernels for 0% -> 0%
where the time goes in v12:
time: 133 us; the launch traced here: 132 us
  blocking collectives  59 us (44%)
  starting transfers between devices  37.3 us (28%)
  waiting for transfers between devices  13.7 us (10%)
  local copies, waits for them, and re-layouts  12 us (9%)
  other arithmetic  5.31 us (4%)
  matrix products  3.26 us (2%)
    all_to_all x3, blocking collectives, exchange(): return lax.all_to_all(blocks, axes, 0, 0)  56.7 us
    all_to_all x1, starting transfers between devices, exchange(): return lax.all_to_all(blocks, axes, 0, 0)  16.8 us
    ppermute x3, starting transfers between devices, shift(): return lax.ppermute(block, 'x', [(i, (i + d) % nx) for i in range(nx)])  10.8 us
    all_to_all x1, waiting for transfers between devices, exchange(): return lax.all_to_all(blocks, axes, 0, 0)  8.38 us
    ppermute x2, starting transfers between devices, local(): lax.ppermute(of(lent, at).astype(jnp.bfloat16), 'zl', swap)  5.97 us
    unnamed x16, local copies, waits for them, and re-layouts  5.45 us
    ppermute x2, waiting for transfers between devices, local(): lax.ppermute(of(lent, at).astype(jnp.bfloat16), 'zl', swap)  4.71 us
    dynamic_update_slice x3, local copies, waits for them, and re-layouts, local(): lax.dynamic_update_slice(held, block[None], at, allow_negative_indices=Fa...  3.24 us
  transfers between devices with their start and end apart: 8, of which 4 were waited for; matrix products, arithmetic and copies ran while one was open for 10% of the time, Pallas kernels for 0%

profile of v12, /device:TPU:8, one launch (start us, length us, event | category | flops | bytes accessed | tf_op | source)
XLA Modules:
  0.0 131.6 jit_solution(842575323961849938)
XLA Ops:
  0.7 0.0 copy-start.3
  0.7 0.3 broadcast_in_dim.27
  0.9 1.3 %copy-done.3 = bf16[1,256,4096]{2,1,0:T(8,128)(2,1)S(1)} copy-done((bf16[1,256,4096]{2,1,0:T(8,128)(2,1)S(1)}, bf16[1,256,4096]{2,1,0:T(8,128)(2,1)}, u32[]{:S(2)}) %copy-start.3) | copy-done | bytes 2097176
  2.3 0.0 copy-start.5
  2.3 1.1 dynamic-slice_bitcast_fusion
  3.4 3.4 %collective-permute-start = (bf16[256,1024]{1,0:T(8,128)(2,1)}, bf16[256,1024]{1,0:T(8,128)(2,1)S(1)}, u32[]{:S(2)}, u32[]{:S(2)}) collective-permute-start(bf16[256,1024]{1,0:T(8,128)(2,1)} %get-tuple-element.19), channel_id=1, source_target_pairs={{0,2},{2,4},{4,6},{6,0},{1,3},{3,5},{5,7},{7,1},{8,10},{10,12},{12... | collective-permute-start | bytes 1572872 | tf_op jit(solution)/shard_map/ppermute | solution.py:55
  6.8 3.7 %collective-permute-start.1 = (bf16[256,1024]{1,0:T(8,128)(2,1)}, bf16[256,1024]{1,0:T(8,128)(2,1)S(1)}, u32[]{:S(2)}, u32[]{:S(2)}) collective-permute-start(bf16[256,1024]{1,0:T(8,128)(2,1)} %get-tuple-element.18), channel_id=1, source_target_pairs={{0,6},{2,0},{4,2},{6,4},{1,7},{3,1},{5,3},{7,5},{8,14},{10,8},{12,... | collective-permute-start | bytes 1572872 | tf_op jit(solution)/shard_map/ppermute | solution.py:55
  10.5 0.0 copy-done.5
  10.5 0.8 broadcast_in_dim.31
  11.3 16.8 %all-to-all-start = ((bf16[64,8,512]{2,1,0:T(8,128)(2,1)}), bf16[64,8,512]{2,1,0:T(8,128)(2,1)}, u32[]{:S(2)}, u32[]{:S(2)}) async-start(bf16[64,8,512]{2,1,0:T(8,128)(2,1)} %broadcast_in_dim.31), calls=%async_computation | async-start | bytes 1048576 | tf_op jit(solution)/shard_map/all_to_all | solution.py:22
  28.1 0.0 collective-permute-done
  28.1 0.0 copy-start.2
  28.1 0.0 collective-permute-done.1
  28.1 0.0 copy-start.1
  28.2 2.5 %bitcast_add_fusion.3 = bf16[256,1024]{1,0:T(8,128)(2,1)} fusion(bf16[256,1024]{1,0:T(8,128)(2,1)S(1)} %collective-permute-done, bf16[256,1024]{1,0:T(8,128)(2,1)S(1)} %collective-permute-done.1, bf16[1,256,4096]{2,1,0:T(8,128)(2,1)} %param.8, s32[]{:T(128)S(6)} %mul.125), kind=kLoop, calls=%fused_computation.34 | loop fusion | flops 2097152 | bytes 2097156 | tf_op jit(solution)/shard_map/add | solution.py:59
  30.7 3.7 %collective-permute-start.2 = (bf16[256,1024]{1,0:T(8,128)(2,1)}, bf16[256,1024]{1,0:T(8,128)(2,1)}, u32[]{:S(2)}, u32[]{:S(2)}) collective-permute-start(bf16[256,1024]{1,0:T(8,128)(2,1)} %bitcast_add_fusion.3), channel_id=1, source_target_pairs={{0,4},{2,6},{4,0},{6,2},{1,5},{3,7},{5,1},{7,3},{8,12},{10,14},{12... | collective-permute-start | bytes 1572872 | tf_op jit(solution)/shard_map/ppermute | solution.py:55
  34.4 0.0 copy-done.2
  34.4 0.0 copy-done.1
  34.4 1.6 %copy.13 = f32[1,512,512]{1,2,0:T(8,128)S(1)} copy(f32[1,512,512]{2,1,0:T(8,128)} %param.10) | data formatting | bytes 2097152 | tf_op args[4]
  36.0 2.5 %copy.14 = f32[1,512,512]{1,2,0:T(8,128)} copy(f32[1,512,512]{2,1,0:T(8,128)} %param.11) | data formatting | bytes 2097152 | tf_op args[5]
  38.5 1.1 bitcast_dynamic-update-slice_fusion.2
  39.6 8.4 %all-to-all-done = bf16[64,8,512]{2,1,0:T(8,128)(2,1)} async-done(((bf16[64,8,512]{2,1,0:T(8,128)(2,1)}), bf16[64,8,512]{2,1,0:T(8,128)(2,1)}, u32[]{:S(2)}, u32[]{:S(2)}) %all-to-all-start) | async-done | bytes 524320 | tf_op jit(solution)/shard_map/all_to_all | solution.py:22
  48.0 1.0 slice.21
  48.9 1.9 %collective-permute-start.3 = (bf16[32,8,512]{2,1,0:T(8,128)(2,1)S(1)}, bf16[32,8,512]{2,1,0:T(8,128)(2,1)S(1)}, u32[]{:S(2)}, u32[]{:S(2)}) collective-permute-start(bf16[32,8,512]{2,1,0:T(8,128)(2,1)S(1)} %slice.21), channel_id=1, source_target_pairs={{0,8},{8,0},{1,9},{9,1},{2,10},{10,2},{3,11},{11,3},{4,12},{12,4},... | collective-permute-start | bytes 786440 | tf_op jit(solution)/shard_map/ppermute | solution.py:69
  50.9 1.1 bitcast_dynamic-update-slice_fusion.1
  51.9 0.0 collective-permute-done.2
  52.0 1.1 bitcast_dynamic-update-slice_fusion
  53.0 0.0 collective-permute-done.3
  53.1 1.1 select_bitcast_fusion.1
  54.1 2.3 %all-gather = bf16[32,16,512]{2,1,0:T(8,128)(2,1)S(1)} all-gather(bf16[32,8,512]{2,1,0:T(8,128)(2,1)S(1)} %get-tuple-element.25), channel_id=2, replica_groups=mesh['zh'=4,'y'=8,'c'=2,'x'=4,'zl'=2] {'c'}, dimensions={1}, use_global_device_ids=true | all-gather | bytes 786432 | tf_op jit(solution)/shard_map/all_gather | solution.py:74
  56.4 0.7 fusion
  57.2 0.8 convolution_add_fusion
  58.0 0.0 copy-start.4
  58.0 18.6 %all_to_all.20 = bf16[4,256,512]{2,1,0:T(8,128)(2,1)S(1)} all-to-all(bf16[4,256,512]{2,1,0:T(8,128)(2,1)S(1)} %bitcast.160), channel_id=1, replica_groups=mesh['zh'=4,'y'=8,'c'=2,'x'=4,'zl'=2] {'x'}, dimensions={0} | all-to-all | bytes 2097152 | tf_op jit(solution)/shard_map/all_to_all | solution.py:22
  76.7 0.1 convert_reduce_fusion
  76.8 0.0 copy-done.4
  76.8 0.1 fusion.21
  76.9 0.1 broadcast_in_dim.33
  77.0 17.2 %all_to_all.21 = bf16[4,256,512]{2,1,0:T(8,128)(2,1)S(1)} all-to-all(bf16[4,256,512]{2,1,0:T(8,128)(2,1)S(1)} %broadcast_in_dim.33), channel_id=1, replica_groups=mesh['zh'=4,'y'=8,'c'=2,'x'=4,'zl'=2] {'x'}, dimensions={0} | all-to-all | bytes 2097152 | tf_op jit(solution)/shard_map/all_to_all | solution.py:22
  94.2 0.9 fusion.3
  95.1 0.0 copy-start
  95.2 2.9 %collective-permute-start.5 = (bf16[32,8,512]{2,1,0:T(8,128)(2,1)S(1)}, bf16[32,8,512]{2,1,0:T(8,128)(2,1)S(1)}, u32[]{:S(2)}, u32[]{:S(2)}) collective-permute-start(bf16[32,8,512]{2,1,0:T(8,128)(2,1)S(1)} %get-tuple-element.23), channel_id=1, source_target_pairs={{0,1},{1,0},{2,3},{3,2},{4,5},{5,4},{6,7},{7,6},{8,9},{9,8},{10,11... | collective-permute-start | bytes 786440 | tf_op jit(solution)/shard_map/ppermute | solution.py:107
  98.0 3.1 %collective-permute-start.4 = (bf16[32,8,512]{2,1,0:T(8,128)(2,1)S(1)}, bf16[32,8,512]{2,1,0:T(8,128)(2,1)S(1)}, u32[]{:S(2)}, u32[]{:S(2)}) collective-permute-start(bf16[32,8,512]{2,1,0:T(8,128)(2,1)S(1)} %get-tuple-element.24), channel_id=1, source_target_pairs={{0,1},{1,0},{2,3},{3,2},{4,5},{5,4},{6,7},{7,6},{8,9},{9,8},{10,11... | collective-permute-start | bytes 786440 | tf_op jit(solution)/shard_map/ppermute | solution.py:107
  101.1 0.9 fusion.5
  102.0 4.2 %collective-permute-done.5 = bf16[32,8,512]{2,1,0:T(8,128)(2,1)S(1)} collective-permute-done((bf16[32,8,512]{2,1,0:T(8,128)(2,1)S(1)}, bf16[32,8,512]{2,1,0:T(8,128)(2,1)S(1)}, u32[]{:S(2)}, u32[]{:S(2)}) %collective-permute-start.5) | collective-permute-done | bytes 262176 | tf_op jit(solution)/shard_map/ppermute | solution.py:107
  106.2 0.0 copy-done
  106.2 0.4 fusion.20
  106.6 0.0 copy-start.6
  106.6 1.9 %collective-permute-start.6 = (bf16[32,8,512]{2,1,0:T(8,128)(2,1)S(1)}, bf16[32,8,512]{2,1,0:T(8,128)(2,1)S(1)}, u32[]{:S(2)}, u32[]{:S(2)}) collective-permute-start(bf16[32,8,512]{2,1,0:T(8,128)(2,1)S(1)} %fusion.20), channel_id=1, source_target_pairs={{0,8},{8,0},{1,9},{9,1},{2,10},{10,2},{3,11},{11,3},{4,12},{12,4},... | collective-permute-start | bytes 786440 | tf_op jit(solution)/shard_map/ppermute | solution.py:122
  108.5 0.5 collective-permute-done.4
  109.0 0.4 fusion.11
  109.4 0.6 collective-permute-done.6
  110.0 0.1 add_convert_fusion
  110.1 20.8 %all_to_all.22 = bf16[32,8,512]{2,1,0:T(8,128)(2,1)S(1)} all-to-all(bf16[32,8,512]{2,1,0:T(8,128)(2,1)S(1)} %add_convert_fusion), channel_id=1, replica_groups=mesh['zh'=4,'y'=8,'c'=2,'x'=4,'zl'=2] {'zh','y'}, dimensions={0} | all-to-all | bytes 524288 | tf_op jit(solution)/shard_map/all_to_all | solution.py:22
  131.0 0.0 copy-done.6
  131.0 0.6 multiply_subtract_fusion
  (4 shorter events, 0.1 us)
Async XLA Ops:
  0.7 1.6 %copy-start.3 = (bf16[1,256,4096]{2,1,0:T(8,128)(2,1)S(1)}, bf16[1,256,4096]{2,1,0:T(8,128)(2,1)}, u32[]{:S(2)}) copy-start(bf16[1,256,4096]{2,1,0:T(8,128)(2,1)} %param.8) | copy-start | bytes 6291460
  2.3 8.2 %copy-start.5 = (f32[512,8]{0,1:T(8,128)S(1)}, f32[512,8]{0,1:T(8,128)}, u32[]{:S(2)}) copy-start(f32[512,8]{0,1:T(8,128)} %param.6) | copy-start | bytes 49156
  3.4 24.7 %collective-permute-start = (bf16[256,1024]{1,0:T(8,128)(2,1)}, bf16[256,1024]{1,0:T(8,128)(2,1)S(1)}, u32[]{:S(2)}, u32[]{:S(2)}) collective-permute-start(bf16[256,1024]{1,0:T(8,128)(2,1)} %get-tuple-element.19), channel_id=1, source_target_pairs={{0,2},{2,4},{4,6},{6,0},{1,3},{3,5},{5,7},{7,1},{8,10},{10,12},{12... | collective-permute-start | bytes 1572872 | tf_op jit(solution)/shard_map/ppermute | solution.py:55
  6.8 21.3 %collective-permute-start.1 = (bf16[256,1024]{1,0:T(8,128)(2,1)}, bf16[256,1024]{1,0:T(8,128)(2,1)S(1)}, u32[]{:S(2)}, u32[]{:S(2)}) collective-permute-start(bf16[256,1024]{1,0:T(8,128)(2,1)} %get-tuple-element.18), channel_id=1, source_target_pairs={{0,6},{2,0},{4,2},{6,4},{1,7},{3,1},{5,3},{7,5},{8,14},{10,8},{12,... | collective-permute-start | bytes 1572872 | tf_op jit(solution)/shard_map/ppermute | solution.py:55
  11.3 36.6 %all-to-all-start = ((bf16[64,8,512]{2,1,0:T(8,128)(2,1)}), bf16[64,8,512]{2,1,0:T(8,128)(2,1)}, u32[]{:S(2)}, u32[]{:S(2)}) async-start(bf16[64,8,512]{2,1,0:T(8,128)(2,1)} %broadcast_in_dim.31), calls=%async_computation | async-start | bytes 1048576 | tf_op jit(solution)/shard_map/all_to_all | solution.py:22
  28.1 6.3 %copy-start.2 = (bf16[256,1024]{1,0:T(8,128)(2,1)}, bf16[256,1024]{1,0:T(8,128)(2,1)S(1)}, u32[]{:S(2)}) copy-start(bf16[256,1024]{1,0:T(8,128)(2,1)S(1)} %collective-permute-done) | copy-start | bytes 1572868
  28.1 6.2 %copy-start.1 = (bf16[256,1024]{1,0:T(8,128)(2,1)}, bf16[256,1024]{1,0:T(8,128)(2,1)S(1)}, u32[]{:S(2)}) copy-start(bf16[256,1024]{1,0:T(8,128)(2,1)S(1)} %collective-permute-done.1) | copy-start | bytes 1572868
  30.7 21.3 %collective-permute-start.2 = (bf16[256,1024]{1,0:T(8,128)(2,1)}, bf16[256,1024]{1,0:T(8,128)(2,1)}, u32[]{:S(2)}, u32[]{:S(2)}) collective-permute-start(bf16[256,1024]{1,0:T(8,128)(2,1)} %bitcast_add_fusion.3), channel_id=1, source_target_pairs={{0,4},{2,6},{4,0},{6,2},{1,5},{3,7},{5,1},{7,3},{8,12},{10,14},{12... | collective-permute-start | bytes 1572872 | tf_op jit(solution)/shard_map/ppermute | solution.py:55
  48.9 4.1 %collective-permute-start.3 = (bf16[32,8,512]{2,1,0:T(8,128)(2,1)S(1)}, bf16[32,8,512]{2,1,0:T(8,128)(2,1)S(1)}, u32[]{:S(2)}, u32[]{:S(2)}) collective-permute-start(bf16[32,8,512]{2,1,0:T(8,128)(2,1)S(1)} %slice.21), channel_id=1, source_target_pairs={{0,8},{8,0},{1,9},{9,1},{2,10},{10,2},{3,11},{11,3},{4,12},{12,4},... | collective-permute-start | bytes 786440 | tf_op jit(solution)/shard_map/ppermute | solution.py:69
  58.0 18.8 %copy-start.4 = (bf16[1,256,512]{2,1,0:T(8,128)(2,1)S(1)}, bf16[1,256,512]{2,1,0:T(8,128)(2,1)}, u32[]{:S(2)}) copy-start(bf16[1,256,512]{2,1,0:T(8,128)(2,1)} %param.9) | copy-start | bytes 786436
  95.1 11.1 %copy-start = (f32[1,512,512]{1,2,0:T(8,128)S(1)}, f32[1,512,512]{1,2,0:T(8,128)}, u32[]{:S(2)}) copy-start(f32[1,512,512]{1,2,0:T(8,128)} %copy.14) | copy-start | bytes 3145732
  95.2 11.1 %collective-permute-start.5 = (bf16[32,8,512]{2,1,0:T(8,128)(2,1)S(1)}, bf16[32,8,512]{2,1,0:T(8,128)(2,1)S(1)}, u32[]{:S(2)}, u32[]{:S(2)}) collective-permute-start(bf16[32,8,512]{2,1,0:T(8,128)(2,1)S(1)} %get-tuple-element.23), channel_id=1, source_target_pairs={{0,1},{1,0},{2,3},{3,2},{4,5},{5,4},{6,7},{7,6},{8,9},{9,8},{10,11... | collective-permute-start | bytes 786440 | tf_op jit(solution)/shard_map/ppermute | solution.py:107
  98.0 11.0 %collective-permute-start.4 = (bf16[32,8,512]{2,1,0:T(8,128)(2,1)S(1)}, bf16[32,8,512]{2,1,0:T(8,128)(2,1)S(1)}, u32[]{:S(2)}, u32[]{:S(2)}) collective-permute-start(bf16[32,8,512]{2,1,0:T(8,128)(2,1)S(1)} %get-tuple-element.24), channel_id=1, source_target_pairs={{0,1},{1,0},{2,3},{3,2},{4,5},{5,4},{6,7},{7,6},{8,9},{9,8},{10,11... | collective-permute-start | bytes 786440 | tf_op jit(solution)/shard_map/ppermute | solution.py:107
  106.6 24.4 %copy-start.6 = (f32[512,8]{0,1:T(8,128)S(1)}, f32[512,8]{0,1:T(8,128)}, u32[]{:S(2)}) copy-start(f32[512,8]{0,1:T(8,128)} %param.7) | copy-start | bytes 49156
  106.6 3.4 %collective-permute-start.6 = (bf16[32,8,512]{2,1,0:T(8,128)(2,1)S(1)}, bf16[32,8,512]{2,1,0:T(8,128)(2,1)S(1)}, u32[]{:S(2)}, u32[]{:S(2)}) collective-permute-start(bf16[32,8,512]{2,1,0:T(8,128)(2,1)S(1)} %fusion.20), channel_id=1, source_target_pairs={{0,8},{8,0},{1,9},{9,1},{2,10},{10,2},{3,11},{11,3},{4,12},{12,4},... | collective-permute-start | bytes 786440 | tf_op jit(solution)/shard_map/ppermute | solution.py:122
